TPU v7x, 256 devices: a whole 4x4x8 slice. The times are simulated.
256 devices in a mesh: boson: 64 (over z, x, core), block: 4 (over y).
Axes of the slice: x: 4, y: 4, z: 8, core: 2. Of those that a mesh axis runs over, the one named last changes fastest.
Arguments:
- gamma_ph: bfloat16 [256, 1024, 1024], P('boson', 'block'), may hold values from -6 to 6
- full_ph: bfloat16 [256, 1024, 1024], P('boson', 'block'), may hold values from -0.1875 to 0.1875
- chi_ph: float32 [256, 1024], P('boson'), may hold values from 0.3 to 3
- pp_vertex: bfloat16 [256, 1024, 1024], P('boson', 'block'), may hold values from -0.1875 to 0.1875
- chi_pp: float32 [256, 1024], P('boson'), may hold values from 0.3 to 3
- relabel: int32 [256, 16, 8], replicated, may hold values from 0 to 255, as said below
Outputs:
- vertex_new: bfloat16 [256, 1024, 1024], P('boson', 'block')
Inputs may be any that keep to these rules, and one draw needn't show every extreme that they name: `relabel`: for each row tile and column block the table is a permutation of the 256 points. The owner of the target point (target // 4) is the source's owner (q // 4) plus a shift modulo 64, and both this shift and the target's position among its owner's points (target % 4) depend only on the row tile, the column block and q % 4. Row tiles b * 4 to (b + 1) * 4 - 1 form row block b; within one row block, at most 3 of the 128 triples of position, row tile and column block share a shift, and some shift is shared by exactly 3; in every row block the shifts 1, 32 and 63 each occur.
All inputs are finite; a program needn't handle non-finite values.
Results may differ from a plain program's by a relative error of at most 0.0063.
Values may be sent and summed in bfloat16 or wider, within the bound.
No kernel may reach another device: no remote copies, remote signals or barrier semaphores. Data moves between devices by JAX's collectives and lax.ppermute only.
A program may use at most 128 MiB of HBM per device.

v0:
```python
import jax
import jax.numpy as jnp
from jax import lax
from jax.sharding import PartitionSpec as P

CB = 8
RS = 4


def to_tiles(matrix):
    points, row_count, order_size = matrix.shape
    tile_width = order_size // CB
    tile_rows = row_count // RS
    return (
        matrix.reshape(points, RS, tile_rows, CB, tile_width)
        .transpose(0, 1, 3, 2, 4)
        .reshape(points * RS * CB, tile_rows, tile_width)
    )


def from_tiles(tile_stack, points):
    total_tiles, tile_rows, tile_width = tile_stack.shape
    return (
        tile_stack.reshape(points, RS, CB, tile_rows, tile_width)
        .transpose(0, 1, 3, 2, 4)
        .reshape(points, RS * tile_rows, CB * tile_width)
    )


def scale_columns(left_side, column_scale):
    return (left_side.astype(jnp.float32) * column_scale[:, None, :]).astype(jnp.bfloat16)


def product_adder(scaled, shard_piece):
    return jnp.einsum("qij,qjk->qik", scaled, shard_piece, preferred_element_type=jnp.float32)


def pack_slots(tile_stack, slot_of_item, slot_total):
    item_total = tile_stack.shape[0]
    matches = (slot_of_item[None, :] == jnp.arange(slot_total, dtype=jnp.int32)[:, None]).astype(
        jnp.int32
    )
    item_index = jnp.sum(matches * jnp.arange(item_total, dtype=jnp.int32)[None, :], axis=1)
    filled = jnp.sum(matches, axis=1).astype(tile_stack.dtype)
    return jnp.take(tile_stack, item_index, axis=0) * filled[:, None, None]


def local(gamma_ph, full_ph, chi_ph, pp_vertex, chi_pp, relabel):
    points = gamma_ph.shape[0]
    nboson = lax.axis_size("boson")
    boson_here = lax.axis_index("boson")
    block_here = lax.axis_index("block")
    item_total = points * RS * CB
    capacity = -(-item_total // nboson) + 1
    phi_ph = product_adder(
        scale_columns(gamma_ph, chi_ph), lax.all_gather(full_ph, "block", axis=1, tiled=True)
    )
    ph_tiles = to_tiles(phi_ph.astype(jnp.bfloat16))
    tile_shape = ph_tiles.shape[1:]
    own_targets = lax.dynamic_slice(
        relabel, (boson_here * points, block_here * RS, 0), (points, RS, CB)
    ).reshape(item_total)
    shifts = (own_targets // points - boson_here) % nboson
    item_range = jnp.arange(item_total, dtype=jnp.int32)
    target = own_targets % points * (RS * CB) + item_range % (RS * CB)
    gather_order = jnp.sum(
        (target[None, :] == item_range[:, None]).astype(jnp.int32) * item_range[None, :], axis=1
    )
    earlier = (shifts[None, :] == shifts[:, None]) & (item_range[None, :] < item_range[:, None])
    slot_rank = jnp.sum(earlier.astype(jnp.int32), axis=1)
    send_slot = (boson_here + shifts) % nboson * capacity + slot_rank
    recv_slot = (boson_here - shifts) % nboson * capacity + slot_rank
    outgoing = pack_slots(ph_tiles, send_slot, nboson * capacity).reshape(
        (nboson, capacity) + tile_shape
    )
    incoming = lax.all_to_all(outgoing, "boson", split_axis=0, concat_axis=0, tiled=True).reshape(
        (nboson * capacity,) + tile_shape
    )
    arrived = jnp.take(incoming, recv_slot, axis=0)
    relabelled = from_tiles(jnp.take(arrived, gather_order, axis=0), points)
    phi_pp = product_adder(
        scale_columns(relabelled, chi_pp), lax.all_gather(pp_vertex, "block", axis=1, tiled=True)
    ).astype(jnp.bfloat16)
    leaving = jnp.take(to_tiles(phi_pp), target, axis=0)
    outgoing_back = pack_slots(leaving, recv_slot, nboson * capacity).reshape(
        (nboson, capacity) + tile_shape
    )
    incoming_back = lax.all_to_all(
        outgoing_back, "boson", split_axis=0, concat_axis=0, tiled=True
    ).reshape((nboson * capacity,) + tile_shape)
    returned = jnp.take(incoming_back, send_slot, axis=0)
    output = (
        gamma_ph.astype(jnp.float32) + phi_ph + from_tiles(returned, points).astype(jnp.float32)
    )
    return output.astype(jnp.bfloat16)


def solution(mesh):
    placed = (
        P("boson", "block", None),
        P("boson", "block", None),
        P("boson", None),
        P("boson", "block", None),
        P("boson", None),
        P(),
    )
    return jax.shard_map(
        local, mesh=mesh, in_specs=placed, out_specs=P("boson", "block", None), check_vma=False
    )
```

profile of v0, /device:TPU:2, one launch (start us, length us, event | category | flops | bytes accessed | tf_op | source)
XLA Modules:
  0.0 341.8 jit_solution(7744677609703114833)
XLA Ops:
  8.8 89.0 %all-gather.3.cloned.1.call-done = bf16[4,1024,1024]{2,1,0:T(8,128)(2,1)} async-done(((bf16[4,256,1024]{2,1,0:T(8,128)(2,1)}), bf16[4,1024,1024]{2,1,0:T(8,128)(2,1)}) %all-gather.3.cloned.1.call-update) | async-done | bytes 8388624 | tf_op jit(solution)/shard_map/all_gather | solution.py:56
  97.8 7.7 %fusion.22 = (bf16[4,256,1024]{2,1,0:T(8,128)(2,1)S(1)}, f32[4,256,1024]{2,1,0:T(8,128)}) fusion(bf16[4,1024,1024]{2,1,0:T(8,128)(2,1)} %all-gather.3.cloned.1.call-done, bf16[4,256,1024]{2,1,0:T(8,128)(2,1)S(1)} %copy-done.2, f32[4,1024]{1,0:T(4,128)S(1)} %copy-done.4), kind=kOutput, calls=%fused_computation.79 | convolution fusion | flops 2151677952 | bytes 16793600 | tf_op jit(solution)/shard_map/qij,qjk->qik/dot_general | solution.py:35
  106.8 2.8 gather_fusion
  109.6 3.8 %select_multiply_fusion.1 = bf16[192,64,128]{2,1,0:T(8,128)(2,1)} fusion(bf16[192,64,128]{2,1,0:T(8,128)(2,1)} %gather_fusion, pred[192]{0:T(512)(128)(4,1)S(1)} %compare_and_fusion.5, bf16[192]{0:T(256)(128)(2,1)S(1)} %convert_element_type.72), kind=kLoop, calls=%fused_computation.15 | loop fusion | flops 3145728 | bytes 6292032 | tf_op jit(solution)/shard_map/mul | solution.py:45
  113.4 10.5 %all-to-all-start = ((bf16[64,3,64,128]{3,2,1,0:T(8,128)(2,1)}), bf16[64,3,64,128]{3,2,1,0:T(8,128)(2,1)S(1)}, u32[]{:S(2)}, u32[]{:S(2)}) async-start(bf16[64,3,64,128]{3,2,1,0:T(8,128)(2,1)} %bitcast.2), calls=%async_computation | async-start | bytes 6291456 | tf_op jit(solution)/shard_map/all_to_all | solution.py:76
  124.2 73.5 %all-to-all-done = bf16[64,3,64,128]{3,2,1,0:T(8,128)(2,1)S(1)} async-done(((bf16[64,3,64,128]{3,2,1,0:T(8,128)(2,1)}), bf16[64,3,64,128]{3,2,1,0:T(8,128)(2,1)S(1)}, u32[]{:S(2)}, u32[]{:S(2)}) %all-to-all-start) | async-done | bytes 3145760 | tf_op jit(solution)/shard_map/all_to_all | solution.py:76
  197.6 2.1 gather_fusion.1
  199.8 1.9 broadcast_select_fusion.3
  201.6 2.1 gather_fusion.2
  203.8 1.9 broadcast_select_fusion.2
  206.1 5.2 %copy.19 = f32[4,4,64,8,128]{4,3,2,1,0:T(8,128)} copy(f32[4,4,64,8,128]{4,2,3,1,0:T(8,128)S(1)} %convert_bitcast_fusion.1) | data formatting | bytes 8388608 | tf_op jit(solution)/shard_map/convert_element_type | solution.py:31
  211.3 4.9 %reshape.233 = f32[4,256,1024]{2,1,0:T(8,128)} reshape(f32[4,4,64,8,128]{4,3,2,1,0:T(8,128)} %copy.19) | data formatting | bytes 8388608 | tf_op jit(solution)/shard_map/convert_element_type | solution.py:31
  216.2 7.0 %fusion.8 = bf16[4,256,1024]{2,1,0:T(8,128)(2,1)S(1)} fusion(bf16[4,1024,1024]{2,1,0:T(8,128)(2,1)} %all-gather.5.cloned.1.call-done, f32[4,256,1024]{2,1,0:T(8,128)} %reshape.233, f32[4,1024]{1,0:T(4,128)S(1)} %copy-done.5), kind=kOutput, calls=%fused_computation.24 | convolution fusion | flops 2150629376 | bytes 14696448 | tf_op jit(solution)/shard_map/qij,qjk->qik/dot_general | solution.py:35
  224.5 2.1 gather_fusion.3
  226.6 1.9 broadcast_select_fusion.1
  228.5 2.7 gather_fusion.4
  231.2 3.8 %select_multiply_fusion = bf16[192,64,128]{2,1,0:T(8,128)(2,1)} fusion(bf16[192,64,128]{2,1,0:T(8,128)(2,1)} %gather_fusion.4, pred[192]{0:T(512)(128)(4,1)S(1)} %compare_and_fusion.1, bf16[192]{0:T(256)(128)(2,1)S(1)} %convert_element_type.80), kind=kLoop, calls=%fused_computation.14 | loop fusion | flops 3145728 | bytes 6292032 | tf_op jit(solution)/shard_map/mul | solution.py:45
  235.0 5.4 %all-to-all-start.1 = ((bf16[64,3,64,128]{3,2,1,0:T(8,128)(2,1)}), bf16[64,3,64,128]{3,2,1,0:T(8,128)(2,1)S(1)}, u32[]{:S(2)}, u32[]{:S(2)}) async-start(bf16[64,3,64,128]{3,2,1,0:T(8,128)(2,1)} %bitcast.8), calls=%async_computation.1 | async-start | bytes 6291456 | tf_op jit(solution)/shard_map/all_to_all | solution.py:88
  240.4 73.7 %all-to-all-done.1 = bf16[64,3,64,128]{3,2,1,0:T(8,128)(2,1)S(1)} async-done(((bf16[64,3,64,128]{3,2,1,0:T(8,128)(2,1)}), bf16[64,3,64,128]{3,2,1,0:T(8,128)(2,1)S(1)}, u32[]{:S(2)}, u32[]{:S(2)}) %all-to-all-start.1) | async-done | bytes 3145760 | tf_op jit(solution)/shard_map/all_to_all | solution.py:88
  314.2 2.1 gather_fusion.5
  316.3 1.9 broadcast_select_fusion
  318.6 5.3 %copy.21 = f32[4,4,64,8,128]{4,3,2,1,0:T(8,128)} copy(f32[4,4,64,8,128]{4,2,3,1,0:T(8,128)S(1)} %convert_bitcast_fusion) | data formatting | bytes 8388608 | tf_op jit(solution)/shard_map/convert_element_type | solution.py:93
  323.9 5.0 %reshape.234 = f32[4,256,1024]{2,1,0:T(8,128)} reshape(f32[4,4,64,8,128]{4,3,2,1,0:T(8,128)} %copy.21) | data formatting | bytes 8388608 | tf_op jit(solution)/shard_map/convert_element_type | solution.py:93
  328.9 6.1 %fusion.2 = bf16[4,256,1024]{2,1,0:T(8,128)(2,1)} fusion(f32[4,256,1024]{2,1,0:T(8,128)} %reshape.234, f32[4,256,1024]{2,1,0:T(8,128)} %get-tuple-element.21, bf16[4,256,1024]{2,1,0:T(8,128)(2,1)S(1)} %copy-done.3), kind=kLoop, calls=%fused_computation.10 | loop fusion | flops 4194304 | bytes 12582912 | tf_op jit(solution)/shard_map/convert_element_type | solution.py:95
  (49 shorter events, 5.8 us)
Async XLA Ops:
  6.5 1.5 copy-start
  6.5 91.3 %copy-start.2 = (bf16[4,256,1024]{2,1,0:T(8,128)(2,1)S(1)}, bf16[4,256,1024]{2,1,0:T(8,128)(2,1)}, u32[]{:S(2)}) copy-start(bf16[4,256,1024]{2,1,0:T(8,128)(2,1)} %param.12) | copy-start | bytes 6291460
  6.5 91.3 %copy-start.4 = (f32[4,1024]{1,0:T(4,128)S(1)}, f32[4,1024]{1,0:T(4,128)}, u32[]{:S(2)}) copy-start(f32[4,1024]{1,0:T(4,128)} %param.14) | copy-start | bytes 49156
  6.5 91.3 %all-gather.3.cloned.1.call-start = ((), (), s32[]{:S(2)}) async-start(), calls=%async_computation.2 | async-start | bytes 10485760 | tf_op jit(solution)/shard_map/all_gather | solution.py:56
  7.3 209.0 %all-gather.5.cloned.1.call-start = ((), (), s32[]{:S(2)}) async-start(), calls=%async_computation.3 | async-start | bytes 10485760 | tf_op jit(solution)/shard_map/all_gather | solution.py:82
  113.4 84.3 %all-to-all-start = ((bf16[64,3,64,128]{3,2,1,0:T(8,128)(2,1)}), bf16[64,3,64,128]{3,2,1,0:T(8,128)(2,1)S(1)}, u32[]{:S(2)}, u32[]{:S(2)}) async-start(bf16[64,3,64,128]{3,2,1,0:T(8,128)(2,1)} %bitcast.2), calls=%async_computation | async-start | bytes 6291456 | tf_op jit(solution)/shard_map/all_to_all | solution.py:76
  211.3 4.9 %copy-start.5 = (f32[4,1024]{1,0:T(4,128)S(1)}, f32[4,1024]{1,0:T(4,128)}, u32[]{:S(2)}) copy-start(f32[4,1024]{1,0:T(4,128)} %param.16) | copy-start | bytes 49156
  235.0 79.2 %all-to-all-start.1 = ((bf16[64,3,64,128]{3,2,1,0:T(8,128)(2,1)}), bf16[64,3,64,128]{3,2,1,0:T(8,128)(2,1)S(1)}, u32[]{:S(2)}, u32[]{:S(2)}) async-start(bf16[64,3,64,128]{3,2,1,0:T(8,128)(2,1)} %bitcast.8), calls=%async_computation.1 | async-start | bytes 6291456 | tf_op jit(solution)/shard_map/all_to_all | solution.py:88
  323.9 5.0 %copy-start.3 = (bf16[4,256,1024]{2,1,0:T(8,128)(2,1)S(1)}, bf16[4,256,1024]{2,1,0:T(8,128)(2,1)}, u32[]{:S(2)}) copy-start(bf16[4,256,1024]{2,1,0:T(8,128)(2,1)} %param.12) | copy-start | bytes 6291460
  328.9 6.1 %copy-start.1 = (s32[256,16,8]{0,2,1:T(8,128)S(1)}, s32[256,16,8]{0,2,1:T(8,128)}, u32[]{:S(2)}) copy-start(s32[256,16,8]{0,2,1:T(8,128)} %param.17) | copy-start | bytes 393220
Sparse Core Ops, SparseCore 0:
  9.2 88.6 all-gather.2
  99.6 86.6 all-gather.4
where the time goes:
time: 342 us
  waiting for transfers between devices  238 us (70%)
  local copies, waits for them, and re-layouts  37.2 us (11%)
  other arithmetic  22.7 us (7%)
  starting transfers between devices  16 us (5%)
  matrix products  14.7 us (4%)
  between operations  13.7 us (4%)
    all_gather x1, waiting for transfers between devices, local(): lax.all_gather(full_ph, 'block', axis=1, tiled=True)  89 us
    all_to_all x1, waiting for transfers between devices, local(): lax.all_to_all(outgoing_back, 'boson', split_axis=0, concat_axis=0, tiled...  73.7 us
    all_to_all x1, waiting for transfers between devices, local(): lax.all_to_all(outgoing, 'boson', split_axis=0, concat_axis=0, tiled=True)  73.5 us
    dot_general x2, matrix products, product_adder(): jnp.einsum('qij,qjk->qik', scaled, shard_piece, preferred_element_type=jn...  14.7 us
    all_to_all x1, starting transfers between devices, local(): lax.all_to_all(outgoing, 'boson', split_axis=0, concat_axis=0, tiled=True)  10.5 us
    convert_element_type x2, local copies, waits for them, and re-layouts, local(): from_tiles(returned, points).astype(jnp.float32)  10.3 us
    convert_element_type x2, local copies, waits for them, and re-layouts, scale_columns(): left_side.astype(jnp.float32) * column_scale[:, None, :]  10.1 us
    mul x2, other arithmetic, pack_slots(): return jnp.take(tile_stack, item_index, axis=0) * filled[:, None, None]  7.57 us
  transfers between devices with their start and end apart: 4, of which 3 were waited for; matrix products, arithmetic and copies ran while one was open for 10% of the time, Pallas kernels for 0%

commit v1 on v0

v1 whole, which is shorter than its diff:
```python
import jax
import jax.numpy as jnp
from jax import lax
from jax.experimental import pallas as pl
from jax.experimental.pallas import tpu as pltpu
from jax.sharding import PartitionSpec as P

CB = 8
RS = 4
CAP = 3
MIB = 1 << 20


def block_rows(shard, after=None):
    n = lax.axis_size("block")
    up = [(i, (i + 1) % n) for i in range(n)]
    down = [(i, (i - 1) % n) for i in range(n)]
    half = shard.shape[1] // 2
    from_below = lax.ppermute(shard, "block", up)
    from_above = lax.ppermute(shard, "block", down)
    far_low = lax.ppermute(from_below[:, :half], "block", up)
    far_high = lax.ppermute(from_above[:, half:], "block", down)
    return shard, from_below, from_above, far_low, far_high


def product(lhs_ref, here, pieces):
    own, below, above, far_low, far_high = pieces
    rows = own.shape[1]
    half = rows // 2
    total = None
    for step, refs in ((0, (own,)), (3, (below,)), (1, (above,)), (2, (far_low, far_high))):
        start = lax.rem(here + step, 4) * rows
        for k, ref in enumerate(refs):
            depth = ref.shape[1]
            columns = pl.ds(pl.multiple_of(start + k * half, half), depth)
            part = jnp.dot(lhs_ref[:, columns], ref[0], preferred_element_type=jnp.float32)
            total = part if total is None else total + part
    return total


def ph_kernel(index, gamma, chi, own, below, above, low, high, base, slots, lhs):
    q = pl.program_id(0)
    g = gamma[0].astype(jnp.float32)
    lhs[...] = (g * chi[0]).astype(jnp.bfloat16)
    phi = product(lhs, index[128], (own, below, above, low, high))
    base[0] = g + phi
    wire = phi.astype(jnp.bfloat16)
    for r in range(RS):
        for c in range(CB):
            slot = index[q * (RS * CB) + r * CB + c]
            slots[slot] = wire[r * 64 : (r + 1) * 64, c * 128 : (c + 1) * 128]


def pp_kernel(index, came, chi, own, below, above, low, high, slots, lhs):
    p = pl.program_id(0)
    for r in range(RS):
        for c in range(CB):
            slot = index[p * (RS * CB) + r * CB + c]
            tile = came[slot].astype(jnp.float32) * chi[0, :, c * 128 : (c + 1) * 128]
            lhs[r * 64 : (r + 1) * 64, c * 128 : (c + 1) * 128] = tile.astype(jnp.bfloat16)
    phi = product(lhs, index[128], (own, below, above, low, high)).astype(jnp.bfloat16)
    for r in range(RS):
        for c in range(CB):
            slot = index[p * (RS * CB) + r * CB + c]
            slots[slot] = phi[r * 64 : (r + 1) * 64, c * 128 : (c + 1) * 128]


def sum_kernel(index, base, came, out):
    q = pl.program_id(0)
    for r in range(RS):
        for c in range(CB):
            slot = index[q * (RS * CB) + r * CB + c]
            rows, columns = slice(r * 64, (r + 1) * 64), slice(c * 128, (c + 1) * 128)
            out[0, rows, columns] = (base[0, rows, columns] + came[slot].astype(jnp.float32)).astype(
                jnp.bfloat16
            )


def point_spec(rows, columns):
    return pl.BlockSpec((1, rows, columns), lambda q, index: (q, 0, 0))


def whole_spec(shape):
    return pl.BlockSpec(shape, lambda q, index: (0,) * len(shape))


PIECES = [point_spec(256, 1024)] * 3 + [point_spec(128, 1024)] * 2
TILES = (192, 64, 128)


def call(kernel, index, operands, in_specs, out_specs, out_shape, scratch, flops, moved):
    return pl.pallas_call(
        kernel,
        grid_spec=pltpu.PrefetchScalarGridSpec(
            num_scalar_prefetch=1,
            grid=(4,),
            in_specs=in_specs,
            out_specs=out_specs,
            scratch_shapes=scratch,
        ),
        out_shape=out_shape,
        compiler_params=pltpu.CompilerParams(vmem_limit_bytes=32 * MIB),
        cost_estimate=pl.CostEstimate(flops=flops, bytes_accessed=moved, transcendentals=0),
    )(index, *operands)


def plan(relabel, points, boson_here, block_here):
    nboson = lax.axis_size("boson")
    item_total = points * RS * CB
    own_targets = lax.dynamic_slice(
        relabel, (boson_here * points, block_here * RS, 0), (points, RS, CB)
    ).reshape(item_total)
    shifts = (own_targets // points - boson_here) % nboson
    item_range = jnp.arange(item_total, dtype=jnp.int32)
    target = own_targets % points * (RS * CB) + item_range % (RS * CB)
    earlier = (shifts[None, :] == shifts[:, None]) & (item_range[None, :] < item_range[:, None])
    rank = jnp.sum(earlier.astype(jnp.int32), axis=1)
    send = (boson_here + shifts) % nboson * CAP + rank
    recv = (boson_here - shifts) % nboson * CAP + rank
    recv_at = jnp.sum(
        (target[None, :] == item_range[:, None]).astype(jnp.int32) * recv[None, :], axis=1
    )
    return send, recv_at


def exchange(slots):
    nboson = lax.axis_size("boson")
    tile = slots.shape[1:]
    return lax.all_to_all(
        slots.reshape((nboson, CAP) + tile), "boson", split_axis=0, concat_axis=0, tiled=True
    ).reshape(slots.shape)


def local(gamma_ph, full_ph, chi_ph, pp_vertex, chi_pp, relabel):
    points = gamma_ph.shape[0]
    block_here = lax.axis_index("block")
    send, recv_at = plan(relabel, points, lax.axis_index("boson"), block_here)
    here = jnp.full((8,), block_here, jnp.int32)
    send_index = jnp.concatenate([send, here])
    recv_index = jnp.concatenate([recv_at, here])
    flops = 2 * 4 * 256 * 1024 * 1024
    ph_pieces = block_rows(full_ph)
    pp_held = lax.optimization_barrier((pp_vertex,) + ph_pieces[1:])[0]
    pp_pieces = block_rows(pp_held)
    lhs = pltpu.VMEM((256, 1024), jnp.bfloat16)
    chi_spec = point_spec(1, 1024)
    tiles = jax.ShapeDtypeStruct(TILES, jnp.bfloat16)
    base, outgoing = call(
        ph_kernel,
        send_index,
        (gamma_ph, chi_ph[:, None, :]) + ph_pieces,
        [point_spec(256, 1024), chi_spec] + PIECES,
        [point_spec(256, 1024), whole_spec(TILES)],
        [jax.ShapeDtypeStruct(gamma_ph.shape, jnp.float32), tiles],
        [lhs],
        flops,
        17 * MIB,
    )
    came = exchange(outgoing)
    leaving = call(
        pp_kernel,
        recv_index,
        (came, chi_pp[:, None, :]) + pp_pieces,
        [whole_spec(TILES), chi_spec] + PIECES,
        whole_spec(TILES),
        tiles,
        [lhs],
        flops,
        14 * MIB,
    )
    back = exchange(leaving)
    return call(
        sum_kernel,
        send_index,
        (base, back),
        [point_spec(256, 1024), whole_spec(TILES)],
        point_spec(256, 1024),
        jax.ShapeDtypeStruct(gamma_ph.shape, jnp.bfloat16),
        [],
        1 * MIB,
        9 * MIB,
    )


def solution(mesh):
    placed = (
        P("boson", "block", None),
        P("boson", "block", None),
        P("boson", None),
        P("boson", "block", None),
        P("boson", None),
        P(),
    )
    return jax.shard_map(
        local, mesh=mesh, in_specs=placed, out_specs=P("boson", "block", None), check_vma=False
    )
```

time: 342 us -> 280 us (0.82)
  waiting for transfers between devices: 238 us -> 135 us
  blocking collectives: 0 us -> 84.1 us
  other arithmetic: 22.7 us -> 0.31 us
  local copies, waits for them, and re-layouts: 37.2 us -> 22.5 us
  matrix products: 14.7 us -> 0 us
  between operations: 13.7 us -> 0.18 us
  Pallas kernels: 0 us -> 12.1 us
  starting transfers between devices: 16 us -> 24.7 us
    all_to_all x2 -> x1, waiting for transfers between devices: 147 us -> 0.01 us  [exchange(): lax.all_to_all(slots.reshape((nboson, CAP) + tile), 'boson', split_axis=0...]
    ppermute x0 -> x8, waiting for transfers between devices: none -> 135 us  [the longest x2 91.7 us: block_rows(): from_below = lax.ppermute(shard, 'block', up)]
    all_gather x2 -> x0, waiting for transfers between devices: 89 us -> none  [the longest x1 89 us: local(): lax.all_gather(full_ph, 'block', axis=1, tiled=True)]
    all_to_all x0 -> x1, blocking collectives: none -> 84.1 us  [exchange(): lax.all_to_all(slots.reshape((nboson, CAP) + tile), 'boson', split_axis=0...]
    convert_element_type x4 -> x0, local copies, waits for them, and re-layouts: 20.4 us -> none  [the longest x2 10.3 us: local(): from_tiles(returned, points).astype(jnp.float32)]
    unnamed x14 -> x38, local copies, waits for them, and re-layouts: 1.26 us -> 20 us
    dot_general x2 -> x0, matrix products: 14.7 us -> none  [product_adder(): jnp.einsum('qij,qjk->qik', scaled, shard_piece, preferred_element_type=jn...]
    gather x6 -> x0, local copies, waits for them, and re-layouts: 14.1 us -> none  [the longest x2 5.53 us: pack_slots(): return jnp.take(tile_stack, item_index, axis=0) * filled[:, None, None]]
  transfers between devices with their start and end apart: 4 -> 9, of which waited for: 3 -> 5; matrix products, arithmetic and copies ran while one was open for 10% -> 1% of each run, Pallas kernels for 0% -> 0%
where the time goes in v1:
time: 280 us; the launch traced here: 279 us
  waiting for transfers between devices  135 us (48%)
  blocking collectives  84.1 us (30%)
  starting transfers between devices  24.7 us (9%)
  local copies, waits for them, and re-layouts  22.5 us (8%)
  Pallas kernels  12.1 us (4%)
    ppermute x2, waiting for transfers between devices, block_rows(): from_below = lax.ppermute(shard, 'block', up)  91.7 us
    all_to_all x1, blocking collectives, exchange(): lax.all_to_all(slots.reshape((nboson, CAP) + tile), 'boson', split_axis=0...  84.1 us
    ppermute x2, waiting for transfers between devices, block_rows(): far_low = lax.ppermute(from_below[:, :half], 'block', up)  41.7 us
    unnamed x38, local copies, waits for them, and re-layouts  20 us
    pallas_call x3, Pallas kernels, call(): pl.pallas_call(kernel, grid_spec=pltpu.PrefetchScalarGridSpec(num_scalar_...  12.1 us
    all_to_all x1, starting transfers between devices, exchange(): lax.all_to_all(slots.reshape((nboson, CAP) + tile), 'boson', split_axis=0...  12 us
  transfers between devices with their start and end apart: 9, of which 5 were waited for; matrix products, arithmetic and copies ran while one was open for 1% of the time, Pallas kernels for 0%

profile of v1, /device:TPU:2, one launch (start us, length us, event | category | flops | bytes accessed | tf_op | source)
XLA Modules:
  0.0 279.1 jit_solution(12344898666507842701)
XLA Ops:
  0.0 1.6 collective-permute-start
  1.6 1.7 collective-permute-start.1
  3.2 45.6 %collective-permute-done.below = bf16[4,256,1024]{2,1,0:T(8,128)(2,1)S(1)} collective-permute-done((bf16[4,256,1024]{2,1,0:T(8,128)(2,1)}, bf16[4,256,1024]{2,1,0:T(8,128)(2,1)S(1)}, u32[]{:S(2)}, u32[]{:S(2)}) %collective-permute-start) | collective-permute-done | bytes 2097184 | tf_op jit(solution)/shard_map/ppermute | solution.py:19
  51.3 1.3 copy-done.1
  52.6 2.9 %collective-permute-start.3 = (bf16[4,128,1024]{2,1,0:T(8,128)(2,1)}, bf16[4,128,1024]{2,1,0:T(8,128)(2,1)}, u32[]{:S(2)}, u32[]{:S(2)}) collective-permute-start(bf16[4,128,1024]{2,1,0:T(8,128)(2,1)} %slice.17), channel_id=1, source_target_pairs={{0,3},{1,0},{2,1},{3,2},{4,7},{5,4},{6,5},{7,6},{8,11},{9,8},{10,9... | collective-permute-start | bytes 3145736 | tf_op jit(solution)/shard_map/ppermute | solution.py:22
  56.1 19.4 %collective-permute-done.2.low = bf16[4,128,1024]{2,1,0:T(8,128)(2,1)S(1)} collective-permute-done((bf16[4,128,1024]{2,1,0:T(8,128)(2,1)}, bf16[4,128,1024]{2,1,0:T(8,128)(2,1)S(1)}, u32[]{:S(2)}, u32[]{:S(2)}) %collective-permute-start.2) | collective-permute-done | bytes 1048608 | tf_op jit(solution)/shard_map/ppermute | solution.py:21
  75.5 1.7 collective-permute-done.3.high
  77.2 1.6 copy-done.2
  78.8 1.6 copy-done.10
  80.4 1.6 copy-done.11
  82.0 5.2 %shard_map.64 = (f32[4,256,1024]{2,1,0:T(8,128)S(1)}, bf16[192,64,128]{2,1,0:T(8,128)(2,1)S(1)}) custom-call(s32[136]{0:T(256)S(1)} %concatenate.6.index, bf16[4,256,1024]{2,1,0:T(8,128)(2,1)S(1)} %copy-done.10, f32[4,1,1024]{2,1,0:T(1,128)S(1)} %broadcast_in_dim.4.chi, bf16[4,256,1024]{2,1,0:T(8,128)(2,1)S(1)} %copy-done.11, ...), custom_call_target="tpu_custom_call" | custom-call | flops 2147483648 | bytes 17825792 | tf_op jit(solution)/shard_map/pallas_call | solution.py:92
  87.2 1.9 copy-done.7
  89.1 1.7 copy-done.9
  90.8 12.0 %all-to-all-start = ((bf16[64,3,64,128]{3,2,1,0:T(8,128)(2,1)}), bf16[64,3,64,128]{3,2,1,0:T(8,128)(2,1)S(1)}, u32[]{:S(2)}, u32[]{:S(2)}) async-start(bf16[64,3,64,128]{3,2,1,0:T(8,128)(2,1)} %bitcast.7), calls=%async_computation | async-start | bytes 6291456 | tf_op jit(solution)/shard_map/all_to_all | solution.py:129
  104.0 2.8 collective-permute-start.5
  106.7 46.1 %collective-permute-done.4.below = bf16[4,256,1024]{2,1,0:T(8,128)(2,1)S(1)} collective-permute-done((bf16[4,256,1024]{2,1,0:T(8,128)(2,1)}, bf16[4,256,1024]{2,1,0:T(8,128)(2,1)S(1)}, u32[]{:S(2)}, u32[]{:S(2)}) %collective-permute-start.4) | collective-permute-done | bytes 2097184 | tf_op jit(solution)/shard_map/ppermute | solution.py:19
  154.1 2.2 collective-permute-start.7
  156.5 22.4 %collective-permute-done.6.low = bf16[4,128,1024]{2,1,0:T(8,128)(2,1)S(1)} collective-permute-done((bf16[4,128,1024]{2,1,0:T(8,128)(2,1)S(1)}, bf16[4,128,1024]{2,1,0:T(8,128)(2,1)S(1)}, u32[]{:S(2)}, u32[]{:S(2)}) %collective-permute-start.6) | collective-permute-done | bytes 1048608 | tf_op jit(solution)/shard_map/ppermute | solution.py:21
  180.8 1.6 copy-done.4
  182.4 1.6 copy-done.6
  184.0 1.6 copy-done.12
  188.1 4.4 %shard_map.65 = bf16[192,64,128]{2,1,0:T(8,128)(2,1)S(1)} custom-call(s32[136]{0:T(256)S(1)} %concatenate.7.index, bf16[192,64,128]{2,1,0:T(8,128)(2,1)S(1)} %bitcast.5, f32[4,1,1024]{2,1,0:T(1,128)S(1)} %broadcast_in_dim.5.chi, bf16[4,256,1024]{2,1,0:T(8,128)(2,1)S(1)} %copy-done.12, bf16[4,256,1024]{2,1,0:T(8,128)(2,1)S(1)} %copy-done.4, ...), custom_call_target="tpu_custom_call" | custom-call | flops 2147483648 | bytes 14680064 | tf_op jit(solution)/shard_map/pallas_call | solution.py:92
  192.5 84.1 %all_to_all.10 = bf16[64,3,64,128]{3,2,1,0:T(8,128)(2,1)S(1)} all-to-all(bf16[64,3,64,128]{3,2,1,0:T(8,128)(2,1)S(1)} %bitcast.6), channel_id=1, replica_groups=mesh['boson'=64,'block'=4] {'boson'}, dimensions={0} | all-to-all | bytes 6291456 | tf_op jit(solution)/shard_map/all_to_all | solution.py:129
  276.6 2.5 shard_map.66
  (51 shorter events, 9.9 us)
Async XLA Ops:
  0.0 55.5 %copy-start = (s32[256,16,8]{0,2,1:T(8,128)S(1)}, s32[256,16,8]{0,2,1:T(8,128)}, u32[]{:S(2)}) copy-start(s32[256,16,8]{0,2,1:T(8,128)} %param.11) | copy-start | bytes 393220
  0.0 56.0 %copy-start.17 = (f32[4,1024]{1,0:T(4,128)S(1)}, f32[4,1024]{1,0:T(4,128)}, u32[]{:S(2)}) copy-start(f32[4,1024]{1,0:T(4,128)} %param.8) | copy-start | bytes 49156
  0.0 48.9 %collective-permute-start = (bf16[4,256,1024]{2,1,0:T(8,128)(2,1)}, bf16[4,256,1024]{2,1,0:T(8,128)(2,1)S(1)}, u32[]{:S(2)}, u32[]{:S(2)}) collective-permute-start(bf16[4,256,1024]{2,1,0:T(8,128)(2,1)} %own.1), channel_id=1, source_target_pairs={{0,1},{1,2},{2,3},{3,0},{4,5},{5,6},{6,7},{7,4},{8,9},{9,10},{10,1... | collective-permute-start | bytes 6291464 | tf_op jit(solution)/shard_map/ppermute | solution.py:19
  1.6 48.7 %collective-permute-start.1 = (bf16[4,256,1024]{2,1,0:T(8,128)(2,1)}, bf16[4,256,1024]{2,1,0:T(8,128)(2,1)S(1)}, u32[]{:S(2)}, u32[]{:S(2)}) collective-permute-start(bf16[4,256,1024]{2,1,0:T(8,128)(2,1)} %own.1), channel_id=1, source_target_pairs={{0,3},{1,0},{2,1},{3,2},{4,7},{5,4},{6,5},{7,6},{8,11},{9,8},{10,9... | collective-permute-start | bytes 6291464 | tf_op jit(solution)/shard_map/ppermute | solution.py:20
  49.9 25.5 %collective-permute-start.2 = (bf16[4,128,1024]{2,1,0:T(8,128)(2,1)}, bf16[4,128,1024]{2,1,0:T(8,128)(2,1)S(1)}, u32[]{:S(2)}, u32[]{:S(2)}) collective-permute-start(bf16[4,128,1024]{2,1,0:T(8,128)(2,1)} %slice.16), channel_id=1, source_target_pairs={{0,1},{1,2},{2,3},{3,0},{4,5},{5,6},{6,7},{7,4},{8,9},{9,10},{10,1... | collective-permute-start | bytes 3145736 | tf_op jit(solution)/shard_map/ppermute | solution.py:21
  51.3 1.3 copy-start.1
  52.6 24.6 %collective-permute-start.3 = (bf16[4,128,1024]{2,1,0:T(8,128)(2,1)}, bf16[4,128,1024]{2,1,0:T(8,128)(2,1)}, u32[]{:S(2)}, u32[]{:S(2)}) collective-permute-start(bf16[4,128,1024]{2,1,0:T(8,128)(2,1)} %slice.17), channel_id=1, source_target_pairs={{0,3},{1,0},{2,1},{3,2},{4,7},{5,4},{6,5},{7,6},{8,11},{9,8},{10,9... | collective-permute-start | bytes 3145736 | tf_op jit(solution)/shard_map/ppermute | solution.py:22
  77.2 1.6 copy-start.2
  78.8 1.6 copy-start.10
  80.4 1.6 copy-start.11
  87.2 1.9 copy-start.7
  89.1 1.7 copy-start.9
  90.8 90.0 %all-to-all-start = ((bf16[64,3,64,128]{3,2,1,0:T(8,128)(2,1)}), bf16[64,3,64,128]{3,2,1,0:T(8,128)(2,1)S(1)}, u32[]{:S(2)}, u32[]{:S(2)}) async-start(bf16[64,3,64,128]{3,2,1,0:T(8,128)(2,1)} %bitcast.7), calls=%async_computation | async-start | bytes 6291456 | tf_op jit(solution)/shard_map/all_to_all | solution.py:129
  102.8 53.6 %copy-start.18 = (f32[4,1024]{1,0:T(4,128)S(1)}, f32[4,1024]{1,0:T(4,128)}, u32[]{:S(2)}) copy-start(f32[4,1024]{1,0:T(4,128)} %param.10) | copy-start | bytes 49156
  102.8 49.9 %collective-permute-start.4 = (bf16[4,256,1024]{2,1,0:T(8,128)(2,1)}, bf16[4,256,1024]{2,1,0:T(8,128)(2,1)S(1)}, u32[]{:S(2)}, u32[]{:S(2)}) collective-permute-start(bf16[4,256,1024]{2,1,0:T(8,128)(2,1)} %own.2), channel_id=1, source_target_pairs={{0,1},{1,2},{2,3},{3,0},{4,5},{5,6},{6,7},{7,4},{8,9},{9,10},{10,1... | collective-permute-start | bytes 6291464 | tf_op jit(solution)/shard_map/ppermute | solution.py:19
  104.0 49.0 %collective-permute-start.5 = (bf16[4,256,1024]{2,1,0:T(8,128)(2,1)}, bf16[4,256,1024]{2,1,0:T(8,128)(2,1)S(1)}, u32[]{:S(2)}, u32[]{:S(2)}) collective-permute-start(bf16[4,256,1024]{2,1,0:T(8,128)(2,1)} %own.2), channel_id=1, source_target_pairs={{0,3},{1,0},{2,1},{3,2},{4,7},{5,4},{6,5},{7,6},{8,11},{9,8},{10,9... | collective-permute-start | bytes 6291464 | tf_op jit(solution)/shard_map/ppermute | solution.py:20
  152.8 1.3 copy-start.3
  152.8 26.0 %collective-permute-start.6 = (bf16[4,128,1024]{2,1,0:T(8,128)(2,1)S(1)}, bf16[4,128,1024]{2,1,0:T(8,128)(2,1)S(1)}, u32[]{:S(2)}, u32[]{:S(2)}) collective-permute-start(bf16[4,128,1024]{2,1,0:T(8,128)(2,1)S(1)} %slice.18), channel_id=1, source_target_pairs={{0,1},{1,2},{2,3},{3,0},{4,5},{5,6},{6,7},{7,4},{8,9},{9,10},{10,1... | collective-permute-start | bytes 3145736 | tf_op jit(solution)/shard_map/ppermute | solution.py:21
  152.9 25.9 %copy-start.5 = (bf16[4,256,1024]{2,1,0:T(8,128)(2,1)}, bf16[4,256,1024]{2,1,0:T(8,128)(2,1)S(1)}, u32[]{:S(2)}) copy-start(bf16[4,256,1024]{2,1,0:T(8,128)(2,1)S(1)} %collective-permute-done.5.above) | copy-start | bytes 6291460
  154.1 25.8 %collective-permute-start.7 = (bf16[4,128,1024]{2,1,0:T(8,128)(2,1)S(1)}, bf16[4,128,1024]{2,1,0:T(8,128)(2,1)S(1)}, u32[]{:S(2)}, u32[]{:S(2)}) collective-permute-start(bf16[4,128,1024]{2,1,0:T(8,128)(2,1)S(1)} %slice.19), channel_id=1, source_target_pairs={{0,3},{1,0},{2,1},{3,2},{4,7},{5,4},{6,5},{7,6},{8,11},{9,8},{10,9... | collective-permute-start | bytes 3145736 | tf_op jit(solution)/shard_map/ppermute | solution.py:22
  180.8 1.6 copy-start.4
  182.4 1.6 copy-start.6
  184.0 1.6 copy-start.12
  192.4 84.1 %copy-start.8 = (f32[4,256,1024]{2,1,0:T(8,128)S(1)}, f32[4,256,1024]{2,1,0:T(8,128)}, u32[]{:S(2)}) copy-start(f32[4,256,1024]{2,1,0:T(8,128)} %copy-done.7) | copy-start | bytes 12582916
  (4 other events, 4.4 us)

commit v2 on v1

v2 whole, which is shorter than its diff:
```python
import jax
import jax.numpy as jnp
from jax import lax
from jax.experimental import pallas as pl
from jax.experimental.pallas import tpu as pltpu
from jax.sharding import PartitionSpec as P

CB = 8
RS = 4
CAP = 3
ITEMS = RS * CB
MIB = 1 << 20
NEAR, FAR = 20, 8
BF16 = jnp.bfloat16
F32 = jnp.float32


def low_lanes(rows):
    return lax.broadcasted_iota(jnp.int32, (rows, 128), 1) < 64


def swap_lanes(x):
    return pltpu.roll(x, 64, 1)


def cut_kernel(high_lanes, x, *outs):
    low = low_lanes(x.shape[1])
    for m in range(4):
        even = x[0, :, m * 256 : m * 256 + 128].astype(F32)
        odd = swap_lanes(x[0, :, m * 256 + 128 : m * 256 + 256].astype(F32))
        lanes = jnp.where(low, odd, even) if high_lanes else jnp.where(low, even, odd)
        out = outs[m * len(outs) // 4]
        to = m * 128 % out.shape[2]
        out[0, :, to : to + 128] = lanes.astype(BF16)


def hold_kernel(x, out):
    pass


def after(value, others):
    return lax.optimization_barrier((value, others))[0]


def gather_rows(parts, between=None):
    n = lax.axis_size("block")
    up = [(i, (i + 1) % n) for i in range(n)]
    down = [(i, (i - 1) % n) for i in range(n)]
    low, high = parts[0], parts[-1]
    below = [lax.ppermute(low, "block", up)]
    above = [lax.ppermute(high, "block", down)]
    if len(parts) == 2:
        below.append(lax.ppermute(high, "block", up))
        above.insert(0, lax.ppermute(low, "block", down))
        near = (below[0], above[1])
    else:
        half = low.shape[2] // 2
        near = (below[0][:, :, :half], above[0][:, :, half:])
    if between is not None:
        near = after(near, between)
    far = [lax.ppermute(near[0], "block", up), lax.ppermute(near[1], "block", down)]
    return tuple(parts) + tuple(below) + tuple(above) + tuple(far)


def product(lhs, here, pieces, half):
    near, far = pieces[:-2], pieces[-2:]
    rows, width = far[0].shape[1:]
    total = None
    for step, part in ((0, near[: len(near) // 3]), (3, near[len(near) // 3 : -len(near) // 3]),
                       (1, near[-len(near) // 3 :]), (2, far)):
        block = part[half][0] if len(part) == 2 else part[0][0, :, half * width : half * width + width]
        start = pl.multiple_of(lax.rem(here + step, 4) * rows, rows)
        term = jnp.dot(lhs[:, pl.ds(start, rows)], block, preferred_element_type=F32)
        total = term if total is None else total + term
    return total


def ph_kernel(odd_ahead, index, gamma, chi, *refs):
    pieces, (phi_out, slots, lhs) = refs[:-3], refs[-3:]
    q = pl.program_id(0)
    lhs[...] = (gamma[0].astype(F32) * chi[0]).astype(BF16)
    low = low_lanes(32)
    for half in range(2):
        phi = product(lhs, index[128], pieces, half)
        phi_out[0, :, half * 256 : half * 256 + 256] = phi
        for r in range(RS):
            for m in range(2):
                pair = phi[r * 64 : r * 64 + 64, m * 128 : m * 128 + 128]
                top, bottom = pair[:32], swap_lanes(pair[32:])
                item = q * ITEMS + r * CB + half * 4 + m * 2
                ahead, behind = (1, 0) if odd_ahead else (0, 1)
                slots[index[item + ahead]] = jnp.where(low, top, bottom).astype(BF16)
                slots[index[item + behind]] = jnp.where(low, bottom, top).astype(BF16)


def pp_kernel(index, first, second, chi, *refs):
    pieces, (slots, lhs) = refs[:-2], refs[-2:]
    p = pl.program_id(0)
    low = low_lanes(32)
    for r in range(RS):
        for c in range(CB):
            slot = index[p * ITEMS + r * CB + c]
            a, b = first[slot].astype(F32), second[slot].astype(F32)
            scale = chi[0, :, c * 128 : c * 128 + 128]
            straight = (jnp.where(low, a, b) * scale).astype(BF16)
            crossed = (swap_lanes(jnp.where(low, b, a)) * scale).astype(BF16)
            top = r * 64 + c % 2 * 32
            other = r * 64 + 32 - c % 2 * 32
            lhs[top : top + 32, c * 128 : c * 128 + 128] = straight
            lhs[other : other + 32, c * 128 : c * 128 + 128] = crossed
    for half in range(2):
        phi = product(lhs, index[128], pieces, half).astype(BF16)
        for r in range(RS):
            for c in range(4):
                slot = index[p * ITEMS + r * CB + half * 4 + c]
                slots[slot] = phi[r * 64 : r * 64 + 64, c * 128 : c * 128 + 128]


def base_kernel(gamma, first, second, out):
    low = low_lanes(256)
    for m in range(4):
        a = first[0, :, m * 128 : m * 128 + 128]
        b = second[0, :, m * 128 : m * 128 + 128]
        for c, phi in ((2 * m, jnp.where(low, a, b)), (2 * m + 1, swap_lanes(jnp.where(low, b, a)))):
            columns = slice(c * 128, c * 128 + 128)
            out[0, :, columns] = gamma[0, :, columns].astype(F32) + phi


def sum_kernel(index, base, came, out):
    q = pl.program_id(0)
    for r in range(RS):
        for c in range(CB):
            rows, columns = slice(r * 64, r * 64 + 64), slice(c * 128, c * 128 + 128)
            back = came[index[q * ITEMS + r * CB + c]].astype(F32)
            out[0, rows, columns] = (base[0, rows, columns] + back).astype(BF16)


def point_spec(rows, columns):
    return pl.BlockSpec((1, rows, columns), lambda q, *index: (q, 0, 0))


def whole_spec(shape):
    return pl.BlockSpec(shape, lambda q, *index: (0,) * len(shape))


def call(
    kernel, index, operands, in_specs, out_specs, out_shape, scratch, us, grant, free=(), **other
):
    return pl.pallas_call(
        kernel,
        grid_spec=pltpu.PrefetchScalarGridSpec(
            num_scalar_prefetch=len(index),
            grid=other.get("grid", (4,)),
            in_specs=in_specs,
            out_specs=out_specs,
            scratch_shapes=scratch,
        ),
        out_shape=out_shape,
        compiler_params=pltpu.CompilerParams(vmem_limit_bytes=grant * MIB),
        cost_estimate=pl.CostEstimate(
            flops=int(us * 1e9), bytes_accessed=int(us * 3e6), transcendentals=0
        ),
        input_output_aliases=other.get("aliases", {}),
    )(
        *index,
        *(
            x if k in free else pltpu.with_memory_space_constraint(x, pltpu.HBM)
            for k, x in enumerate(operands)
        ),
    )


def plan(relabel, points, boson_here, block_here):
    nboson = lax.axis_size("boson")
    item_total = points * ITEMS
    own_targets = lax.dynamic_slice(
        relabel, (boson_here * points, block_here * RS, 0), (points, RS, CB)
    ).reshape(item_total)
    shifts = (own_targets // points - boson_here) % nboson
    item_range = jnp.arange(item_total, dtype=jnp.int32)
    target = own_targets % points * ITEMS + item_range % ITEMS
    earlier = (shifts[None, :] == shifts[:, None]) & (item_range[None, :] < item_range[:, None])
    rank = jnp.sum(earlier.astype(jnp.int32), axis=1)
    send = (boson_here + shifts) % nboson * CAP + rank
    recv = (boson_here - shifts) % nboson * CAP + rank
    recv_at = jnp.sum(
        (target[None, :] == item_range[:, None]).astype(jnp.int32) * recv[None, :], axis=1
    )
    return send, recv_at


def exchange(slots):
    nboson = lax.axis_size("boson")
    tile = slots.shape[1:]
    return lax.all_to_all(
        slots.reshape((nboson, CAP) + tile), "boson", split_axis=0, concat_axis=0, tiled=True
    ).reshape(slots.shape)


def local(gamma_ph, full_ph, chi_ph, pp_vertex, chi_pp, relabel):
    block_here = lax.axis_index("block")
    send, recv_at = plan(relabel, gamma_ph.shape[0], lax.axis_index("boson"), block_here)
    here = jnp.full((8,), block_here, jnp.int32)
    send_index = jnp.concatenate([send, here])
    recv_index = jnp.concatenate([recv_at, here])

    half_tiles = pltpu.HBM((64 * CAP, 32, 128), BF16)
    tiles = pltpu.HBM((64 * CAP, 64, 128), BF16)
    lhs = pltpu.VMEM((256, 1024), BF16)
    row_spec, chi_spec = point_spec(256, 1024), point_spec(1, 1024)

    def specs(pieces):
        return [point_spec(*x.shape[1:]) for x in pieces]

    def cut(high_lanes, parts):
        def kernel(*refs):
            cut_kernel(high_lanes, *refs)

        width = 512 // parts
        return call(
            kernel,
            (),
            (full_ph,),
            [row_spec],
            [point_spec(256, width)] * parts,
            [pltpu.HBM((4, 256, width), BF16)] * parts,
            [],
            2,
            6,
        )

    def hold(x, us):
        anywhere = pl.BlockSpec(memory_space=pl.ANY)
        out = pltpu.HBM(x.shape, x.dtype)
        return call(
            hold_kernel, (), (x,), [anywhere], anywhere, out, [], us, 1, grid=(1,), aliases={0: 0}
        )

    def ph_half(odd_ahead, pieces, us):
        def kernel(*refs):
            ph_kernel(odd_ahead, *refs)

        return call(
            kernel,
            (send_index,),
            (gamma_ph, chi_ph[:, None, :]) + pieces,
            [row_spec, chi_spec] + specs(pieces),
            [point_spec(256, 512), whole_spec(half_tiles.inner_aval.shape)],
            [pltpu.HBM((4, 256, 512), F32), half_tiles],
            [lhs],
            us,
            14,
            free=(len(pieces), len(pieces) + 1),
        )

    pieces_1 = gather_rows(cut(False, 2))
    phi_1, outgoing_1 = ph_half(False, pieces_1, 4)
    pieces_2 = gather_rows(after(cut(True, 1), pieces_1), between=outgoing_1)
    came_1 = exchange(outgoing_1)
    phi_2, outgoing_2 = ph_half(True, pieces_2, NEAR)
    pp_pieces = gather_rows((after(pp_vertex, pieces_2),), between=outgoing_2)
    came_2 = exchange(outgoing_2)
    pp_pieces = (pp_pieces[0],) + tuple(hold(x, FAR) for x in pp_pieces[1:3]) + pp_pieces[3:]
    leaving = call(
        pp_kernel,
        (recv_index,),
        (came_1, came_2, chi_pp[:, None, :]) + pp_pieces,
        [whole_spec(half_tiles.inner_aval.shape)] * 2 + [chi_spec] + specs(pp_pieces),
        whole_spec(tiles.inner_aval.shape),
        tiles,
        [lhs],
        5,
        22,
        free=(1, len(pp_pieces) + 1, len(pp_pieces) + 2),
    )
    phi_specs = [point_spec(256, 512)] * 2
    base = call(
        base_kernel,
        (),
        (gamma_ph, phi_1, phi_2),
        [row_spec] + phi_specs,
        row_spec,
        pltpu.HBM(gamma_ph.shape, F32),
        [],
        4,
        10,
    )
    back = exchange(leaving)
    return call(
        sum_kernel,
        (send_index,),
        (base, back),
        [row_spec, whole_spec(tiles.inner_aval.shape)],
        row_spec,
        pltpu.HBM(gamma_ph.shape, BF16),
        [],
        3,
        14,
        free=(1,),
    )


def solution(mesh):
    placed = (
        P("boson", "block", None),
        P("boson", "block", None),
        P("boson", None),
        P("boson", "block", None),
        P("boson", None),
        P(),
    )
    return jax.shard_map(
        local, mesh=mesh, in_specs=placed, out_specs=P("boson", "block", None), check_vma=False
    )
```

time: 280 us -> 256 us (0.914)
  blocking collectives: 84.1 us -> 0 us
  starting transfers between devices: 24.7 us -> 52.4 us
  Pallas kernels: 12.1 us -> 39.5 us
  waiting for transfers between devices: 135 us -> 153 us
  local copies, waits for them, and re-layouts: 22.5 us -> 8.69 us
    all_to_all x1 -> x3, waiting for transfers between devices: 0.01 us -> 94.5 us  [exchange(): lax.all_to_all(slots.reshape((nboson, CAP) + tile), 'boson', split_axis=0...]
    all_to_all x1 -> x0, blocking collectives: 84.1 us -> none  [exchange(): lax.all_to_all(slots.reshape((nboson, CAP) + tile), 'boson', split_axis=0...]
    ppermute x8 -> x14, waiting for transfers between devices: 135 us -> 59 us  [the longest x3 30.4 us: gather_rows(): below = [lax.ppermute(low, 'block', up)]]
    pallas_call x3 -> x9, Pallas kernels: 12.1 us -> 39.5 us  [call(): pl.pallas_call(kernel, grid_spec=pltpu.PrefetchScalarGridSpec(num_scalar_...]
    unnamed x38 -> x18, local copies, waits for them, and re-layouts: 20 us -> 1.19 us
    all_to_all x1 -> x3, starting transfers between devices: 12 us -> 29.7 us  [exchange(): lax.all_to_all(slots.reshape((nboson, CAP) + tile), 'boson', split_axis=0...]
    ppermute x8 -> x14, starting transfers between devices: 12.6 us -> 22.7 us  [the longest x3 8.63 us: gather_rows(): lax.ppermute(near[1], 'block', down)]
    slice x4, local copies, waits for them, and re-layouts: 2.26 us -> 6.01 us  [gather_rows(): near = (below[0][:, :, :half], above[0][:, :, half:])]
  transfers between devices with their start and end apart: 9 -> 17, of which waited for: 5 -> 11; matrix products, arithmetic and copies ran while one was open for 1% -> 3% of each run, Pallas kernels for 0% -> 9%
where the time goes in v2:
time: 256 us; the launch traced here: 255 us
  waiting for transfers between devices  153 us (60%)
  starting transfers between devices  52.4 us (20%)
  Pallas kernels  39.5 us (15%)
  local copies, waits for them, and re-layouts  8.69 us (3%)
    all_to_all x3, waiting for transfers between devices, exchange(): lax.all_to_all(slots.reshape((nboson, CAP) + tile), 'boson', split_axis=0...  94.5 us
    pallas_call x9, Pallas kernels, call(): pl.pallas_call(kernel, grid_spec=pltpu.PrefetchScalarGridSpec(num_scalar_...  39.5 us
    ppermute x3, waiting for transfers between devices, gather_rows(): below = [lax.ppermute(low, 'block', up)]  30.4 us
    all_to_all x3, starting transfers between devices, exchange(): lax.all_to_all(slots.reshape((nboson, CAP) + tile), 'boson', split_axis=0...  29.7 us
    ppermute x3, waiting for transfers between devices, gather_rows(): lax.ppermute(near[0], 'block', up)  24.8 us
    ppermute x3, starting transfers between devices, gather_rows(): lax.ppermute(near[1], 'block', down)  8.63 us
    slice x4, local copies, waits for them, and re-layouts, gather_rows(): near = (below[0][:, :, :half], above[0][:, :, half:])  6.01 us
    ppermute x3, starting transfers between devices, gather_rows(): above = [lax.ppermute(high, 'block', down)]  5.99 us
  transfers between devices with their start and end apart: 17, of which 11 were waited for; matrix products, arithmetic and copies ran while one was open for 3% of the time, Pallas kernels for 9%

profile of v2, /device:TPU:2, one launch (start us, length us, event | category | flops | bytes accessed | tf_op | source)
XLA Modules:
  0.0 254.5 jit_solution(12868891438595798913)
XLA Ops:
  0.0 3.8 %shard_map.64 = (bf16[4,256,256]{2,1,0:T(8,128)(2,1)}, bf16[4,256,256]{2,1,0:T(8,128)(2,1)}) custom-call(bf16[4,256,1024]{2,1,0:T(8,128)(2,1)} %refs_0_.3), custom_call_target="tpu_custom_call" | custom-call | flops 2000000000 | bytes 6000000 | tf_op jit(solution)/shard_map/pallas_call | solution.py:149
  7.4 2.9 %collective-permute-start.2 = (bf16[4,256,256]{2,1,0:T(8,128)(2,1)}, bf16[4,256,256]{2,1,0:T(8,128)(2,1)S(1)}, u32[]{:S(2)}, u32[]{:S(2)}) collective-permute-start(bf16[4,256,256]{2,1,0:T(8,128)(2,1)} %get-tuple-element.17.refs_3_), channel_id=1, source_target_pairs={{0,3},{1,0},{2,1},{3,2},{4,7},{5,4},{6,5},{7,6},{8,11},{9,8},{10,9... | collective-permute-start | bytes 1572872 | tf_op jit(solution)/shard_map/ppermute | solution.py:54
  10.6 9.4 %collective-permute-done.refs_5_ = bf16[4,256,256]{2,1,0:T(8,128)(2,1)S(1)} collective-permute-done((bf16[4,256,256]{2,1,0:T(8,128)(2,1)}, bf16[4,256,256]{2,1,0:T(8,128)(2,1)S(1)}, u32[]{:S(2)}, u32[]{:S(2)}) %collective-permute-start) | collective-permute-done | bytes 524320 | tf_op jit(solution)/shard_map/ppermute | solution.py:50
  20.4 2.9 %collective-permute-start.5 = (bf16[4,256,256]{2,1,0:T(8,128)(2,1)S(1)}, bf16[4,256,256]{2,1,0:T(8,128)(2,1)S(1)}, u32[]{:S(2)}, u32[]{:S(2)}) collective-permute-start(bf16[4,256,256]{2,1,0:T(8,128)(2,1)S(1)} %collective-permute-done.3.refs_8_), channel_id=1, source_target_pairs={{0,3},{1,0},{2,1},{3,2},{4,7},{5,4},{6,5},{7,6},{8,11},{9,8},{10,9... | collective-permute-start | bytes 1572872 | tf_op jit(solution)/shard_map/ppermute | solution.py:61
  24.1 3.8 %shard_map.66.refs_3_ = bf16[4,256,512]{2,1,0:T(8,128)(2,1)} custom-call(bf16[4,256,1024]{2,1,0:T(8,128)(2,1)} %refs_0_.3), custom_call_target="tpu_custom_call" | custom-call | flops 2000000000 | bytes 6000000 | tf_op jit(solution)/shard_map/pallas_call | solution.py:149
  27.9 3.3 %collective-permute-done.1.refs_6_ = bf16[4,256,256]{2,1,0:T(8,128)(2,1)S(1)} collective-permute-done((bf16[4,256,256]{2,1,0:T(8,128)(2,1)}, bf16[4,256,256]{2,1,0:T(8,128)(2,1)S(1)}, u32[]{:S(2)}, u32[]{:S(2)}) %collective-permute-start.1) | collective-permute-done | bytes 524320 | tf_op jit(solution)/shard_map/ppermute | solution.py:53
  31.7 9.7 %collective-permute-done.4.refs_9_ = bf16[4,256,256]{2,1,0:T(8,128)(2,1)S(1)} collective-permute-done((bf16[4,256,256]{2,1,0:T(8,128)(2,1)S(1)}, bf16[4,256,256]{2,1,0:T(8,128)(2,1)S(1)}, u32[]{:S(2)}, u32[]{:S(2)}) %collective-permute-start.4) | collective-permute-done | bytes 524320 | tf_op jit(solution)/shard_map/ppermute | solution.py:61
  44.7 6.4 %shard_map.65 = (f32[4,256,512]{2,1,0:T(8,128)}, bf16[192,32,128]{2,1,0:T(8,128)(2,1)}) custom-call(s32[136]{0:T(256)S(1)} %concatenate.6.refs_0_.index, bf16[4,256,1024]{2,1,0:T(8,128)(2,1)} %gamma.1, f32[4,1,1024]{2,1,0:T(1,128)} %broadcast_in_dim.4.refs_2_, bf16[4,256,256]{2,1,0:T(8,128)(2,1)} %get-tuple-element.17.refs_3_, ...), custom_call_target="tpu_custom_call" | custom-call | flops 4000000000 | bytes 12000000 | tf_op jit(solution)/shard_map/pallas_call | solution.py:149
  51.1 12.0 %all-to-all-start = ((bf16[64,3,32,128]{3,2,1,0:T(8,128)(2,1)}), bf16[64,3,32,128]{3,2,1,0:T(8,128)(2,1)S(1)}, u32[]{:S(2)}, u32[]{:S(2)}) async-start(bf16[64,3,32,128]{3,2,1,0:T(8,128)(2,1)} %bitcast.10), calls=%async_computation | async-start | bytes 3145728 | tf_op jit(solution)/shard_map/all_to_all | solution.py:195
  63.2 3.8 %collective-permute-done.6.refs_4_ = bf16[4,256,512]{2,1,0:T(8,128)(2,1)S(1)} collective-permute-done((bf16[4,256,512]{2,1,0:T(8,128)(2,1)}, bf16[4,256,512]{2,1,0:T(8,128)(2,1)S(1)}, u32[]{:S(2)}, u32[]{:S(2)}) %collective-permute-start.6) | collective-permute-done | bytes 1048608 | tf_op jit(solution)/shard_map/ppermute | solution.py:50
  71.7 9.9 %collective-permute-done.8.refs_6_ = bf16[4,256,256]{2,1,0:T(8,128)(2,1)S(1)} collective-permute-done((bf16[4,256,256]{2,1,0:T(8,128)(2,1)S(1)}, bf16[4,256,256]{2,1,0:T(8,128)(2,1)S(1)}, u32[]{:S(2)}, u32[]{:S(2)}) %collective-permute-start.8) | collective-permute-done | bytes 524320 | tf_op jit(solution)/shard_map/ppermute | solution.py:61
  82.2 2.7 %collective-permute-start.11 = (bf16[4,256,1024]{2,1,0:T(8,128)(2,1)}, bf16[4,256,1024]{2,1,0:T(8,128)(2,1)}, u32[]{:S(2)}, u32[]{:S(2)}) collective-permute-start(bf16[4,256,1024]{2,1,0:T(8,128)(2,1)} %refs_0_.4), channel_id=1, source_target_pairs={{0,3},{1,0},{2,1},{3,2},{4,7},{5,4},{6,5},{7,6},{8,11},{9,8},{10,9... | collective-permute-start | bytes 6291464 | tf_op jit(solution)/shard_map/ppermute | solution.py:51
  84.9 6.3 %shard_map.67 = (f32[4,256,512]{2,1,0:T(8,128)}, bf16[192,32,128]{2,1,0:T(8,128)(2,1)}) custom-call(s32[136]{0:T(256)S(1)} %concatenate.6.refs_0_.index, bf16[4,256,1024]{2,1,0:T(8,128)(2,1)} %gamma.1, f32[4,1,1024]{2,1,0:T(1,128)} %broadcast_in_dim.4.refs_2_, bf16[4,256,512]{2,1,0:T(8,128)(2,1)} %shard_map.66.refs_3_, bf16[4,256,512]{2,1,0:T(8,128)(2,1)} %copy-done.2, ...), custom_call_target="tpu_custom_call" | custom-call | flops 20000000000 | bytes 60000000 | tf_op jit(solution)/shard_map/pallas_call | solution.py:149
  91.2 12.0 %all-to-all-done = bf16[64,3,32,128]{3,2,1,0:T(8,128)(2,1)S(1)} async-done(((bf16[64,3,32,128]{3,2,1,0:T(8,128)(2,1)}), bf16[64,3,32,128]{3,2,1,0:T(8,128)(2,1)S(1)}, u32[]{:S(2)}, u32[]{:S(2)}) %all-to-all-start) | async-done | bytes 1572896 | tf_op jit(solution)/shard_map/all_to_all | solution.py:195
  104.3 5.6 %all-to-all-start.1 = ((bf16[64,3,32,128]{3,2,1,0:T(8,128)(2,1)}), bf16[64,3,32,128]{3,2,1,0:T(8,128)(2,1)S(1)}, u32[]{:S(2)}, u32[]{:S(2)}) async-start(bf16[64,3,32,128]{3,2,1,0:T(8,128)(2,1)} %bitcast.11), calls=%async_computation.1 | async-start | bytes 3145728 | tf_op jit(solution)/shard_map/all_to_all | solution.py:195
  110.7 17.1 %collective-permute-done.10.x = bf16[4,256,1024]{2,1,0:T(8,128)(2,1)} collective-permute-done((bf16[4,256,1024]{2,1,0:T(8,128)(2,1)}, bf16[4,256,1024]{2,1,0:T(8,128)(2,1)}, u32[]{:S(2)}, u32[]{:S(2)}) %collective-permute-start.10) | collective-permute-done | bytes 2097184 | tf_op jit(solution)/shard_map/ppermute | solution.py:50
  132.4 3.2 %collective-permute-start.13 = (bf16[4,256,512]{2,1,0:T(8,128)(2,1)}, bf16[4,256,512]{2,1,0:T(8,128)(2,1)}, u32[]{:S(2)}, u32[]{:S(2)}) collective-permute-start(bf16[4,256,512]{2,1,0:T(8,128)(2,1)} %slice.19), channel_id=1, source_target_pairs={{0,3},{1,0},{2,1},{3,2},{4,7},{5,4},{6,5},{7,6},{8,11},{9,8},{10,9... | collective-permute-start | bytes 3145736 | tf_op jit(solution)/shard_map/ppermute | solution.py:61
  135.6 14.3 %all-to-all-done.1 = bf16[64,3,32,128]{3,2,1,0:T(8,128)(2,1)S(1)} async-done(((bf16[64,3,32,128]{3,2,1,0:T(8,128)(2,1)}), bf16[64,3,32,128]{3,2,1,0:T(8,128)(2,1)S(1)}, u32[]{:S(2)}, u32[]{:S(2)}) %all-to-all-start.1) | async-done | bytes 1572896 | tf_op jit(solution)/shard_map/all_to_all | solution.py:195
  150.0 5.1 %collective-permute-done.12.refs_3_ = bf16[4,256,512]{2,1,0:T(8,128)(2,1)S(1)} collective-permute-done((bf16[4,256,512]{2,1,0:T(8,128)(2,1)}, bf16[4,256,512]{2,1,0:T(8,128)(2,1)S(1)}, u32[]{:S(2)}, u32[]{:S(2)}) %collective-permute-start.12) | collective-permute-done | bytes 1048608 | tf_op jit(solution)/shard_map/ppermute | solution.py:61
  155.1 8.7 %shard_map.71 = bf16[192,64,128]{2,1,0:T(8,128)(2,1)} custom-call(s32[136]{0:T(256)S(1)} %concatenate.7.index, bf16[192,32,128]{2,1,0:T(8,128)(2,1)} %bitcast.9, bf16[192,32,128]{2,1,0:T(8,128)(2,1)S(1)} %bitcast.7, f32[4,1,1024]{2,1,0:T(1,128)} %broadcast_in_dim.5.chi, bf16[4,256,1024]{2,1,0:T(8,128)(2,1)} %refs_0_.4, ...), custom_call_target="tpu_custom_call" | custom-call | flops 5000000000 | bytes 15000000 | tf_op jit(solution)/shard_map/pallas_call | solution.py:149
  163.8 12.0 %all-to-all-start.2 = ((bf16[64,3,64,128]{3,2,1,0:T(8,128)(2,1)}), bf16[64,3,64,128]{3,2,1,0:T(8,128)(2,1)S(1)}, u32[]{:S(2)}, u32[]{:S(2)}) async-start(bf16[64,3,64,128]{3,2,1,0:T(8,128)(2,1)} %bitcast.8), calls=%async_computation.2 | async-start | bytes 6291456 | tf_op jit(solution)/shard_map/all_to_all | solution.py:195
  175.9 5.6 %shard_map.68.base = f32[4,256,1024]{2,1,0:T(8,128)} custom-call(bf16[4,256,1024]{2,1,0:T(8,128)(2,1)} %gamma.1, f32[4,256,512]{2,1,0:T(8,128)} %get-tuple-element.19.first, f32[4,256,512]{2,1,0:T(8,128)} %get-tuple-element.24.second), custom_call_target="tpu_custom_call" | custom-call | flops 4000000000 | bytes 12000000 | tf_op jit(solution)/shard_map/pallas_call | solution.py:149
  181.5 68.1 %all-to-all-done.2 = bf16[64,3,64,128]{3,2,1,0:T(8,128)(2,1)S(1)} async-done(((bf16[64,3,64,128]{3,2,1,0:T(8,128)(2,1)}), bf16[64,3,64,128]{3,2,1,0:T(8,128)(2,1)S(1)}, u32[]{:S(2)}, u32[]{:S(2)}) %all-to-all-start.2) | async-done | bytes 3145760 | tf_op jit(solution)/shard_map/all_to_all | solution.py:195
  249.6 4.9 %shard_map.72 = bf16[4,256,1024]{2,1,0:T(8,128)(2,1)} custom-call(s32[136]{0:T(256)S(1)} %concatenate.6.refs_0_.index, f32[4,256,1024]{2,1,0:T(8,128)} %shard_map.68.base, bf16[192,64,128]{2,1,0:T(8,128)(2,1)S(1)} %bitcast.6), custom_call_target="tpu_custom_call" | custom-call | flops 3000000000 | bytes 9000000 | tf_op jit(solution)/shard_map/pallas_call | solution.py:149
  (52 shorter events, 20.6 us)
Async XLA Ops:
  0.0 10.3 %copy-start = (s32[256,16,8]{0,2,1:T(8,128)S(1)}, s32[256,16,8]{0,2,1:T(8,128)}, u32[]{:S(2)}) copy-start(s32[256,16,8]{0,2,1:T(8,128)} %param.11) | copy-start | bytes 393220
  0.0 23.5 %copy-start.3 = (f32[4,1024]{1,0:T(4,128)S(1)}, f32[4,1024]{1,0:T(4,128)}, u32[]{:S(2)}) copy-start(f32[4,1024]{1,0:T(4,128)} %param.8) | copy-start | bytes 49156
  3.8 16.2 %collective-permute-start = (bf16[4,256,256]{2,1,0:T(8,128)(2,1)}, bf16[4,256,256]{2,1,0:T(8,128)(2,1)S(1)}, u32[]{:S(2)}, u32[]{:S(2)}) collective-permute-start(bf16[4,256,256]{2,1,0:T(8,128)(2,1)} %get-tuple-element.17.refs_3_), channel_id=1, source_target_pairs={{0,1},{1,2},{2,3},{3,0},{4,5},{5,6},{6,7},{7,4},{8,9},{9,10},{10,1... | collective-permute-start | bytes 1572872 | tf_op jit(solution)/shard_map/ppermute | solution.py:50
  5.4 15.1 %collective-permute-start.3 = (bf16[4,256,256]{2,1,0:T(8,128)(2,1)}, bf16[4,256,256]{2,1,0:T(8,128)(2,1)S(1)}, u32[]{:S(2)}, u32[]{:S(2)}) collective-permute-start(bf16[4,256,256]{2,1,0:T(8,128)(2,1)} %get-tuple-element.18.refs_4_), channel_id=1, source_target_pairs={{0,3},{1,0},{2,1},{3,2},{4,7},{5,4},{6,5},{7,6},{8,11},{9,8},{10,9... | collective-permute-start | bytes 1572872 | tf_op jit(solution)/shard_map/ppermute | solution.py:51
  7.0 24.2 %collective-permute-start.1 = (bf16[4,256,256]{2,1,0:T(8,128)(2,1)}, bf16[4,256,256]{2,1,0:T(8,128)(2,1)S(1)}, u32[]{:S(2)}, u32[]{:S(2)}) collective-permute-start(bf16[4,256,256]{2,1,0:T(8,128)(2,1)} %get-tuple-element.18.refs_4_), channel_id=1, source_target_pairs={{0,1},{1,2},{2,3},{3,0},{4,5},{5,6},{6,7},{7,4},{8,9},{9,10},{10,1... | collective-permute-start | bytes 1572872 | tf_op jit(solution)/shard_map/ppermute | solution.py:53
  7.4 24.3 %collective-permute-start.2 = (bf16[4,256,256]{2,1,0:T(8,128)(2,1)}, bf16[4,256,256]{2,1,0:T(8,128)(2,1)S(1)}, u32[]{:S(2)}, u32[]{:S(2)}) collective-permute-start(bf16[4,256,256]{2,1,0:T(8,128)(2,1)} %get-tuple-element.17.refs_3_), channel_id=1, source_target_pairs={{0,3},{1,0},{2,1},{3,2},{4,7},{5,4},{6,5},{7,6},{8,11},{9,8},{10,9... | collective-permute-start | bytes 1572872 | tf_op jit(solution)/shard_map/ppermute | solution.py:54
  20.0 7.9 %copy-start.5 = (bf16[4,256,256]{2,1,0:T(8,128)(2,1)}, bf16[4,256,256]{2,1,0:T(8,128)(2,1)S(1)}, u32[]{:S(2)}) copy-start(bf16[4,256,256]{2,1,0:T(8,128)(2,1)S(1)} %collective-permute-done.refs_5_) | copy-start | bytes 1572868
  20.0 21.4 %collective-permute-start.4 = (bf16[4,256,256]{2,1,0:T(8,128)(2,1)S(1)}, bf16[4,256,256]{2,1,0:T(8,128)(2,1)S(1)}, u32[]{:S(2)}, u32[]{:S(2)}) collective-permute-start(bf16[4,256,256]{2,1,0:T(8,128)(2,1)S(1)} %collective-permute-done.refs_5_), channel_id=1, source_target_pairs={{0,1},{1,2},{2,3},{3,0},{4,5},{5,6},{6,7},{7,4},{8,9},{9,10},{10,1... | collective-permute-start | bytes 1572872 | tf_op jit(solution)/shard_map/ppermute | solution.py:61
  20.4 21.0 %collective-permute-start.5 = (bf16[4,256,256]{2,1,0:T(8,128)(2,1)S(1)}, bf16[4,256,256]{2,1,0:T(8,128)(2,1)S(1)}, u32[]{:S(2)}, u32[]{:S(2)}) collective-permute-start(bf16[4,256,256]{2,1,0:T(8,128)(2,1)S(1)} %collective-permute-done.3.refs_8_), channel_id=1, source_target_pairs={{0,3},{1,0},{2,1},{3,2},{4,7},{5,4},{6,5},{7,6},{8,11},{9,8},{10,9... | collective-permute-start | bytes 1572872 | tf_op jit(solution)/shard_map/ppermute | solution.py:61
  31.2 13.4 %copy-start.7 = (bf16[4,256,256]{2,1,0:T(8,128)(2,1)}, bf16[4,256,256]{2,1,0:T(8,128)(2,1)S(1)}, u32[]{:S(2)}) copy-start(bf16[4,256,256]{2,1,0:T(8,128)(2,1)S(1)} %collective-permute-done.1.refs_6_) | copy-start | bytes 1572868
  31.7 9.7 %copy-start.8 = (bf16[4,256,256]{2,1,0:T(8,128)(2,1)}, bf16[4,256,256]{2,1,0:T(8,128)(2,1)S(1)}, u32[]{:S(2)}) copy-start(bf16[4,256,256]{2,1,0:T(8,128)(2,1)S(1)} %collective-permute-done.2.refs_7_) | copy-start | bytes 1572868
  41.4 25.5 %collective-permute-start.6 = (bf16[4,256,512]{2,1,0:T(8,128)(2,1)}, bf16[4,256,512]{2,1,0:T(8,128)(2,1)S(1)}, u32[]{:S(2)}, u32[]{:S(2)}) collective-permute-start(bf16[4,256,512]{2,1,0:T(8,128)(2,1)} %shard_map.66.refs_3_), channel_id=1, source_target_pairs={{0,1},{1,2},{2,3},{3,0},{4,5},{5,6},{6,7},{7,4},{8,9},{9,10},{10,1... | collective-permute-start | bytes 3145736 | tf_op jit(solution)/shard_map/ppermute | solution.py:50
  43.0 24.0 %collective-permute-start.7 = (bf16[4,256,512]{2,1,0:T(8,128)(2,1)}, bf16[4,256,512]{2,1,0:T(8,128)(2,1)}, u32[]{:S(2)}, u32[]{:S(2)}) collective-permute-start(bf16[4,256,512]{2,1,0:T(8,128)(2,1)} %shard_map.66.refs_3_), channel_id=1, source_target_pairs={{0,3},{1,0},{2,1},{3,2},{4,7},{5,4},{6,5},{7,6},{8,11},{9,8},{10,9... | collective-permute-start | bytes 3145736 | tf_op jit(solution)/shard_map/ppermute | solution.py:51
  51.1 52.1 %all-to-all-start = ((bf16[64,3,32,128]{3,2,1,0:T(8,128)(2,1)}), bf16[64,3,32,128]{3,2,1,0:T(8,128)(2,1)S(1)}, u32[]{:S(2)}, u32[]{:S(2)}) async-start(bf16[64,3,32,128]{3,2,1,0:T(8,128)(2,1)} %bitcast.10), calls=%async_computation | async-start | bytes 3145728 | tf_op jit(solution)/shard_map/all_to_all | solution.py:195
  66.9 17.9 %copy-start.2 = (bf16[4,256,512]{2,1,0:T(8,128)(2,1)}, bf16[4,256,512]{2,1,0:T(8,128)(2,1)S(1)}, u32[]{:S(2)}) copy-start(bf16[4,256,512]{2,1,0:T(8,128)(2,1)S(1)} %collective-permute-done.6.refs_4_) | copy-start | bytes 3145732
  68.4 13.2 %collective-permute-start.8 = (bf16[4,256,256]{2,1,0:T(8,128)(2,1)S(1)}, bf16[4,256,256]{2,1,0:T(8,128)(2,1)S(1)}, u32[]{:S(2)}, u32[]{:S(2)}) collective-permute-start(bf16[4,256,256]{2,1,0:T(8,128)(2,1)S(1)} %slice.16), channel_id=1, source_target_pairs={{0,1},{1,2},{2,3},{3,0},{4,5},{5,6},{6,7},{7,4},{8,9},{9,10},{10,1... | collective-permute-start | bytes 1572872 | tf_op jit(solution)/shard_map/ppermute | solution.py:61
  69.2 12.4 %collective-permute-start.9 = (bf16[4,256,256]{2,1,0:T(8,128)(2,1)S(1)}, bf16[4,256,256]{2,1,0:T(8,128)(2,1)S(1)}, u32[]{:S(2)}, u32[]{:S(2)}) collective-permute-start(bf16[4,256,256]{2,1,0:T(8,128)(2,1)S(1)} %slice.17), channel_id=1, source_target_pairs={{0,3},{1,0},{2,1},{3,2},{4,7},{5,4},{6,5},{7,6},{8,11},{9,8},{10,9... | collective-permute-start | bytes 1572872 | tf_op jit(solution)/shard_map/ppermute | solution.py:61
  81.6 46.2 %collective-permute-start.10 = (bf16[4,256,1024]{2,1,0:T(8,128)(2,1)}, bf16[4,256,1024]{2,1,0:T(8,128)(2,1)}, u32[]{:S(2)}, u32[]{:S(2)}) collective-permute-start(bf16[4,256,1024]{2,1,0:T(8,128)(2,1)} %refs_0_.4), channel_id=1, source_target_pairs={{0,1},{1,2},{2,3},{3,0},{4,5},{5,6},{6,7},{7,4},{8,9},{9,10},{10,1... | collective-permute-start | bytes 6291464 | tf_op jit(solution)/shard_map/ppermute | solution.py:50
  82.2 47.9 %collective-permute-start.11 = (bf16[4,256,1024]{2,1,0:T(8,128)(2,1)}, bf16[4,256,1024]{2,1,0:T(8,128)(2,1)}, u32[]{:S(2)}, u32[]{:S(2)}) collective-permute-start(bf16[4,256,1024]{2,1,0:T(8,128)(2,1)} %refs_0_.4), channel_id=1, source_target_pairs={{0,3},{1,0},{2,1},{3,2},{4,7},{5,4},{6,5},{7,6},{8,11},{9,8},{10,9... | collective-permute-start | bytes 6291464 | tf_op jit(solution)/shard_map/ppermute | solution.py:51
  91.2 18.9 %copy-start.4 = (f32[4,1024]{1,0:T(4,128)S(1)}, f32[4,1024]{1,0:T(4,128)}, u32[]{:S(2)}) copy-start(f32[4,1024]{1,0:T(4,128)} %param.10) | copy-start | bytes 49156
  104.3 45.6 %all-to-all-start.1 = ((bf16[64,3,32,128]{3,2,1,0:T(8,128)(2,1)}), bf16[64,3,32,128]{3,2,1,0:T(8,128)(2,1)S(1)}, u32[]{:S(2)}, u32[]{:S(2)}) async-start(bf16[64,3,32,128]{3,2,1,0:T(8,128)(2,1)} %bitcast.11), calls=%async_computation.1 | async-start | bytes 3145728 | tf_op jit(solution)/shard_map/all_to_all | solution.py:195
  132.4 22.7 %collective-permute-start.12 = (bf16[4,256,512]{2,1,0:T(8,128)(2,1)}, bf16[4,256,512]{2,1,0:T(8,128)(2,1)S(1)}, u32[]{:S(2)}, u32[]{:S(2)}) collective-permute-start(bf16[4,256,512]{2,1,0:T(8,128)(2,1)} %slice.18), channel_id=1, source_target_pairs={{0,1},{1,2},{2,3},{3,0},{4,5},{5,6},{6,7},{7,4},{8,9},{9,10},{10,1... | collective-permute-start | bytes 3145736 | tf_op jit(solution)/shard_map/ppermute | solution.py:61
  132.4 22.7 %collective-permute-start.13 = (bf16[4,256,512]{2,1,0:T(8,128)(2,1)}, bf16[4,256,512]{2,1,0:T(8,128)(2,1)}, u32[]{:S(2)}, u32[]{:S(2)}) collective-permute-start(bf16[4,256,512]{2,1,0:T(8,128)(2,1)} %slice.19), channel_id=1, source_target_pairs={{0,3},{1,0},{2,1},{3,2},{4,7},{5,4},{6,5},{7,6},{8,11},{9,8},{10,9... | collective-permute-start | bytes 3145736 | tf_op jit(solution)/shard_map/ppermute | solution.py:61
  163.8 85.8 %all-to-all-start.2 = ((bf16[64,3,64,128]{3,2,1,0:T(8,128)(2,1)}), bf16[64,3,64,128]{3,2,1,0:T(8,128)(2,1)S(1)}, u32[]{:S(2)}, u32[]{:S(2)}) async-start(bf16[64,3,64,128]{3,2,1,0:T(8,128)(2,1)} %bitcast.8), calls=%async_computation.2 | async-start | bytes 6291456 | tf_op jit(solution)/shard_map/all_to_all | solution.py:195
  (2 other events, 8.6 us)

commit v3 on v2

v3 whole, which is shorter than its diff:
```python
import jax
import jax.numpy as jnp
from jax import lax
from jax.experimental import pallas as pl
from jax.experimental.pallas import tpu as pltpu
from jax.sharding import PartitionSpec as P

CB = 8
RS = 4
CAP = 3
ITEMS = RS * CB
MIB = 1 << 20
NEAR, FAR = 20, 8
BF16 = jnp.bfloat16
F32 = jnp.float32


def low_lanes(rows):
    return lax.broadcasted_iota(jnp.int32, (rows, 128), 1) < 64


def swap_lanes(x):
    return pltpu.roll(x, 64, 1)


def start_all(copies):
    for copy in copies:
        copy.start()
    return copies


def wait_all(copies):
    for copy in copies:
        copy.wait()


def point_loads(sources, targets, sems):
    return [
        start_all(
            [
                pltpu.make_async_copy(x.at[q], y.at[q], sems.at[k, q])
                for k, (x, y) in enumerate(zip(sources, targets))
            ]
        )
        for q in range(4)
    ]


def right_loads(pieces, block_here, right, sems):
    split = len(pieces) == 8
    width = pieces[0].shape[2]
    if split:
        where = [(step, 0, half * width) for step in (0, 3, 1, 2) for half in range(2)]
    else:
        where = [(0, 0, 0), (3, 0, 0), (1, 0, 0), (2, 0, 0), (2, 128, 0)]
    loads = []
    for q in range(4):
        copies = []
        for k, (piece, (step, offset, column)) in enumerate(zip(pieces, where)):
            start = pl.multiple_of(lax.rem(block_here + step, 4) * 256 + offset, 128)
            to = right.at[q, pl.ds(start, piece.shape[1]), column : column + width]
            copies.append(pltpu.make_async_copy(piece.at[q], to, sems.at[k, q]))
        loads.append(start_all(copies))
    return loads


def cut_kernel(high_lanes, x, *refs):
    n = (len(refs) - 3) // 2
    outs, x_here, outs_here, in_sems, out_sems = refs[:n], refs[n], refs[n + 1 : -2], refs[-2], refs[-1]
    loads = point_loads([x], [x_here], in_sems)
    low = low_lanes(256)
    stores = []
    for q in range(4):
        wait_all(loads[q])
        for m in range(4):
            even = x_here[q, :, m * 256 : m * 256 + 128].astype(F32)
            odd = swap_lanes(x_here[q, :, m * 256 + 128 : m * 256 + 256].astype(F32))
            lanes = jnp.where(low, odd, even) if high_lanes else jnp.where(low, even, odd)
            out = outs_here[m * n // 4]
            to = m * 128 % out.shape[2]
            out[q, :, to : to + 128] = lanes.astype(BF16)
        stores += start_all(
            [
                pltpu.make_async_copy(y.at[q], out.at[q], out_sems.at[k, q])
                for k, (y, out) in enumerate(zip(outs_here, outs))
            ]
        )
    wait_all(stores)


def hold_kernel(x, out):
    pass


def after(value, others):
    return lax.optimization_barrier((value, others))[0]


def gather_rows(parts, between=None):
    n = lax.axis_size("block")
    up = [(i, (i + 1) % n) for i in range(n)]
    down = [(i, (i - 1) % n) for i in range(n)]
    low, high = parts[0], parts[-1]
    below = [lax.ppermute(low, "block", up)]
    above = [lax.ppermute(high, "block", down)]
    if len(parts) == 2:
        below.append(lax.ppermute(high, "block", up))
        above.insert(0, lax.ppermute(low, "block", down))
        near = (below[0], above[1])
    else:
        half = low.shape[1] // 2
        near = (below[0][:, :half], above[0][:, half:])
    if between is not None:
        near = after(near, between)
    far = [lax.ppermute(near[0], "block", up), lax.ppermute(near[1], "block", down)]
    return tuple(parts) + tuple(below) + tuple(above) + tuple(far)


def scale_kernel(gamma, chi, out):
    row = chi[pl.ds(pl.program_id(0), 1), :]
    out[0] = (gamma[0].astype(F32) * row).astype(BF16)


def ph_kernel(odd_ahead, n, index, scaled, *refs):
    pieces, (phi_out, slots_out) = refs[:n], refs[n : n + 2]
    left, right, phi, slots, left_sems, in_sems, out_sems = refs[n + 2 :]
    left_loads = point_loads([scaled], [left], left_sems)
    loads = right_loads(pieces, index[128], right, in_sems)
    low = low_lanes(32)
    stores = []
    for q in range(4):
        wait_all(left_loads[q] + loads[q])
        for half in range(2):
            columns = slice(half * 256, half * 256 + 256)
            part = jnp.dot(left[q], right[q, :, columns], preferred_element_type=F32)
            phi[q, :, columns] = part
            for r in range(RS):
                for m in range(2):
                    pair = part[r * 64 : r * 64 + 64, m * 128 : m * 128 + 128]
                    top, bottom = pair[:32], swap_lanes(pair[32:])
                    item = q * ITEMS + r * CB + half * 4 + m * 2
                    ahead, behind = (1, 0) if odd_ahead else (0, 1)
                    slots[index[item + ahead]] = jnp.where(low, top, bottom).astype(BF16)
                    slots[index[item + behind]] = jnp.where(low, bottom, top).astype(BF16)
        stores += start_all([pltpu.make_async_copy(phi.at[q], phi_out.at[q], out_sems.at[q])])
    stores += start_all([pltpu.make_async_copy(slots, slots_out, out_sems.at[4])])
    wait_all(stores)


def pp_kernel(n, index, first_in, second_in, chi, *refs):
    pieces, slots_out = refs[:n], refs[n]
    right, first, second, slots, lhs, in_sems, slot_sems = refs[n + 1 :]
    arrivals = start_all(
        [
            pltpu.make_async_copy(first_in, first, slot_sems.at[0]),
            pltpu.make_async_copy(second_in, second, slot_sems.at[1]),
        ]
    )
    loads = right_loads(pieces, index[128], right, in_sems)
    wait_all(arrivals)
    low = low_lanes(32)
    for p in range(4):
        row = chi[p : p + 1, :]
        for r in range(RS):
            for c in range(CB):
                slot = index[p * ITEMS + r * CB + c]
                a, b = first[slot].astype(F32), second[slot].astype(F32)
                scale = row[:, c * 128 : c * 128 + 128]
                straight = (jnp.where(low, a, b) * scale).astype(BF16)
                crossed = (swap_lanes(jnp.where(low, b, a)) * scale).astype(BF16)
                top = r * 64 + c % 2 * 32
                other = r * 64 + 32 - c % 2 * 32
                lhs[top : top + 32, c * 128 : c * 128 + 128] = straight
                lhs[other : other + 32, c * 128 : c * 128 + 128] = crossed
        wait_all(loads[p])
        for half in range(2):
            columns = slice(half * 512, half * 512 + 512)
            phi = jnp.dot(lhs[...], right[p, :, columns], preferred_element_type=F32).astype(BF16)
            for r in range(RS):
                for c in range(4):
                    slot = index[p * ITEMS + r * CB + half * 4 + c]
                    slots[slot] = phi[r * 64 : r * 64 + 64, c * 128 : c * 128 + 128]
    wait_all(start_all([pltpu.make_async_copy(slots, slots_out, slot_sems.at[2])]))


def base_kernel(gamma, first, second, out):
    low = low_lanes(256)
    for m in range(4):
        a = first[0, :, m * 128 : m * 128 + 128]
        b = second[0, :, m * 128 : m * 128 + 128]
        for c, phi in ((2 * m, jnp.where(low, a, b)), (2 * m + 1, swap_lanes(jnp.where(low, b, a)))):
            columns = slice(c * 128, c * 128 + 128)
            out[0, :, columns] = gamma[0, :, columns].astype(F32) + phi


def sum_kernel(index, base_in, came_in, out, base, came, total, in_sems, out_sems):
    arrival = start_all([pltpu.make_async_copy(came_in, came, out_sems.at[4])])
    loads = point_loads([base_in], [base], in_sems)
    wait_all(arrival)
    stores = []
    for q in range(4):
        wait_all(loads[q])
        for r in range(RS):
            for c in range(CB):
                rows, columns = slice(r * 64, r * 64 + 64), slice(c * 128, c * 128 + 128)
                back = came[index[q * ITEMS + r * CB + c]].astype(F32)
                total[q, rows, columns] = (base[q, rows, columns] + back).astype(BF16)
        stores += start_all([pltpu.make_async_copy(total.at[q], out.at[q], out_sems.at[q])])
    wait_all(stores)


def point_spec(rows, columns):
    return pl.BlockSpec((1, rows, columns), lambda q, *index: (q, 0, 0))


def whole_spec(shape):
    return pl.BlockSpec(shape, lambda q, *index: (0,) * len(shape))


def call(
    kernel, index, operands, in_specs, out_specs, out_shape, scratch, us, grant, free=(), **other
):
    return pl.pallas_call(
        kernel,
        grid_spec=pltpu.PrefetchScalarGridSpec(
            num_scalar_prefetch=len(index),
            grid=other.get("grid", (4,)),
            in_specs=in_specs,
            out_specs=out_specs,
            scratch_shapes=scratch,
        ),
        out_shape=out_shape,
        compiler_params=pltpu.CompilerParams(vmem_limit_bytes=grant * MIB),
        cost_estimate=pl.CostEstimate(
            flops=int(us * 1e9), bytes_accessed=int(us * 3e6), transcendentals=0
        ),
        input_output_aliases=other.get("aliases", {}),
    )(
        *index,
        *(
            x if k in free else pltpu.with_memory_space_constraint(x, pltpu.HBM)
            for k, x in enumerate(operands)
        ),
    )


def plan(relabel, points, boson_here, block_here):
    nboson = lax.axis_size("boson")
    item_total = points * ITEMS
    own_targets = lax.dynamic_slice(
        relabel, (boson_here * points, block_here * RS, 0), (points, RS, CB)
    ).reshape(item_total)
    shifts = (own_targets // points - boson_here) % nboson
    item_range = jnp.arange(item_total, dtype=jnp.int32)
    target = own_targets % points * ITEMS + item_range % ITEMS
    earlier = (shifts[None, :] == shifts[:, None]) & (item_range[None, :] < item_range[:, None])
    rank = jnp.sum(earlier.astype(jnp.int32), axis=1)
    send = (boson_here + shifts) % nboson * CAP + rank
    recv = (boson_here - shifts) % nboson * CAP + rank
    recv_at = jnp.sum(
        (target[None, :] == item_range[:, None]).astype(jnp.int32) * recv[None, :], axis=1
    )
    return send, recv_at


def exchange(slots):
    nboson = lax.axis_size("boson")
    tile = slots.shape[1:]
    return lax.all_to_all(
        slots.reshape((nboson, CAP) + tile), "boson", split_axis=0, concat_axis=0, tiled=True
    ).reshape(slots.shape)


HALF_TILES = (64 * CAP, 32, 128)
TILES = (64 * CAP, 64, 128)
ROWS = point_spec(256, 1024)
CHI = whole_spec((4, 1024))


def specs(pieces):
    return [point_spec(*x.shape[1:]) for x in pieces]


ANY = pl.BlockSpec(memory_space=pl.ANY)
DMA = pltpu.SemaphoreType.DMA


def vmem(x):
    return pltpu.VMEM(x.shape, x.dtype)


def cut(full, high_lanes, parts):
    def kernel(*refs):
        cut_kernel(high_lanes, *refs)

    shape = (4, 256, 512 // parts)
    scratch = [vmem(full)] + [pltpu.VMEM(shape, BF16)] * parts + [DMA((1, 4)), DMA((parts, 4))]
    outs = [jax.ShapeDtypeStruct(shape, BF16)] * parts
    return call(kernel, (), (full,), [ANY], [ANY] * parts, outs, scratch, 2, 6, grid=())


def scale_rows(gamma, chi):
    out = jax.ShapeDtypeStruct(gamma.shape, BF16)
    return call(scale_kernel, (), (gamma, chi), [ROWS, CHI], ROWS, out, [], 2, 6)


def hold(x, us):
    anywhere = pl.BlockSpec(memory_space=pl.ANY)
    out = pltpu.HBM(x.shape, x.dtype)
    return call(
        hold_kernel, (), (x,), [anywhere], anywhere, out, [], us, 1, grid=(1,), aliases={0: 0}
    )


def ph_half(odd_ahead, index, scaled, pieces, us):
    n = len(pieces)

    def kernel(*refs):
        ph_kernel(odd_ahead, n, *refs)

    phi = (4, 256, 512)
    scratch = [vmem(scaled), pltpu.VMEM((4, 1024, 512), BF16), pltpu.VMEM(phi, F32)]
    scratch += [pltpu.VMEM(HALF_TILES, BF16), DMA((1, 4)), DMA((n, 4)), DMA((5,))]
    outs = [pltpu.HBM(phi, F32), pltpu.HBM(HALF_TILES, BF16)]
    return call(
        kernel,
        (index,),
        (scaled,) + pieces,
        [ANY] * (n + 1),
        [ANY] * 2,
        outs,
        scratch,
        us,
        14,
        free=tuple(range(n + 1)) if n == 8 else (),
        grid=(),
    )


def pp_whole(index, came_1, came_2, chi, pieces):
    n = len(pieces)

    def kernel(*refs):
        pp_kernel(n, *refs)

    scratch = [pltpu.VMEM((4, 1024, 1024), BF16), vmem(came_1), vmem(came_2)]
    scratch += [pltpu.VMEM(TILES, BF16), pltpu.VMEM((256, 1024), BF16), DMA((n, 4)), DMA((3,))]
    return call(
        kernel,
        (index,),
        (came_1, came_2, chi) + pieces,
        [ANY, ANY, pl.BlockSpec(memory_space=pltpu.VMEM)] + [ANY] * n,
        ANY,
        pltpu.HBM(TILES, BF16),
        scratch,
        5,
        22,
        free=(1, n + 1, n + 2),
        grid=(),
    )


def base_sum(gamma, phi_1, phi_2):
    return call(
        base_kernel,
        (),
        (gamma, phi_1, phi_2),
        [ROWS] + [point_spec(256, 512)] * 2,
        ROWS,
        pltpu.HBM(gamma.shape, F32),
        [],
        4,
        10,
    )


def last_sum(index, base, back):
    out = pltpu.HBM(base.shape, BF16)
    scratch = [vmem(base), vmem(back), pltpu.VMEM(base.shape, BF16), DMA((1, 4)), DMA((5,))]
    return call(
        sum_kernel, (index,), (base, back), [ANY] * 2, ANY, out, scratch, 3, 14, free=(1,), grid=()
    )


def local(gamma_ph, full_ph, chi_ph, pp_vertex, chi_pp, relabel):
    block_here = lax.axis_index("block")
    send, recv_at = plan(relabel, gamma_ph.shape[0], lax.axis_index("boson"), block_here)
    here = jnp.full((8,), block_here, jnp.int32)
    send_index = jnp.concatenate([send, here])
    recv_index = jnp.concatenate([recv_at, here])

    full_ph, gamma_ph = after((full_ph, gamma_ph), (send_index, recv_index))
    scaled = scale_rows(gamma_ph, chi_ph)
    pieces_1 = gather_rows(cut(full_ph, False, 2))
    phi_1, outgoing_1 = ph_half(False, send_index, scaled, pieces_1, 4)
    pieces_2 = gather_rows(after(cut(full_ph, True, 1), pieces_1), between=outgoing_1)
    came_1 = exchange(outgoing_1)
    phi_2, outgoing_2 = ph_half(True, send_index, scaled, pieces_2, NEAR)
    pp_pieces = gather_rows((after(pp_vertex, pieces_2),), between=outgoing_2)
    came_2 = exchange(outgoing_2)
    pp_pieces = (pp_pieces[0],) + tuple(hold(x, FAR) for x in pp_pieces[1:3]) + pp_pieces[3:]
    leaving = pp_whole(recv_index, came_1, came_2, chi_pp, pp_pieces)
    base = base_sum(gamma_ph, phi_1, phi_2)
    return last_sum(send_index, base, exchange(leaving))


def solution(mesh):
    placed = (
        P("boson", "block", None),
        P("boson", "block", None),
        P("boson", None),
        P("boson", "block", None),
        P("boson", None),
        P(),
    )
    return jax.shard_map(
        local, mesh=mesh, in_specs=placed, out_specs=P("boson", "block", None), check_vma=False
    )
```

time: 256 us -> 255 us (level)
  waiting for transfers between devices: 153 us -> 157 us
  Pallas kernels: 39.5 us -> 36.2 us
    ppermute x3, waiting for transfers between devices: 0.04 us -> 24.5 us  [gather_rows(): above = [lax.ppermute(high, 'block', down)]]
    ppermute x3, waiting for transfers between devices: 30.4 us -> 14.3 us  [gather_rows(): below = [lax.ppermute(low, 'block', up)]]
    all_to_all x3, waiting for transfers between devices: 94.5 us -> 88.2 us  [exchange(): lax.all_to_all(slots.reshape((nboson, CAP) + tile), 'boson', split_axis=0...]
    pallas_call x9 -> x10, Pallas kernels: 39.5 us -> 36.2 us  [call(): pl.pallas_call(kernel, grid_spec=pltpu.PrefetchScalarGridSpec(num_scalar_...]
    ppermute x1, waiting for transfers between devices: 3.34 us -> 0.01 us  [gather_rows(): below.append(lax.ppermute(high, 'block', up))]
    ppermute x1, waiting for transfers between devices: 0.41 us -> 3.71 us  [gather_rows(): above.insert(0, lax.ppermute(low, 'block', down))]
  transfers between devices with their start and end apart: 17 -> 17, of which waited for: 11 -> 12; matrix products, arithmetic and copies ran while one was open for 3% -> 3% of each run, Pallas kernels for 9% -> 8%
where the time goes in v3:
time: 255 us; the launch traced here: 254 us
  waiting for transfers between devices  157 us (62%)
  starting transfers between devices  50.5 us (20%)
  Pallas kernels  36.2 us (14%)
  local copies, waits for them, and re-layouts  9.11 us (4%)
    all_to_all x3, waiting for transfers between devices, exchange(): lax.all_to_all(slots.reshape((nboson, CAP) + tile), 'boson', split_axis=0...  88.2 us
    pallas_call x10, Pallas kernels, call(): pl.pallas_call(kernel, grid_spec=pltpu.PrefetchScalarGridSpec(num_scalar_...  36.2 us
    all_to_all x3, starting transfers between devices, exchange(): lax.all_to_all(slots.reshape((nboson, CAP) + tile), 'boson', split_axis=0...  29.5 us
    ppermute x3, waiting for transfers between devices, gather_rows(): lax.ppermute(near[0], 'block', up)  26.5 us
    ppermute x3, waiting for transfers between devices, gather_rows(): above = [lax.ppermute(high, 'block', down)]  24.5 us
    ppermute x3, waiting for transfers between devices, gather_rows(): below = [lax.ppermute(low, 'block', up)]  14.3 us
    ppermute x3, starting transfers between devices, gather_rows(): lax.ppermute(near[1], 'block', down)  9.31 us
    ppermute x3, starting transfers between devices, gather_rows(): above = [lax.ppermute(high, 'block', down)]  7.63 us
  transfers between devices with their start and end apart: 17, of which 12 were waited for; matrix products, arithmetic and copies ran while one was open for 3% of the time, Pallas kernels for 8%

profile of v3, /device:TPU:2, one launch (start us, length us, event | category | flops | bytes accessed | tf_op | source)
XLA Modules:
  0.0 253.8 jit_solution(14068760903625673901)
XLA Ops:
  1.5 3.1 %shard_map.65 = (bf16[4,256,256]{2,1,0:T(8,128)(2,1)S(1)}, bf16[4,256,256]{2,1,0:T(8,128)(2,1)S(1)}) custom-call(bf16[4,256,1024]{2,1,0:T(8,128)(2,1)} %refs_0_.1), custom_call_target="tpu_custom_call" | custom-call | flops 2000000000 | bytes 6000000 | tf_op jit(solution)/shard_map/pallas_call | solution.py:223
  9.9 10.7 %collective-permute-done.refs_4_ = bf16[4,256,256]{2,1,0:T(8,128)(2,1)S(1)} collective-permute-done((bf16[4,256,256]{2,1,0:T(8,128)(2,1)S(1)}, bf16[4,256,256]{2,1,0:T(8,128)(2,1)S(1)}, u32[]{:S(2)}, u32[]{:S(2)}) %collective-permute-start) | collective-permute-done | bytes 524320 | tf_op jit(solution)/shard_map/ppermute | solution.py:104
  25.7 2.9 %shard_map.64.refs_1_ = bf16[4,256,1024]{2,1,0:T(8,128)(2,1)S(1)} custom-call(bf16[4,256,1024]{2,1,0:T(8,128)(2,1)} %gamma.1, f32[4,1024]{1,0:T(4,128)} %chi.1), custom_call_target="tpu_custom_call" | custom-call | flops 2000000000 | bytes 6000000 | tf_op jit(solution)/shard_map/pallas_call | solution.py:223
  28.6 3.7 %collective-permute-done.2.refs_6_ = bf16[4,256,256]{2,1,0:T(8,128)(2,1)S(1)} collective-permute-done((bf16[4,256,256]{2,1,0:T(8,128)(2,1)S(1)}, bf16[4,256,256]{2,1,0:T(8,128)(2,1)S(1)}, u32[]{:S(2)}, u32[]{:S(2)}) %collective-permute-start.2) | collective-permute-done | bytes 524320 | tf_op jit(solution)/shard_map/ppermute | solution.py:108
  32.3 9.7 %collective-permute-done.4.refs_8_ = bf16[4,256,256]{2,1,0:T(8,128)(2,1)S(1)} collective-permute-done((bf16[4,256,256]{2,1,0:T(8,128)(2,1)S(1)}, bf16[4,256,256]{2,1,0:T(8,128)(2,1)S(1)}, u32[]{:S(2)}, u32[]{:S(2)}) %collective-permute-start.4) | collective-permute-done | bytes 524320 | tf_op jit(solution)/shard_map/ppermute | solution.py:115
  42.1 3.0 %collective-permute-start.7 = (bf16[4,256,512]{2,1,0:T(8,128)(2,1)S(1)}, bf16[4,256,512]{2,1,0:T(8,128)(2,1)}, u32[]{:S(2)}, u32[]{:S(2)}) collective-permute-start(bf16[4,256,512]{2,1,0:T(8,128)(2,1)S(1)} %shard_map.67.refs_2_), channel_id=1, source_target_pairs={{0,3},{1,0},{2,1},{3,2},{4,7},{5,4},{6,5},{7,6},{8,11},{9,8},{10,9... | collective-permute-start | bytes 3145736 | tf_op jit(solution)/shard_map/ppermute | solution.py:105
  45.1 4.8 %shard_map.66 = (f32[4,256,512]{2,1,0:T(8,128)}, bf16[192,32,128]{2,1,0:T(8,128)(2,1)}) custom-call(s32[136]{0:T(256)S(1)} %concatenate.6.refs_0_.index, bf16[4,256,1024]{2,1,0:T(8,128)(2,1)S(1)} %shard_map.64.refs_1_, bf16[4,256,256]{2,1,0:T(8,128)(2,1)S(1)} %get-tuple-element.21.refs_2_, bf16[4,256,256]{2,1,0:T(8,128)(2,1)S(1)} %get-tuple-element.22.refs_3_, ...), custom_call_target="tpu_custom_call" | custom-call | flops 4000000000 | bytes 12000000 | tf_op jit(solution)/shard_map/pallas_call | solution.py:223
  50.0 12.0 %all-to-all-start = ((bf16[64,3,32,128]{3,2,1,0:T(8,128)(2,1)}), bf16[64,3,32,128]{3,2,1,0:T(8,128)(2,1)S(1)}, u32[]{:S(2)}, u32[]{:S(2)}) async-start(bf16[64,3,32,128]{3,2,1,0:T(8,128)(2,1)} %bitcast.10), calls=%async_computation | async-start | bytes 3145728 | tf_op jit(solution)/shard_map/all_to_all | solution.py:269
  62.0 4.5 %collective-permute-done.7.refs_4_ = bf16[4,256,512]{2,1,0:T(8,128)(2,1)} collective-permute-done((bf16[4,256,512]{2,1,0:T(8,128)(2,1)S(1)}, bf16[4,256,512]{2,1,0:T(8,128)(2,1)}, u32[]{:S(2)}, u32[]{:S(2)}) %collective-permute-start.7) | collective-permute-done | bytes 1048608 | tf_op jit(solution)/shard_map/ppermute | solution.py:105
  71.2 3.2 %collective-permute-start.9 = (bf16[4,128,512]{2,1,0:T(8,128)(2,1)S(1)}, bf16[4,128,512]{2,1,0:T(8,128)(2,1)S(1)}, u32[]{:S(2)}, u32[]{:S(2)}) collective-permute-start(bf16[4,128,512]{2,1,0:T(8,128)(2,1)S(1)} %slice.17), channel_id=1, source_target_pairs={{0,3},{1,0},{2,1},{3,2},{4,7},{5,4},{6,5},{7,6},{8,11},{9,8},{10,9... | collective-permute-start | bytes 1572872 | tf_op jit(solution)/shard_map/ppermute | solution.py:115
  74.4 9.4 %collective-permute-done.8.refs_5_ = bf16[4,128,512]{2,1,0:T(8,128)(2,1)S(1)} collective-permute-done((bf16[4,128,512]{2,1,0:T(8,128)(2,1)S(1)}, bf16[4,128,512]{2,1,0:T(8,128)(2,1)S(1)}, u32[]{:S(2)}, u32[]{:S(2)}) %collective-permute-start.8) | collective-permute-done | bytes 524320 | tf_op jit(solution)/shard_map/ppermute | solution.py:115
  83.9 3.0 %collective-permute-start.11 = (bf16[4,256,1024]{2,1,0:T(8,128)(2,1)}, bf16[4,256,1024]{2,1,0:T(8,128)(2,1)}, u32[]{:S(2)}, u32[]{:S(2)}) collective-permute-start(bf16[4,256,1024]{2,1,0:T(8,128)(2,1)} %refs_4_), channel_id=1, source_target_pairs={{0,3},{1,0},{2,1},{3,2},{4,7},{5,4},{6,5},{7,6},{8,11},{9,8},{10,9... | collective-permute-start | bytes 6291464 | tf_op jit(solution)/shard_map/ppermute | solution.py:105
  86.8 6.2 %shard_map.68 = (f32[4,256,512]{2,1,0:T(8,128)}, bf16[192,32,128]{2,1,0:T(8,128)(2,1)}) custom-call(s32[136]{0:T(256)S(1)} %concatenate.6.refs_0_.index, bf16[4,256,1024]{2,1,0:T(8,128)(2,1)} %copy-done.2, bf16[4,256,512]{2,1,0:T(8,128)(2,1)} %copy-done.1, bf16[4,256,512]{2,1,0:T(8,128)(2,1)} %collective-permute-done.6.refs_3_, ...), custom_call_target="tpu_custom_call" | custom-call | flops 20000000000 | bytes 60000000 | tf_op jit(solution)/shard_map/pallas_call | solution.py:223
  93.1 8.9 %all-to-all-done = bf16[64,3,32,128]{3,2,1,0:T(8,128)(2,1)S(1)} async-done(((bf16[64,3,32,128]{3,2,1,0:T(8,128)(2,1)}), bf16[64,3,32,128]{3,2,1,0:T(8,128)(2,1)S(1)}, u32[]{:S(2)}, u32[]{:S(2)}) %all-to-all-start) | async-done | bytes 1572896 | tf_op jit(solution)/shard_map/all_to_all | solution.py:269
  103.2 5.4 %all-to-all-start.1 = ((bf16[64,3,32,128]{3,2,1,0:T(8,128)(2,1)}), bf16[64,3,32,128]{3,2,1,0:T(8,128)(2,1)S(1)}, u32[]{:S(2)}, u32[]{:S(2)}) async-start(bf16[64,3,32,128]{3,2,1,0:T(8,128)(2,1)} %bitcast.11), calls=%async_computation.1 | async-start | bytes 3145728 | tf_op jit(solution)/shard_map/all_to_all | solution.py:269
  108.6 20.0 %collective-permute-done.11.x = bf16[4,256,1024]{2,1,0:T(8,128)(2,1)} collective-permute-done((bf16[4,256,1024]{2,1,0:T(8,128)(2,1)}, bf16[4,256,1024]{2,1,0:T(8,128)(2,1)}, u32[]{:S(2)}, u32[]{:S(2)}) %collective-permute-start.11) | collective-permute-done | bytes 2097184 | tf_op jit(solution)/shard_map/ppermute | solution.py:105
  134.3 3.2 %collective-permute-start.13 = (bf16[4,128,1024]{2,1,0:T(8,128)(2,1)}, bf16[4,128,1024]{2,1,0:T(8,128)(2,1)}, u32[]{:S(2)}, u32[]{:S(2)}) collective-permute-start(bf16[4,128,1024]{2,1,0:T(8,128)(2,1)} %slice.19), channel_id=1, source_target_pairs={{0,3},{1,0},{2,1},{3,2},{4,7},{5,4},{6,5},{7,6},{8,11},{9,8},{10,9... | collective-permute-start | bytes 3145736 | tf_op jit(solution)/shard_map/ppermute | solution.py:115
  137.5 11.1 %all-to-all-done.1 = bf16[64,3,32,128]{3,2,1,0:T(8,128)(2,1)S(1)} async-done(((bf16[64,3,32,128]{3,2,1,0:T(8,128)(2,1)}), bf16[64,3,32,128]{3,2,1,0:T(8,128)(2,1)S(1)}, u32[]{:S(2)}, u32[]{:S(2)}) %all-to-all-start.1) | async-done | bytes 1572896 | tf_op jit(solution)/shard_map/all_to_all | solution.py:269
  148.7 7.3 %collective-permute-done.12.refs_7_ = bf16[4,128,1024]{2,1,0:T(8,128)(2,1)S(1)} collective-permute-done((bf16[4,128,1024]{2,1,0:T(8,128)(2,1)}, bf16[4,128,1024]{2,1,0:T(8,128)(2,1)S(1)}, u32[]{:S(2)}, u32[]{:S(2)}) %collective-permute-start.12) | collective-permute-done | bytes 1048608 | tf_op jit(solution)/shard_map/ppermute | solution.py:115
  156.0 7.9 %shard_map.72 = bf16[192,64,128]{2,1,0:T(8,128)(2,1)} custom-call(s32[136]{0:T(256)S(1)} %concatenate.7.refs_0_, bf16[192,32,128]{2,1,0:T(8,128)(2,1)} %bitcast.9, bf16[192,32,128]{2,1,0:T(8,128)(2,1)S(1)} %bitcast.7, f32[4,1024]{1,0:T(4,128)} %refs_3_.1, bf16[4,256,1024]{2,1,0:T(8,128)(2,1)} %refs_4_, bf16[4,256,1024]{2,1,0:T(8,128)(2,1)} %shard_map.70.refs_5_, ...), custom_call_target="tpu_custom_call" | custom-call | flops 5000000000 | bytes 15000000 | tf_op jit(solution)/shard_map/pallas_call | solution.py:223
  163.9 12.0 %all-to-all-start.2 = ((bf16[64,3,64,128]{3,2,1,0:T(8,128)(2,1)}), bf16[64,3,64,128]{3,2,1,0:T(8,128)(2,1)S(1)}, u32[]{:S(2)}, u32[]{:S(2)}) async-start(bf16[64,3,64,128]{3,2,1,0:T(8,128)(2,1)} %bitcast.8), calls=%async_computation.2 | async-start | bytes 6291456 | tf_op jit(solution)/shard_map/all_to_all | solution.py:269
  176.0 5.6 %shard_map.69.base_in = f32[4,256,1024]{2,1,0:T(8,128)} custom-call(bf16[4,256,1024]{2,1,0:T(8,128)(2,1)} %gamma.1, f32[4,256,512]{2,1,0:T(8,128)} %get-tuple-element.23.first, f32[4,256,512]{2,1,0:T(8,128)} %get-tuple-element.28.second), custom_call_target="tpu_custom_call" | custom-call | flops 4000000000 | bytes 12000000 | tf_op jit(solution)/shard_map/pallas_call | solution.py:223
  181.5 68.1 %all-to-all-done.2 = bf16[64,3,64,128]{3,2,1,0:T(8,128)(2,1)S(1)} async-done(((bf16[64,3,64,128]{3,2,1,0:T(8,128)(2,1)}), bf16[64,3,64,128]{3,2,1,0:T(8,128)(2,1)S(1)}, u32[]{:S(2)}, u32[]{:S(2)}) %all-to-all-start.2) | async-done | bytes 3145760 | tf_op jit(solution)/shard_map/all_to_all | solution.py:269
  249.7 3.9 %shard_map.73 = bf16[4,256,1024]{2,1,0:T(8,128)(2,1)} custom-call(s32[136]{0:T(256)S(1)} %concatenate.6.refs_0_.index, f32[4,256,1024]{2,1,0:T(8,128)} %shard_map.69.base_in, bf16[192,64,128]{2,1,0:T(8,128)(2,1)S(1)} %bitcast.6), custom_call_target="tpu_custom_call" | custom-call | flops 3000000000 | bytes 9000000 | tf_op jit(solution)/shard_map/pallas_call | solution.py:223
  (45 shorter events, 23.5 us)
Async XLA Ops:
  0.0 0.9 copy-start
  4.6 16.1 %collective-permute-start = (bf16[4,256,256]{2,1,0:T(8,128)(2,1)S(1)}, bf16[4,256,256]{2,1,0:T(8,128)(2,1)S(1)}, u32[]{:S(2)}, u32[]{:S(2)}) collective-permute-start(bf16[4,256,256]{2,1,0:T(8,128)(2,1)S(1)} %get-tuple-element.21.refs_2_), channel_id=1, source_target_pairs={{0,1},{1,2},{2,3},{3,0},{4,5},{5,6},{6,7},{7,4},{8,9},{9,10},{10,1... | collective-permute-start | bytes 1572872 | tf_op jit(solution)/shard_map/ppermute | solution.py:104
  6.3 14.8 %collective-permute-start.3 = (bf16[4,256,256]{2,1,0:T(8,128)(2,1)S(1)}, bf16[4,256,256]{2,1,0:T(8,128)(2,1)S(1)}, u32[]{:S(2)}, u32[]{:S(2)}) collective-permute-start(bf16[4,256,256]{2,1,0:T(8,128)(2,1)S(1)} %get-tuple-element.22.refs_3_), channel_id=1, source_target_pairs={{0,3},{1,0},{2,1},{3,2},{4,7},{5,4},{6,5},{7,6},{8,11},{9,8},{10,9... | collective-permute-start | bytes 1572872 | tf_op jit(solution)/shard_map/ppermute | solution.py:105
  7.9 24.4 %collective-permute-start.2 = (bf16[4,256,256]{2,1,0:T(8,128)(2,1)S(1)}, bf16[4,256,256]{2,1,0:T(8,128)(2,1)S(1)}, u32[]{:S(2)}, u32[]{:S(2)}) collective-permute-start(bf16[4,256,256]{2,1,0:T(8,128)(2,1)S(1)} %get-tuple-element.21.refs_2_), channel_id=1, source_target_pairs={{0,3},{1,0},{2,1},{3,2},{4,7},{5,4},{6,5},{7,6},{8,11},{9,8},{10,9... | collective-permute-start | bytes 1572872 | tf_op jit(solution)/shard_map/ppermute | solution.py:108
  9.7 22.6 %collective-permute-start.1 = (bf16[4,256,256]{2,1,0:T(8,128)(2,1)S(1)}, bf16[4,256,256]{2,1,0:T(8,128)(2,1)S(1)}, u32[]{:S(2)}, u32[]{:S(2)}) collective-permute-start(bf16[4,256,256]{2,1,0:T(8,128)(2,1)S(1)} %get-tuple-element.22.refs_3_), channel_id=1, source_target_pairs={{0,1},{1,2},{2,3},{3,0},{4,5},{5,6},{6,7},{7,4},{8,9},{9,10},{10,1... | collective-permute-start | bytes 1572872 | tf_op jit(solution)/shard_map/ppermute | solution.py:107
  20.7 21.4 %collective-permute-start.4 = (bf16[4,256,256]{2,1,0:T(8,128)(2,1)S(1)}, bf16[4,256,256]{2,1,0:T(8,128)(2,1)S(1)}, u32[]{:S(2)}, u32[]{:S(2)}) collective-permute-start(bf16[4,256,256]{2,1,0:T(8,128)(2,1)S(1)} %collective-permute-done.refs_4_), channel_id=1, source_target_pairs={{0,1},{1,2},{2,3},{3,0},{4,5},{5,6},{6,7},{7,4},{8,9},{9,10},{10,1... | collective-permute-start | bytes 1572872 | tf_op jit(solution)/shard_map/ppermute | solution.py:115
  21.1 21.0 %collective-permute-start.5 = (bf16[4,256,256]{2,1,0:T(8,128)(2,1)S(1)}, bf16[4,256,256]{2,1,0:T(8,128)(2,1)S(1)}, u32[]{:S(2)}, u32[]{:S(2)}) collective-permute-start(bf16[4,256,256]{2,1,0:T(8,128)(2,1)S(1)} %collective-permute-done.3.refs_7_), channel_id=1, source_target_pairs={{0,3},{1,0},{2,1},{3,2},{4,7},{5,4},{6,5},{7,6},{8,11},{9,8},{10,9... | collective-permute-start | bytes 1572872 | tf_op jit(solution)/shard_map/ppermute | solution.py:115
  25.7 19.4 %copy-start.1 = (bf16[4,256,512]{2,1,0:T(8,128)(2,1)}, bf16[4,256,512]{2,1,0:T(8,128)(2,1)S(1)}, u32[]{:S(2)}) copy-start(bf16[4,256,512]{2,1,0:T(8,128)(2,1)S(1)} %shard_map.67.refs_2_) | copy-start | bytes 3145732
  28.6 21.3 %copy-start.2 = (bf16[4,256,1024]{2,1,0:T(8,128)(2,1)}, bf16[4,256,1024]{2,1,0:T(8,128)(2,1)S(1)}, u32[]{:S(2)}) copy-start(bf16[4,256,1024]{2,1,0:T(8,128)(2,1)S(1)} %shard_map.64.refs_1_) | copy-start | bytes 6291460
  42.1 24.4 %collective-permute-start.7 = (bf16[4,256,512]{2,1,0:T(8,128)(2,1)S(1)}, bf16[4,256,512]{2,1,0:T(8,128)(2,1)}, u32[]{:S(2)}, u32[]{:S(2)}) collective-permute-start(bf16[4,256,512]{2,1,0:T(8,128)(2,1)S(1)} %shard_map.67.refs_2_), channel_id=1, source_target_pairs={{0,3},{1,0},{2,1},{3,2},{4,7},{5,4},{6,5},{7,6},{8,11},{9,8},{10,9... | collective-permute-start | bytes 3145736 | tf_op jit(solution)/shard_map/ppermute | solution.py:105
  45.1 24.9 %collective-permute-start.6 = (bf16[4,256,512]{2,1,0:T(8,128)(2,1)S(1)}, bf16[4,256,512]{2,1,0:T(8,128)(2,1)}, u32[]{:S(2)}, u32[]{:S(2)}) collective-permute-start(bf16[4,256,512]{2,1,0:T(8,128)(2,1)S(1)} %shard_map.67.refs_2_), channel_id=1, source_target_pairs={{0,1},{1,2},{2,3},{3,0},{4,5},{5,6},{6,7},{7,4},{8,9},{9,10},{10,1... | collective-permute-start | bytes 3145736 | tf_op jit(solution)/shard_map/ppermute | solution.py:104
  50.0 52.1 %all-to-all-start = ((bf16[64,3,32,128]{3,2,1,0:T(8,128)(2,1)}), bf16[64,3,32,128]{3,2,1,0:T(8,128)(2,1)S(1)}, u32[]{:S(2)}, u32[]{:S(2)}) async-start(bf16[64,3,32,128]{3,2,1,0:T(8,128)(2,1)} %bitcast.10), calls=%async_computation | async-start | bytes 3145728 | tf_op jit(solution)/shard_map/all_to_all | solution.py:269
  71.1 12.7 %collective-permute-start.8 = (bf16[4,128,512]{2,1,0:T(8,128)(2,1)S(1)}, bf16[4,128,512]{2,1,0:T(8,128)(2,1)S(1)}, u32[]{:S(2)}, u32[]{:S(2)}) collective-permute-start(bf16[4,128,512]{2,1,0:T(8,128)(2,1)S(1)} %slice.16), channel_id=1, source_target_pairs={{0,1},{1,2},{2,3},{3,0},{4,5},{5,6},{6,7},{7,4},{8,9},{9,10},{10,1... | collective-permute-start | bytes 1572872 | tf_op jit(solution)/shard_map/ppermute | solution.py:115
  71.2 12.6 %collective-permute-start.9 = (bf16[4,128,512]{2,1,0:T(8,128)(2,1)S(1)}, bf16[4,128,512]{2,1,0:T(8,128)(2,1)S(1)}, u32[]{:S(2)}, u32[]{:S(2)}) collective-permute-start(bf16[4,128,512]{2,1,0:T(8,128)(2,1)S(1)} %slice.17), channel_id=1, source_target_pairs={{0,3},{1,0},{2,1},{3,2},{4,7},{5,4},{6,5},{7,6},{8,11},{9,8},{10,9... | collective-permute-start | bytes 1572872 | tf_op jit(solution)/shard_map/ppermute | solution.py:115
  83.9 3.0 %copy-start.4 = (bf16[4,128,512]{2,1,0:T(8,128)(2,1)}, bf16[4,128,512]{2,1,0:T(8,128)(2,1)S(1)}, u32[]{:S(2)}) copy-start(bf16[4,128,512]{2,1,0:T(8,128)(2,1)S(1)} %collective-permute-done.8.refs_5_) | copy-start | bytes 1572868
  83.9 3.0 %copy-start.5 = (bf16[4,128,512]{2,1,0:T(8,128)(2,1)}, bf16[4,128,512]{2,1,0:T(8,128)(2,1)S(1)}, u32[]{:S(2)}) copy-start(bf16[4,128,512]{2,1,0:T(8,128)(2,1)S(1)} %collective-permute-done.9.refs_6_) | copy-start | bytes 1572868
  83.9 44.7 %collective-permute-start.11 = (bf16[4,256,1024]{2,1,0:T(8,128)(2,1)}, bf16[4,256,1024]{2,1,0:T(8,128)(2,1)}, u32[]{:S(2)}, u32[]{:S(2)}) collective-permute-start(bf16[4,256,1024]{2,1,0:T(8,128)(2,1)} %refs_4_), channel_id=1, source_target_pairs={{0,3},{1,0},{2,1},{3,2},{4,7},{5,4},{6,5},{7,6},{8,11},{9,8},{10,9... | collective-permute-start | bytes 6291464 | tf_op jit(solution)/shard_map/ppermute | solution.py:105
  86.8 45.2 %collective-permute-start.10 = (bf16[4,256,1024]{2,1,0:T(8,128)(2,1)}, bf16[4,256,1024]{2,1,0:T(8,128)(2,1)}, u32[]{:S(2)}, u32[]{:S(2)}) collective-permute-start(bf16[4,256,1024]{2,1,0:T(8,128)(2,1)} %refs_4_), channel_id=1, source_target_pairs={{0,1},{1,2},{2,3},{3,0},{4,5},{5,6},{6,7},{7,4},{8,9},{9,10},{10,1... | collective-permute-start | bytes 6291464 | tf_op jit(solution)/shard_map/ppermute | solution.py:104
  102.0 1.2 copy-start.3
  103.2 45.5 %all-to-all-start.1 = ((bf16[64,3,32,128]{3,2,1,0:T(8,128)(2,1)}), bf16[64,3,32,128]{3,2,1,0:T(8,128)(2,1)S(1)}, u32[]{:S(2)}, u32[]{:S(2)}) async-start(bf16[64,3,32,128]{3,2,1,0:T(8,128)(2,1)} %bitcast.11), calls=%async_computation.1 | async-start | bytes 3145728 | tf_op jit(solution)/shard_map/all_to_all | solution.py:269
  134.3 21.7 %collective-permute-start.12 = (bf16[4,128,1024]{2,1,0:T(8,128)(2,1)}, bf16[4,128,1024]{2,1,0:T(8,128)(2,1)S(1)}, u32[]{:S(2)}, u32[]{:S(2)}) collective-permute-start(bf16[4,128,1024]{2,1,0:T(8,128)(2,1)} %slice.18), channel_id=1, source_target_pairs={{0,1},{1,2},{2,3},{3,0},{4,5},{5,6},{6,7},{7,4},{8,9},{9,10},{10,1... | collective-permute-start | bytes 3145736 | tf_op jit(solution)/shard_map/ppermute | solution.py:115
  134.3 21.7 %collective-permute-start.13 = (bf16[4,128,1024]{2,1,0:T(8,128)(2,1)}, bf16[4,128,1024]{2,1,0:T(8,128)(2,1)}, u32[]{:S(2)}, u32[]{:S(2)}) collective-permute-start(bf16[4,128,1024]{2,1,0:T(8,128)(2,1)} %slice.19), channel_id=1, source_target_pairs={{0,3},{1,0},{2,1},{3,2},{4,7},{5,4},{6,5},{7,6},{8,11},{9,8},{10,9... | collective-permute-start | bytes 3145736 | tf_op jit(solution)/shard_map/ppermute | solution.py:115
  163.9 85.7 %all-to-all-start.2 = ((bf16[64,3,64,128]{3,2,1,0:T(8,128)(2,1)}), bf16[64,3,64,128]{3,2,1,0:T(8,128)(2,1)S(1)}, u32[]{:S(2)}, u32[]{:S(2)}) async-start(bf16[64,3,64,128]{3,2,1,0:T(8,128)(2,1)} %bitcast.8), calls=%async_computation.2 | async-start | bytes 6291456 | tf_op jit(solution)/shard_map/all_to_all | solution.py:269

commit v4 on v3

--- a/solution.py
+++ b/solution.py
@@ -47,18 +47,14 @@
 
 
 def right_loads(pieces, block_here, right, sems):
-    split = len(pieces) == 8
-    width = pieces[0].shape[2]
-    if split:
-        where = [(step, 0, half * width) for step in (0, 3, 1, 2) for half in range(2)]
-    else:
-        where = [(0, 0, 0), (3, 0, 0), (1, 0, 0), (2, 0, 0), (2, 128, 0)]
+    where = [(step, offset) for step in STEPS for offset in (0, 128)]
+    where = [(s, o) for k, (s, o) in enumerate(where) if len(pieces) == 8 or o == 0 or k == 7]
     loads = []
     for q in range(4):
         copies = []
-        for k, (piece, (step, offset, column)) in enumerate(zip(pieces, where)):
+        for k, (piece, (step, offset)) in enumerate(zip(pieces, where)):
             start = pl.multiple_of(lax.rem(block_here + step, 4) * 256 + offset, 128)
-            to = right.at[q, pl.ds(start, piece.shape[1]), column : column + width]
+            to = right.at[q, pl.ds(start, piece.shape[1])]
             copies.append(pltpu.make_async_copy(piece.at[q], to, sems.at[k, q]))
         loads.append(start_all(copies))
     return loads
@@ -96,24 +92,50 @@
     return lax.optimization_barrier((value, others))[0]
 
 
-def gather_rows(parts, between=None):
+def gather_rows(low, high, between=None):
     n = lax.axis_size("block")
     up = [(i, (i + 1) % n) for i in range(n)]
     down = [(i, (i - 1) % n) for i in range(n)]
-    low, high = parts[0], parts[-1]
-    below = [lax.ppermute(low, "block", up)]
-    above = [lax.ppermute(high, "block", down)]
-    if len(parts) == 2:
-        below.append(lax.ppermute(high, "block", up))
-        above.insert(0, lax.ppermute(low, "block", down))
-        near = (below[0], above[1])
-    else:
-        half = low.shape[1] // 2
-        near = (below[0][:, :half], above[0][:, half:])
+    below_low = lax.ppermute(low, "block", up)
+    above_high = lax.ppermute(high, "block", down)
+    below_high = lax.ppermute(high, "block", up)
+    above_low = lax.ppermute(low, "block", down)
+    near = (below_low, above_high)
     if between is not None:
         near = after(near, between)
-    far = [lax.ppermute(near[0], "block", up), lax.ppermute(near[1], "block", down)]
-    return tuple(parts) + tuple(below) + tuple(above) + tuple(far)
+    far_low = lax.ppermute(near[0], "block", up)
+    far_high = lax.ppermute(near[1], "block", down)
+    return low, high, below_low, below_high, above_low, above_high, far_low, far_high
+
+
+def gather_whole(own, between):
+    n = lax.axis_size("block")
+    up = [(i, (i + 1) % n) for i in range(n)]
+    down = [(i, (i - 1) % n) for i in range(n)]
+    half = own.shape[1] // 2
+    below = lax.ppermute(own, "block", up)
+    above = lax.ppermute(own, "block", down)
+    near_low, near_high = after((below[:, :half], above[:, half:]), between)
+    return (
+        own,
+        below,
+        above,
+        lax.ppermute(near_low, "block", up),
+        lax.ppermute(near_high, "block", down),
+    )
+
+
+STEPS = (0, 3, 1, 2)
+
+
+def product(lhs, here, pieces, q, half):
+    total = None
+    for k, step in enumerate(STEPS):
+        start = pl.multiple_of(lax.rem(here + step, 4) * 256, 256)
+        block = pieces[2 * k + half][q]
+        term = jnp.dot(lhs[:, pl.ds(start, 256)], block, preferred_element_type=F32)
+        total = term if total is None else total + term
+    return total
 
 
 def scale_kernel(gamma, chi, out):
@@ -121,25 +143,31 @@
     out[0] = (gamma[0].astype(F32) * row).astype(BF16)
 
 
-def ph_kernel(odd_ahead, n, index, scaled, *refs):
-    pieces, (phi_out, slots_out) = refs[:n], refs[n : n + 2]
-    left, right, phi, slots, left_sems, in_sems, out_sems = refs[n + 2 :]
-    left_loads = point_loads([scaled], [left], left_sems)
-    loads = right_loads(pieces, index[128], right, in_sems)
+def ph_kernel(second, index, scaled, *refs):
+    n = 5 if second else 8
+    pieces, (phi_out, slots_out, phi, slots, out_sems) = refs[:n], refs[n : n + 5]
+    if second:
+        left, right, left_sems, in_sems = refs[n + 5 :]
+        left_loads = point_loads([scaled], [left], left_sems)
+        loads = right_loads(pieces, index[128], right, in_sems)
     low = low_lanes(32)
     stores = []
     for q in range(4):
-        wait_all(left_loads[q] + loads[q])
+        if second:
+            wait_all(left_loads[q] + loads[q])
         for half in range(2):
             columns = slice(half * 256, half * 256 + 256)
-            part = jnp.dot(left[q], right[q, :, columns], preferred_element_type=F32)
+            if second:
+                part = jnp.dot(left[q], right[q, :, columns], preferred_element_type=F32)
+            else:
+                part = product(scaled.at[q], index[128], pieces, q, half)
             phi[q, :, columns] = part
             for r in range(RS):
                 for m in range(2):
                     pair = part[r * 64 : r * 64 + 64, m * 128 : m * 128 + 128]
                     top, bottom = pair[:32], swap_lanes(pair[32:])
                     item = q * ITEMS + r * CB + half * 4 + m * 2
-                    ahead, behind = (1, 0) if odd_ahead else (0, 1)
+                    ahead, behind = (1, 0) if second else (0, 1)
                     slots[index[item + ahead]] = jnp.where(low, top, bottom).astype(BF16)
                     slots[index[item + behind]] = jnp.where(low, bottom, top).astype(BF16)
         stores += start_all([pltpu.make_async_copy(phi.at[q], phi_out.at[q], out_sems.at[q])])
@@ -147,15 +175,10 @@
     wait_all(stores)
 
 
-def pp_kernel(n, index, first_in, second_in, chi, *refs):
-    pieces, slots_out = refs[:n], refs[n]
-    right, first, second, slots, lhs, in_sems, slot_sems = refs[n + 1 :]
-    arrivals = start_all(
-        [
-            pltpu.make_async_copy(first_in, first, slot_sems.at[0]),
-            pltpu.make_async_copy(second_in, second, slot_sems.at[1]),
-        ]
-    )
+def pp_kernel(index, first_in, second, chi, *refs):
+    pieces, slots_out = refs[:8], refs[8]
+    right, first, slots, lhs, in_sems, slot_sems = refs[9:]
+    arrivals = start_all([pltpu.make_async_copy(first_in, first, slot_sems.at[0])])
     loads = right_loads(pieces, index[128], right, in_sems)
     wait_all(arrivals)
     low = low_lanes(32)
@@ -180,7 +203,7 @@
                 for c in range(4):
                     slot = index[p * ITEMS + r * CB + half * 4 + c]
                     slots[slot] = phi[r * 64 : r * 64 + 64, c * 128 : c * 128 + 128]
-    wait_all(start_all([pltpu.make_async_copy(slots, slots_out, slot_sems.at[2])]))
+    wait_all(start_all([pltpu.make_async_copy(slots, slots_out, slot_sems.at[1])]))
 
 
 def base_kernel(gamma, first, second, out):
@@ -193,10 +216,8 @@
             out[0, :, columns] = gamma[0, :, columns].astype(F32) + phi
 
 
-def sum_kernel(index, base_in, came_in, out, base, came, total, in_sems, out_sems):
-    arrival = start_all([pltpu.make_async_copy(came_in, came, out_sems.at[4])])
+def sum_kernel(index, base_in, came, out, base, total, in_sems, out_sems):
     loads = point_loads([base_in], [base], in_sems)
-    wait_all(arrival)
     stores = []
     for q in range(4):
         wait_all(loads[q])
@@ -282,6 +303,7 @@
 
 
 ANY = pl.BlockSpec(memory_space=pl.ANY)
+NEAR_BY = pl.BlockSpec(memory_space=pltpu.VMEM)
 DMA = pltpu.SemaphoreType.DMA
 
 
@@ -289,10 +311,11 @@
     return pltpu.VMEM(x.shape, x.dtype)
 
 
-def cut(full, high_lanes, parts):
+def cut(full, high_lanes):
     def kernel(*refs):
         cut_kernel(high_lanes, *refs)
 
+    parts = 1 if high_lanes else 2
     shape = (4, 256, 512 // parts)
     scratch = [vmem(full)] + [pltpu.VMEM(shape, BF16)] * parts + [DMA((1, 4)), DMA((parts, 4))]
     outs = [jax.ShapeDtypeStruct(shape, BF16)] * parts
@@ -312,50 +335,43 @@
     )
 
 
-def ph_half(odd_ahead, index, scaled, pieces, us):
-    n = len(pieces)
-
+def ph_half(second, index, scaled, pieces, us):
     def kernel(*refs):
-        ph_kernel(odd_ahead, n, *refs)
+        ph_kernel(second, *refs)
 
     phi = (4, 256, 512)
-    scratch = [vmem(scaled), pltpu.VMEM((4, 1024, 512), BF16), pltpu.VMEM(phi, F32)]
-    scratch += [pltpu.VMEM(HALF_TILES, BF16), DMA((1, 4)), DMA((n, 4)), DMA((5,))]
-    outs = [pltpu.HBM(phi, F32), pltpu.HBM(HALF_TILES, BF16)]
+    scratch = [pltpu.VMEM(phi, F32), pltpu.VMEM(HALF_TILES, BF16), DMA((5,))]
+    if second:
+        scratch += [vmem(scaled), pltpu.VMEM((4, 1024, 512), BF16), DMA((1, 4)), DMA((5, 4))]
     return call(
         kernel,
         (index,),
         (scaled,) + pieces,
-        [ANY] * (n + 1),
+        [ANY if second else NEAR_BY] * (len(pieces) + 1),
         [ANY] * 2,
-        outs,
+        [pltpu.HBM(phi, F32), pltpu.HBM(HALF_TILES, BF16)],
         scratch,
         us,
-        14,
-        free=tuple(range(n + 1)) if n == 8 else (),
+        14 if second else 8,
+        free=() if second else tuple(range(9)),
         grid=(),
     )
 
 
 def pp_whole(index, came_1, came_2, chi, pieces):
-    n = len(pieces)
-
-    def kernel(*refs):
-        pp_kernel(n, *refs)
-
-    scratch = [pltpu.VMEM((4, 1024, 1024), BF16), vmem(came_1), vmem(came_2)]
-    scratch += [pltpu.VMEM(TILES, BF16), pltpu.VMEM((256, 1024), BF16), DMA((n, 4)), DMA((3,))]
+    scratch = [pltpu.VMEM((4, 1024, 1024), BF16), vmem(came_1), pltpu.VMEM(TILES, BF16)]
+    scratch += [pltpu.VMEM((256, 1024), BF16), DMA((8, 4)), DMA((2,))]
     return call(
-        kernel,
+        pp_kernel,
         (index,),
         (came_1, came_2, chi) + pieces,
-        [ANY, ANY, pl.BlockSpec(memory_space=pltpu.VMEM)] + [ANY] * n,
+        [ANY, NEAR_BY, NEAR_BY] + [ANY] * 8,
         ANY,
         pltpu.HBM(TILES, BF16),
         scratch,
         5,
-        22,
-        free=(1, n + 1, n + 2),
+        20,
+        free=(1, 2, 9, 10),
         grid=(),
     )
 
@@ -376,9 +392,19 @@
 
 def last_sum(index, base, back):
     out = pltpu.HBM(base.shape, BF16)
-    scratch = [vmem(base), vmem(back), pltpu.VMEM(base.shape, BF16), DMA((1, 4)), DMA((5,))]
+    scratch = [vmem(base), pltpu.VMEM(base.shape, BF16), DMA((1, 4)), DMA((4,))]
     return call(
-        sum_kernel, (index,), (base, back), [ANY] * 2, ANY, out, scratch, 3, 14, free=(1,), grid=()
+        sum_kernel,
+        (index,),
+        (base, back),
+        [ANY, NEAR_BY],
+        ANY,
+        out,
+        scratch,
+        3,
+        10,
+        free=(1,),
+        grid=(),
     )
 
 
@@ -391,15 +417,18 @@
 
     full_ph, gamma_ph = after((full_ph, gamma_ph), (send_index, recv_index))
     scaled = scale_rows(gamma_ph, chi_ph)
-    pieces_1 = gather_rows(cut(full_ph, False, 2))
+    pp_halves = (pp_vertex[:, :128], pp_vertex[:, 128:])
+    pieces_1 = gather_rows(*cut(full_ph, False), between=pp_halves)
     phi_1, outgoing_1 = ph_half(False, send_index, scaled, pieces_1, 4)
-    pieces_2 = gather_rows(after(cut(full_ph, True, 1), pieces_1), between=outgoing_1)
+    pieces_2 = gather_whole(after(cut(full_ph, True)[0], pieces_1), outgoing_1)
     came_1 = exchange(outgoing_1)
     phi_2, outgoing_2 = ph_half(True, send_index, scaled, pieces_2, NEAR)
-    pp_pieces = gather_rows((after(pp_vertex, pieces_2),), between=outgoing_2)
+    pp_pieces = gather_rows(*after(pp_halves, pieces_2), between=outgoing_2)
     came_2 = exchange(outgoing_2)
-    pp_pieces = (pp_pieces[0],) + tuple(hold(x, FAR) for x in pp_pieces[1:3]) + pp_pieces[3:]
-    leaving = pp_whole(recv_index, came_1, came_2, chi_pp, pp_pieces)
+    held = tuple(hold(x, FAR) for x in pp_pieces[2:6])
+    leaving = pp_whole(
+        recv_index, came_1, came_2, chi_pp, pp_pieces[:2] + held + pp_pieces[6:]
+    )
     base = base_sum(gamma_ph, phi_1, phi_2)
     return last_sum(send_index, base, exchange(leaving))
 

time: 255 us -> 255 us (level)
  starting transfers between devices: 50.5 us -> 56.5 us
  waiting for transfers between devices: 157 us -> 154 us
    all_to_all x3, waiting for transfers between devices: 88.2 us -> 73.5 us  [exchange(): lax.all_to_all(slots.reshape((nboson, CAP) + tile), 'boson', split_axis=0...]
    ppermute x14 -> x16, waiting for transfers between devices: 69.1 us -> 80 us  [the longest x2 30.9 us: gather_rows(): below_low = lax.ppermute(low, 'block', up)]
    ppermute x14 -> x16, starting transfers between devices: 21.1 us -> 25.8 us  [the longest x2 6.13 us: gather_rows(): above_low = lax.ppermute(low, 'block', down)]
    unnamed x12 -> x22, local copies, waits for them, and re-layouts: 2.1 us -> 5.3 us
    slice x4 -> x3, local copies, waits for them, and re-layouts: 6.73 us -> 3.65 us  [the longest x2 2.16 us: gather_whole(): near_low, near_high = after((below[:, :half], above[:, half:]), between)]
    pallas_call x10 -> x12, Pallas kernels: 36.2 us -> 33.9 us  [call(): pl.pallas_call(kernel, grid_spec=pltpu.PrefetchScalarGridSpec(num_scalar_...]
  transfers between devices with their start and end apart: 17 -> 19, of which waited for: 12 -> 11; matrix products, arithmetic and copies ran while one was open for 3% -> 1% of each run, Pallas kernels for 8% -> 8%
where the time goes in v4:
time: 255 us; the launch traced here: 254 us
  waiting for transfers between devices  154 us (60%)
  starting transfers between devices  56.5 us (22%)
  Pallas kernels  33.9 us (13%)
  local copies, waits for them, and re-layouts  9.23 us (4%)
    all_to_all x3, waiting for transfers between devices, exchange(): lax.all_to_all(slots.reshape((nboson, CAP) + tile), 'boson', split_axis=0...  73.5 us
    pallas_call x12, Pallas kernels, call(): pl.pallas_call(kernel, grid_spec=pltpu.PrefetchScalarGridSpec(num_scalar_...  33.9 us
    ppermute x2, waiting for transfers between devices, gather_rows(): below_low = lax.ppermute(low, 'block', up)  30.9 us
    all_to_all x3, starting transfers between devices, exchange(): lax.all_to_all(slots.reshape((nboson, CAP) + tile), 'boson', split_axis=0...  30.7 us
    ppermute x2, waiting for transfers between devices, gather_rows(): far_low = lax.ppermute(near[0], 'block', up)  28.7 us
    ppermute x1, waiting for transfers between devices, gather_whole(): lax.ppermute(near_low, 'block', up)  9.89 us
    ppermute x1, waiting for transfers between devices, gather_whole(): below = lax.ppermute(own, 'block', up)  6.83 us
    ppermute x2, starting transfers between devices, gather_rows(): above_low = lax.ppermute(low, 'block', down)  6.13 us
  transfers between devices with their start and end apart: 19, of which 11 were waited for; matrix products, arithmetic and copies ran while one was open for 1% of the time, Pallas kernels for 8%

profile of v4, /device:TPU:2, one launch (start us, length us, event | category | flops | bytes accessed | tf_op | source)
XLA Modules:
  0.0 253.8 jit_solution(2177751491401833890)
XLA Ops:
  1.5 3.2 %shard_map.65 = (bf16[4,256,256]{2,1,0:T(8,128)(2,1)S(1)}, bf16[4,256,256]{2,1,0:T(8,128)(2,1)S(1)}) custom-call(bf16[4,256,1024]{2,1,0:T(8,128)(2,1)} %refs_0_.1), custom_call_target="tpu_custom_call" | custom-call | flops 2000000000 | bytes 6000000 | tf_op jit(solution)/shard_map/pallas_call | solution.py:244
  8.4 2.9 %collective-permute-start.2 = (bf16[4,256,256]{2,1,0:T(8,128)(2,1)S(1)}, bf16[4,256,256]{2,1,0:T(8,128)(2,1)S(1)}, u32[]{:S(2)}, u32[]{:S(2)}) collective-permute-start(bf16[4,256,256]{2,1,0:T(8,128)(2,1)S(1)} %get-tuple-element.24.refs_2_), channel_id=1, source_target_pairs={{0,3},{1,0},{2,1},{3,2},{4,7},{5,4},{6,5},{7,6},{8,11},{9,8},{10,9... | collective-permute-start | bytes 1572872 | tf_op jit(solution)/shard_map/ppermute | solution.py:102
  12.8 8.0 %collective-permute-done.refs_4_ = bf16[4,256,256]{2,1,0:T(8,128)(2,1)S(1)} collective-permute-done((bf16[4,256,256]{2,1,0:T(8,128)(2,1)S(1)}, bf16[4,256,256]{2,1,0:T(8,128)(2,1)S(1)}, u32[]{:S(2)}, u32[]{:S(2)}) %collective-permute-start) | collective-permute-done | bytes 524320 | tf_op jit(solution)/shard_map/ppermute | solution.py:99
  26.3 2.9 %shard_map.64.refs_1_ = bf16[4,256,1024]{2,1,0:T(8,128)(2,1)S(1)} custom-call(bf16[4,256,1024]{2,1,0:T(8,128)(2,1)} %gamma.1, f32[4,1024]{1,0:T(4,128)} %chi.2), custom_call_target="tpu_custom_call" | custom-call | flops 2000000000 | bytes 6000000 | tf_op jit(solution)/shard_map/pallas_call | solution.py:244
  29.2 2.9 %collective-permute-done.1.refs_5_ = bf16[4,256,256]{2,1,0:T(8,128)(2,1)S(1)} collective-permute-done((bf16[4,256,256]{2,1,0:T(8,128)(2,1)S(1)}, bf16[4,256,256]{2,1,0:T(8,128)(2,1)S(1)}, u32[]{:S(2)}, u32[]{:S(2)}) %collective-permute-start.1) | collective-permute-done | bytes 524320 | tf_op jit(solution)/shard_map/ppermute | solution.py:101
  32.5 9.7 %collective-permute-done.4.refs_8_ = bf16[4,256,256]{2,1,0:T(8,128)(2,1)S(1)} collective-permute-done((bf16[4,256,256]{2,1,0:T(8,128)(2,1)S(1)}, bf16[4,256,256]{2,1,0:T(8,128)(2,1)S(1)}, u32[]{:S(2)}, u32[]{:S(2)}) %collective-permute-start.4) | collective-permute-done | bytes 524320 | tf_op jit(solution)/shard_map/ppermute | solution.py:106
  45.5 3.3 %shard_map.66 = (f32[4,256,512]{2,1,0:T(8,128)}, bf16[192,32,128]{2,1,0:T(8,128)(2,1)}) custom-call(s32[136]{0:T(256)S(1)} %concatenate.6.refs_0_.index, bf16[4,256,1024]{2,1,0:T(8,128)(2,1)S(1)} %shard_map.64.refs_1_, bf16[4,256,256]{2,1,0:T(8,128)(2,1)S(1)} %get-tuple-element.24.refs_2_, bf16[4,256,256]{2,1,0:T(8,128)(2,1)S(1)} %get-tuple-element.25.refs_3_, ...), custom_call_target="tpu_custom_call" | custom-call | flops 4000000000 | bytes 12000000 | tf_op jit(solution)/shard_map/pallas_call | solution.py:244
  48.8 12.0 %all-to-all-start = ((bf16[64,3,32,128]{3,2,1,0:T(8,128)(2,1)}), bf16[64,3,32,128]{3,2,1,0:T(8,128)(2,1)S(1)}, u32[]{:S(2)}, u32[]{:S(2)}) async-start(bf16[64,3,32,128]{3,2,1,0:T(8,128)(2,1)} %bitcast.10), calls=%async_computation | async-start | bytes 3145728 | tf_op jit(solution)/shard_map/all_to_all | solution.py:290
  60.8 6.8 %collective-permute-done.6.refs_3_ = bf16[4,256,512]{2,1,0:T(8,128)(2,1)} collective-permute-done((bf16[4,256,512]{2,1,0:T(8,128)(2,1)S(1)}, bf16[4,256,512]{2,1,0:T(8,128)(2,1)}, u32[]{:S(2)}, u32[]{:S(2)}) %collective-permute-start.6) | collective-permute-done | bytes 1048608 | tf_op jit(solution)/shard_map/ppermute | solution.py:116
  69.9 3.2 %collective-permute-start.9 = (bf16[4,128,512]{2,1,0:T(8,128)(2,1)S(1)}, bf16[4,128,512]{2,1,0:T(8,128)(2,1)S(1)}, u32[]{:S(2)}, u32[]{:S(2)}) collective-permute-start(bf16[4,128,512]{2,1,0:T(8,128)(2,1)S(1)} %slice.17), channel_id=1, source_target_pairs={{0,3},{1,0},{2,1},{3,2},{4,7},{5,4},{6,5},{7,6},{8,11},{9,8},{10,9... | collective-permute-start | bytes 1572872 | tf_op jit(solution)/shard_map/ppermute | solution.py:124
  73.2 9.9 %collective-permute-done.8.refs_5_ = bf16[4,128,512]{2,1,0:T(8,128)(2,1)S(1)} collective-permute-done((bf16[4,128,512]{2,1,0:T(8,128)(2,1)S(1)}, bf16[4,128,512]{2,1,0:T(8,128)(2,1)S(1)}, u32[]{:S(2)}, u32[]{:S(2)}) %collective-permute-start.8) | collective-permute-done | bytes 524320 | tf_op jit(solution)/shard_map/ppermute | solution.py:123
  83.1 3.0 %collective-permute-start.13 = (bf16[4,128,1024]{2,1,0:T(8,128)(2,1)}, bf16[4,128,1024]{2,1,0:T(8,128)(2,1)}, u32[]{:S(2)}, u32[]{:S(2)}) collective-permute-start(bf16[4,128,1024]{2,1,0:T(8,128)(2,1)} %get-tuple-element.36.refs_1_), channel_id=1, source_target_pairs={{0,3},{1,0},{2,1},{3,2},{4,7},{5,4},{6,5},{7,6},{8,11},{9,8},{10,9... | collective-permute-start | bytes 3145736 | tf_op jit(solution)/shard_map/ppermute | solution.py:100
  86.0 3.3 %collective-permute-start.12 = (bf16[4,128,1024]{2,1,0:T(8,128)(2,1)}, bf16[4,128,1024]{2,1,0:T(8,128)(2,1)}, u32[]{:S(2)}, u32[]{:S(2)}) collective-permute-start(bf16[4,128,1024]{2,1,0:T(8,128)(2,1)} %get-tuple-element.35.refs_0_), channel_id=1, source_target_pairs={{0,3},{1,0},{2,1},{3,2},{4,7},{5,4},{6,5},{7,6},{8,11},{9,8},{10,9... | collective-permute-start | bytes 3145736 | tf_op jit(solution)/shard_map/ppermute | solution.py:102
  89.3 6.2 %shard_map.68 = (f32[4,256,512]{2,1,0:T(8,128)}, bf16[192,32,128]{2,1,0:T(8,128)(2,1)}) custom-call(s32[136]{0:T(256)S(1)} %concatenate.6.refs_0_.index, bf16[4,256,1024]{2,1,0:T(8,128)(2,1)} %copy-done.5, bf16[4,256,512]{2,1,0:T(8,128)(2,1)} %copy-done.1, bf16[4,256,512]{2,1,0:T(8,128)(2,1)} %collective-permute-done.6.refs_3_, ...), custom_call_target="tpu_custom_call" | custom-call | flops 20000000000 | bytes 60000000 | tf_op jit(solution)/shard_map/pallas_call | solution.py:244
  95.5 5.3 %all-to-all-done = bf16[64,3,32,128]{3,2,1,0:T(8,128)(2,1)S(1)} async-done(((bf16[64,3,32,128]{3,2,1,0:T(8,128)(2,1)}), bf16[64,3,32,128]{3,2,1,0:T(8,128)(2,1)S(1)}, u32[]{:S(2)}, u32[]{:S(2)}) %all-to-all-start) | async-done | bytes 1572896 | tf_op jit(solution)/shard_map/all_to_all | solution.py:290
  102.0 6.7 %all-to-all-start.1 = ((bf16[64,3,32,128]{3,2,1,0:T(8,128)(2,1)}), bf16[64,3,32,128]{3,2,1,0:T(8,128)(2,1)S(1)}, u32[]{:S(2)}, u32[]{:S(2)}) async-start(bf16[64,3,32,128]{3,2,1,0:T(8,128)(2,1)} %bitcast.11), calls=%async_computation.1 | async-start | bytes 3145728 | tf_op jit(solution)/shard_map/all_to_all | solution.py:290
  108.7 22.8 %collective-permute-done.10.x = bf16[4,128,1024]{2,1,0:T(8,128)(2,1)S(1)} collective-permute-done((bf16[4,128,1024]{2,1,0:T(8,128)(2,1)}, bf16[4,128,1024]{2,1,0:T(8,128)(2,1)S(1)}, u32[]{:S(2)}, u32[]{:S(2)}) %collective-permute-start.10) | collective-permute-done | bytes 1048608 | tf_op jit(solution)/shard_map/ppermute | solution.py:99
  132.6 3.2 %collective-permute-start.15 = (bf16[4,128,1024]{2,1,0:T(8,128)(2,1)}, bf16[4,128,1024]{2,1,0:T(8,128)(2,1)S(1)}, u32[]{:S(2)}, u32[]{:S(2)}) collective-permute-start(bf16[4,128,1024]{2,1,0:T(8,128)(2,1)} %collective-permute-done.13.x), channel_id=1, source_target_pairs={{0,3},{1,0},{2,1},{3,2},{4,7},{5,4},{6,5},{7,6},{8,11},{9,8},{10,9... | collective-permute-start | bytes 3145736 | tf_op jit(solution)/shard_map/ppermute | solution.py:107
  135.8 18.9 %collective-permute-done.14.refs_6_ = bf16[4,128,1024]{2,1,0:T(8,128)(2,1)S(1)} collective-permute-done((bf16[4,128,1024]{2,1,0:T(8,128)(2,1)}, bf16[4,128,1024]{2,1,0:T(8,128)(2,1)S(1)}, u32[]{:S(2)}, u32[]{:S(2)}) %collective-permute-start.14) | collective-permute-done | bytes 1048608 | tf_op jit(solution)/shard_map/ppermute | solution.py:106
  157.0 7.2 %shard_map.74 = bf16[192,64,128]{2,1,0:T(8,128)(2,1)} custom-call(s32[136]{0:T(256)S(1)} %concatenate.7.index, bf16[192,32,128]{2,1,0:T(8,128)(2,1)} %bitcast.9, bf16[192,32,128]{2,1,0:T(8,128)(2,1)S(1)} %bitcast.7, f32[4,1024]{1,0:T(4,128)S(1)} %copy-done.4, bf16[4,128,1024]{2,1,0:T(8,128)(2,1)} %get-tuple-element.35.refs_0_, ...), custom_call_target="tpu_custom_call" | custom-call | flops 5000000000 | bytes 15000000 | tf_op jit(solution)/shard_map/pallas_call | solution.py:244
  164.2 12.0 %all-to-all-start.2 = ((bf16[64,3,64,128]{3,2,1,0:T(8,128)(2,1)}), bf16[64,3,64,128]{3,2,1,0:T(8,128)(2,1)S(1)}, u32[]{:S(2)}, u32[]{:S(2)}) async-start(bf16[64,3,64,128]{3,2,1,0:T(8,128)(2,1)} %bitcast.8), calls=%async_computation.2 | async-start | bytes 6291456 | tf_op jit(solution)/shard_map/all_to_all | solution.py:290
  176.2 5.6 %shard_map.69.base_in = f32[4,256,1024]{2,1,0:T(8,128)} custom-call(bf16[4,256,1024]{2,1,0:T(8,128)(2,1)} %gamma.1, f32[4,256,512]{2,1,0:T(8,128)} %get-tuple-element.28.first, f32[4,256,512]{2,1,0:T(8,128)} %get-tuple-element.33.second), custom_call_target="tpu_custom_call" | custom-call | flops 4000000000 | bytes 12000000 | tf_op jit(solution)/shard_map/pallas_call | solution.py:244
  181.8 68.1 %all-to-all-done.2 = bf16[64,3,64,128]{3,2,1,0:T(8,128)(2,1)S(1)} async-done(((bf16[64,3,64,128]{3,2,1,0:T(8,128)(2,1)}), bf16[64,3,64,128]{3,2,1,0:T(8,128)(2,1)S(1)}, u32[]{:S(2)}, u32[]{:S(2)}) %all-to-all-start.2) | async-done | bytes 3145760 | tf_op jit(solution)/shard_map/all_to_all | solution.py:290
  250.0 3.7 %shard_map.75 = bf16[4,256,1024]{2,1,0:T(8,128)(2,1)} custom-call(s32[136]{0:T(256)S(1)} %concatenate.6.refs_0_.index, f32[4,256,1024]{2,1,0:T(8,128)} %shard_map.69.base_in, bf16[192,64,128]{2,1,0:T(8,128)(2,1)S(1)} %bitcast.6), custom_call_target="tpu_custom_call" | custom-call | flops 3000000000 | bytes 9000000 | tf_op jit(solution)/shard_map/pallas_call | solution.py:244
  (60 shorter events, 22.4 us)
Async XLA Ops:
  1.5 9.8 %copy-start.6 = (bf16[4,256,1024]{2,1,0:T(8,128)(2,1)S(1)}, bf16[4,256,1024]{2,1,0:T(8,128)(2,1)}, u32[]{:S(2)}) copy-start(bf16[4,256,1024]{2,1,0:T(8,128)(2,1)} %param.9) | copy-start | bytes 6291460
  4.8 16.1 %collective-permute-start = (bf16[4,256,256]{2,1,0:T(8,128)(2,1)S(1)}, bf16[4,256,256]{2,1,0:T(8,128)(2,1)S(1)}, u32[]{:S(2)}, u32[]{:S(2)}) collective-permute-start(bf16[4,256,256]{2,1,0:T(8,128)(2,1)S(1)} %get-tuple-element.24.refs_2_), channel_id=1, source_target_pairs={{0,1},{1,2},{2,3},{3,0},{4,5},{5,6},{6,7},{7,4},{8,9},{9,10},{10,1... | collective-permute-start | bytes 1572872 | tf_op jit(solution)/shard_map/ppermute | solution.py:99
  6.4 14.8 %collective-permute-start.3 = (bf16[4,256,256]{2,1,0:T(8,128)(2,1)S(1)}, bf16[4,256,256]{2,1,0:T(8,128)(2,1)S(1)}, u32[]{:S(2)}, u32[]{:S(2)}) collective-permute-start(bf16[4,256,256]{2,1,0:T(8,128)(2,1)S(1)} %get-tuple-element.25.refs_3_), channel_id=1, source_target_pairs={{0,3},{1,0},{2,1},{3,2},{4,7},{5,4},{6,5},{7,6},{8,11},{9,8},{10,9... | collective-permute-start | bytes 1572872 | tf_op jit(solution)/shard_map/ppermute | solution.py:100
  8.1 24.0 %collective-permute-start.1 = (bf16[4,256,256]{2,1,0:T(8,128)(2,1)S(1)}, bf16[4,256,256]{2,1,0:T(8,128)(2,1)S(1)}, u32[]{:S(2)}, u32[]{:S(2)}) collective-permute-start(bf16[4,256,256]{2,1,0:T(8,128)(2,1)S(1)} %get-tuple-element.25.refs_3_), channel_id=1, source_target_pairs={{0,1},{1,2},{2,3},{3,0},{4,5},{5,6},{6,7},{7,4},{8,9},{9,10},{10,1... | collective-permute-start | bytes 1572872 | tf_op jit(solution)/shard_map/ppermute | solution.py:101
  8.4 24.1 %collective-permute-start.2 = (bf16[4,256,256]{2,1,0:T(8,128)(2,1)S(1)}, bf16[4,256,256]{2,1,0:T(8,128)(2,1)S(1)}, u32[]{:S(2)}, u32[]{:S(2)}) collective-permute-start(bf16[4,256,256]{2,1,0:T(8,128)(2,1)S(1)} %get-tuple-element.24.refs_2_), channel_id=1, source_target_pairs={{0,3},{1,0},{2,1},{3,2},{4,7},{5,4},{6,5},{7,6},{8,11},{9,8},{10,9... | collective-permute-start | bytes 1572872 | tf_op jit(solution)/shard_map/ppermute | solution.py:102
  21.3 21.0 %collective-permute-start.4 = (bf16[4,256,256]{2,1,0:T(8,128)(2,1)S(1)}, bf16[4,256,256]{2,1,0:T(8,128)(2,1)S(1)}, u32[]{:S(2)}, u32[]{:S(2)}) collective-permute-start(bf16[4,256,256]{2,1,0:T(8,128)(2,1)S(1)} %collective-permute-done.refs_4_), channel_id=1, source_target_pairs={{0,1},{1,2},{2,3},{3,0},{4,5},{5,6},{6,7},{7,4},{8,9},{9,10},{10,1... | collective-permute-start | bytes 1572872 | tf_op jit(solution)/shard_map/ppermute | solution.py:106
  22.8 19.4 %collective-permute-start.5 = (bf16[4,256,256]{2,1,0:T(8,128)(2,1)S(1)}, bf16[4,256,256]{2,1,0:T(8,128)(2,1)S(1)}, u32[]{:S(2)}, u32[]{:S(2)}) collective-permute-start(bf16[4,256,256]{2,1,0:T(8,128)(2,1)S(1)} %collective-permute-done.3.refs_7_), channel_id=1, source_target_pairs={{0,3},{1,0},{2,1},{3,2},{4,7},{5,4},{6,5},{7,6},{8,11},{9,8},{10,9... | collective-permute-start | bytes 1572872 | tf_op jit(solution)/shard_map/ppermute | solution.py:107
  26.3 17.6 %copy-start.1 = (bf16[4,256,512]{2,1,0:T(8,128)(2,1)}, bf16[4,256,512]{2,1,0:T(8,128)(2,1)S(1)}, u32[]{:S(2)}) copy-start(bf16[4,256,512]{2,1,0:T(8,128)(2,1)S(1)} %shard_map.67.refs_2_) | copy-start | bytes 3145732
  29.2 19.6 %copy-start.5 = (bf16[4,256,1024]{2,1,0:T(8,128)(2,1)}, bf16[4,256,1024]{2,1,0:T(8,128)(2,1)S(1)}, u32[]{:S(2)}) copy-start(bf16[4,256,1024]{2,1,0:T(8,128)(2,1)S(1)} %shard_map.64.refs_1_) | copy-start | bytes 6291460
  42.3 25.4 %collective-permute-start.6 = (bf16[4,256,512]{2,1,0:T(8,128)(2,1)S(1)}, bf16[4,256,512]{2,1,0:T(8,128)(2,1)}, u32[]{:S(2)}, u32[]{:S(2)}) collective-permute-start(bf16[4,256,512]{2,1,0:T(8,128)(2,1)S(1)} %shard_map.67.refs_2_), channel_id=1, source_target_pairs={{0,1},{1,2},{2,3},{3,0},{4,5},{5,6},{6,7},{7,4},{8,9},{9,10},{10,1... | collective-permute-start | bytes 3145736 | tf_op jit(solution)/shard_map/ppermute | solution.py:116
  43.8 24.9 %collective-permute-start.7 = (bf16[4,256,512]{2,1,0:T(8,128)(2,1)S(1)}, bf16[4,256,512]{2,1,0:T(8,128)(2,1)}, u32[]{:S(2)}, u32[]{:S(2)}) collective-permute-start(bf16[4,256,512]{2,1,0:T(8,128)(2,1)S(1)} %shard_map.67.refs_2_), channel_id=1, source_target_pairs={{0,3},{1,0},{2,1},{3,2},{4,7},{5,4},{6,5},{7,6},{8,11},{9,8},{10,9... | collective-permute-start | bytes 3145736 | tf_op jit(solution)/shard_map/ppermute | solution.py:117
  48.8 52.1 %all-to-all-start = ((bf16[64,3,32,128]{3,2,1,0:T(8,128)(2,1)}), bf16[64,3,32,128]{3,2,1,0:T(8,128)(2,1)S(1)}, u32[]{:S(2)}, u32[]{:S(2)}) async-start(bf16[64,3,32,128]{3,2,1,0:T(8,128)(2,1)} %bitcast.10), calls=%async_computation | async-start | bytes 3145728 | tf_op jit(solution)/shard_map/all_to_all | solution.py:290
  69.8 13.2 %collective-permute-start.8 = (bf16[4,128,512]{2,1,0:T(8,128)(2,1)S(1)}, bf16[4,128,512]{2,1,0:T(8,128)(2,1)S(1)}, u32[]{:S(2)}, u32[]{:S(2)}) collective-permute-start(bf16[4,128,512]{2,1,0:T(8,128)(2,1)S(1)} %slice.16), channel_id=1, source_target_pairs={{0,1},{1,2},{2,3},{3,0},{4,5},{5,6},{6,7},{7,4},{8,9},{9,10},{10,1... | collective-permute-start | bytes 1572872 | tf_op jit(solution)/shard_map/ppermute | solution.py:123
  69.9 13.1 %collective-permute-start.9 = (bf16[4,128,512]{2,1,0:T(8,128)(2,1)S(1)}, bf16[4,128,512]{2,1,0:T(8,128)(2,1)S(1)}, u32[]{:S(2)}, u32[]{:S(2)}) collective-permute-start(bf16[4,128,512]{2,1,0:T(8,128)(2,1)S(1)} %slice.17), channel_id=1, source_target_pairs={{0,3},{1,0},{2,1},{3,2},{4,7},{5,4},{6,5},{7,6},{8,11},{9,8},{10,9... | collective-permute-start | bytes 1572872 | tf_op jit(solution)/shard_map/ppermute | solution.py:124
  83.0 6.2 %copy-start.9 = (bf16[4,128,512]{2,1,0:T(8,128)(2,1)}, bf16[4,128,512]{2,1,0:T(8,128)(2,1)S(1)}, u32[]{:S(2)}) copy-start(bf16[4,128,512]{2,1,0:T(8,128)(2,1)S(1)} %collective-permute-done.8.refs_5_) | copy-start | bytes 1572868
  83.1 6.2 %copy-start.10 = (bf16[4,128,512]{2,1,0:T(8,128)(2,1)}, bf16[4,128,512]{2,1,0:T(8,128)(2,1)S(1)}, u32[]{:S(2)}) copy-start(bf16[4,128,512]{2,1,0:T(8,128)(2,1)S(1)} %collective-permute-done.9.refs_6_) | copy-start | bytes 1572868
  83.1 49.5 %collective-permute-start.13 = (bf16[4,128,1024]{2,1,0:T(8,128)(2,1)}, bf16[4,128,1024]{2,1,0:T(8,128)(2,1)}, u32[]{:S(2)}, u32[]{:S(2)}) collective-permute-start(bf16[4,128,1024]{2,1,0:T(8,128)(2,1)} %get-tuple-element.36.refs_1_), channel_id=1, source_target_pairs={{0,3},{1,0},{2,1},{3,2},{4,7},{5,4},{6,5},{7,6},{8,11},{9,8},{10,9... | collective-permute-start | bytes 3145736 | tf_op jit(solution)/shard_map/ppermute | solution.py:100
  86.0 49.8 %collective-permute-start.11 = (bf16[4,128,1024]{2,1,0:T(8,128)(2,1)}, bf16[4,128,1024]{2,1,0:T(8,128)(2,1)}, u32[]{:S(2)}, u32[]{:S(2)}) collective-permute-start(bf16[4,128,1024]{2,1,0:T(8,128)(2,1)} %get-tuple-element.36.refs_1_), channel_id=1, source_target_pairs={{0,1},{1,2},{2,3},{3,0},{4,5},{5,6},{6,7},{7,4},{8,9},{9,10},{10,1... | collective-permute-start | bytes 3145736 | tf_op jit(solution)/shard_map/ppermute | solution.py:101
  86.0 45.6 %collective-permute-start.10 = (bf16[4,128,1024]{2,1,0:T(8,128)(2,1)}, bf16[4,128,1024]{2,1,0:T(8,128)(2,1)S(1)}, u32[]{:S(2)}, u32[]{:S(2)}) collective-permute-start(bf16[4,128,1024]{2,1,0:T(8,128)(2,1)} %get-tuple-element.35.refs_0_), channel_id=1, source_target_pairs={{0,1},{1,2},{2,3},{3,0},{4,5},{5,6},{6,7},{7,4},{8,9},{9,10},{10,1... | collective-permute-start | bytes 3145736 | tf_op jit(solution)/shard_map/ppermute | solution.py:99
  86.0 49.8 %collective-permute-start.12 = (bf16[4,128,1024]{2,1,0:T(8,128)(2,1)}, bf16[4,128,1024]{2,1,0:T(8,128)(2,1)}, u32[]{:S(2)}, u32[]{:S(2)}) collective-permute-start(bf16[4,128,1024]{2,1,0:T(8,128)(2,1)} %get-tuple-element.35.refs_0_), channel_id=1, source_target_pairs={{0,3},{1,0},{2,1},{3,2},{4,7},{5,4},{6,5},{7,6},{8,11},{9,8},{10,9... | collective-permute-start | bytes 3145736 | tf_op jit(solution)/shard_map/ppermute | solution.py:102
  102.0 53.7 %all-to-all-start.1 = ((bf16[64,3,32,128]{3,2,1,0:T(8,128)(2,1)}), bf16[64,3,32,128]{3,2,1,0:T(8,128)(2,1)S(1)}, u32[]{:S(2)}, u32[]{:S(2)}) async-start(bf16[64,3,32,128]{3,2,1,0:T(8,128)(2,1)} %bitcast.11), calls=%async_computation.1 | async-start | bytes 3145728 | tf_op jit(solution)/shard_map/all_to_all | solution.py:290
  132.6 22.2 %collective-permute-start.14 = (bf16[4,128,1024]{2,1,0:T(8,128)(2,1)}, bf16[4,128,1024]{2,1,0:T(8,128)(2,1)S(1)}, u32[]{:S(2)}, u32[]{:S(2)}) collective-permute-start(bf16[4,128,1024]{2,1,0:T(8,128)(2,1)} %copy-done.8), channel_id=1, source_target_pairs={{0,1},{1,2},{2,3},{3,0},{4,5},{5,6},{6,7},{7,4},{8,9},{9,10},{10,1... | collective-permute-start | bytes 3145736 | tf_op jit(solution)/shard_map/ppermute | solution.py:106
  132.6 22.2 %collective-permute-start.15 = (bf16[4,128,1024]{2,1,0:T(8,128)(2,1)}, bf16[4,128,1024]{2,1,0:T(8,128)(2,1)S(1)}, u32[]{:S(2)}, u32[]{:S(2)}) collective-permute-start(bf16[4,128,1024]{2,1,0:T(8,128)(2,1)} %collective-permute-done.13.x), channel_id=1, source_target_pairs={{0,3},{1,0},{2,1},{3,2},{4,7},{5,4},{6,5},{7,6},{8,11},{9,8},{10,9... | collective-permute-start | bytes 3145736 | tf_op jit(solution)/shard_map/ppermute | solution.py:107
  164.2 85.8 %all-to-all-start.2 = ((bf16[64,3,64,128]{3,2,1,0:T(8,128)(2,1)}), bf16[64,3,64,128]{3,2,1,0:T(8,128)(2,1)S(1)}, u32[]{:S(2)}, u32[]{:S(2)}) async-start(bf16[64,3,64,128]{3,2,1,0:T(8,128)(2,1)} %bitcast.8), calls=%async_computation.2 | async-start | bytes 6291456 | tf_op jit(solution)/shard_map/all_to_all | solution.py:290
  (6 other events, 6.3 us)

commit v5 on v4

--- a/solution.py
+++ b/solution.py
@@ -10,7 +10,7 @@
 CAP = 3
 ITEMS = RS * CB
 MIB = 1 << 20
-NEAR, FAR = 20, 8
+NEAR, LATE = 20, 20
 BF16 = jnp.bfloat16
 F32 = jnp.float32
 
@@ -47,17 +47,37 @@
 
 
 def right_loads(pieces, block_here, right, sems):
-    where = [(step, offset) for step in STEPS for offset in (0, 128)]
-    where = [(s, o) for k, (s, o) in enumerate(where) if len(pieces) == 8 or o == 0 or k == 7]
+    whole = len(pieces) == 5
+    where = [(step, 0, half * 256) for step in STEPS for half in range(2)]
+    if whole:
+        where = [(step, 0, 0) for step in STEPS] + [(STEPS[3], 128, 0)]
     loads = []
     for q in range(4):
         copies = []
-        for k, (piece, (step, offset)) in enumerate(zip(pieces, where)):
+        for k, (piece, (step, offset, column)) in enumerate(zip(pieces, where)):
+            rows, width = piece.shape[1:]
             start = pl.multiple_of(lax.rem(block_here + step, 4) * 256 + offset, 128)
-            to = right.at[q, pl.ds(start, piece.shape[1])]
+            to = right.at[q, pl.ds(start, rows), column : column + width]
             copies.append(pltpu.make_async_copy(piece.at[q], to, sems.at[k, q]))
         loads.append(start_all(copies))
     return loads
+
+
+def pack(second, index, q, half, part, slots):
+    low = low_lanes(32)
+    for r in range(RS):
+        for m in range(2):
+            pair = part[r * 64 : r * 64 + 64, m * 128 : m * 128 + 128]
+            top, bottom = pair[:32], swap_lanes(pair[32:])
+            item = q * ITEMS + r * CB + half * 4 + m * 2
+            ahead, behind = (1, 0) if second else (0, 1)
+            slots[index[item + ahead]] = jnp.where(low, top, bottom).astype(BF16)
+            slots[index[item + behind]] = jnp.where(low, bottom, top).astype(BF16)
+
+
+def tile_rows(r, c):
+    straight, crossed = r * 64 + c % 2 * 32, r * 64 + 32 - c % 2 * 32
+    return slice(straight, straight + 32), slice(crossed, crossed + 32)
 
 
 def cut_kernel(high_lanes, x, *refs):
@@ -84,10 +104,6 @@
     wait_all(stores)
 
 
-def hold_kernel(x, out):
-    pass
-
-
 def after(value, others):
     return lax.optimization_barrier((value, others))[0]
 
@@ -150,7 +166,6 @@
         left, right, left_sems, in_sems = refs[n + 5 :]
         left_loads = point_loads([scaled], [left], left_sems)
         loads = right_loads(pieces, index[128], right, in_sems)
-    low = low_lanes(32)
     stores = []
     for q in range(4):
         if second:
@@ -162,23 +177,22 @@
             else:
                 part = product(scaled.at[q], index[128], pieces, q, half)
             phi[q, :, columns] = part
-            for r in range(RS):
-                for m in range(2):
-                    pair = part[r * 64 : r * 64 + 64, m * 128 : m * 128 + 128]
-                    top, bottom = pair[:32], swap_lanes(pair[32:])
-                    item = q * ITEMS + r * CB + half * 4 + m * 2
-                    ahead, behind = (1, 0) if second else (0, 1)
-                    slots[index[item + ahead]] = jnp.where(low, top, bottom).astype(BF16)
-                    slots[index[item + behind]] = jnp.where(low, bottom, top).astype(BF16)
+            pack(second, index, q, half, part, slots)
         stores += start_all([pltpu.make_async_copy(phi.at[q], phi_out.at[q], out_sems.at[q])])
     stores += start_all([pltpu.make_async_copy(slots, slots_out, out_sems.at[4])])
     wait_all(stores)
 
 
-def pp_kernel(index, first_in, second, chi, *refs):
-    pieces, slots_out = refs[:8], refs[8]
-    right, first, slots, lhs, in_sems, slot_sems = refs[9:]
-    arrivals = start_all([pltpu.make_async_copy(first_in, first, slot_sems.at[0])])
+def pp_kernel(second, index, first_in, second_in, chi, *refs):
+    n = 5 if second else 8
+    pieces, slots_out = refs[:n], refs[n]
+    right, first, last, slots, lhs, in_sems, slot_sems = refs[n + 1 :]
+    arrivals = start_all(
+        [
+            pltpu.make_async_copy(first_in, first, slot_sems.at[0]),
+            pltpu.make_async_copy(second_in, last, slot_sems.at[1]),
+        ]
+    )
     loads = right_loads(pieces, index[128], right, in_sems)
     wait_all(arrivals)
     low = low_lanes(32)
@@ -187,45 +201,52 @@
         for r in range(RS):
             for c in range(CB):
                 slot = index[p * ITEMS + r * CB + c]
-                a, b = first[slot].astype(F32), second[slot].astype(F32)
-                scale = row[:, c * 128 : c * 128 + 128]
-                straight = (jnp.where(low, a, b) * scale).astype(BF16)
-                crossed = (swap_lanes(jnp.where(low, b, a)) * scale).astype(BF16)
-                top = r * 64 + c % 2 * 32
-                other = r * 64 + 32 - c % 2 * 32
-                lhs[top : top + 32, c * 128 : c * 128 + 128] = straight
-                lhs[other : other + 32, c * 128 : c * 128 + 128] = crossed
+                a, b = first[slot].astype(F32), last[slot].astype(F32)
+                columns = slice(c * 128, c * 128 + 128)
+                straight, crossed = tile_rows(r, c)
+                scale = row[:, columns]
+                lhs[straight, columns] = (jnp.where(low, a, b) * scale).astype(BF16)
+                lhs[crossed, columns] = (swap_lanes(jnp.where(low, b, a)) * scale).astype(BF16)
         wait_all(loads[p])
         for half in range(2):
-            columns = slice(half * 512, half * 512 + 512)
-            phi = jnp.dot(lhs[...], right[p, :, columns], preferred_element_type=F32).astype(BF16)
-            for r in range(RS):
-                for c in range(4):
-                    slot = index[p * ITEMS + r * CB + half * 4 + c]
-                    slots[slot] = phi[r * 64 : r * 64 + 64, c * 128 : c * 128 + 128]
-    wait_all(start_all([pltpu.make_async_copy(slots, slots_out, slot_sems.at[1])]))
-
-
-def base_kernel(gamma, first, second, out):
+            columns = slice(half * 256, half * 256 + 256)
+            part = jnp.dot(lhs[...], right[p, :, columns], preferred_element_type=F32)
+            pack(second, index, p, half, part, slots)
+    wait_all(start_all([pltpu.make_async_copy(slots, slots_out, slot_sems.at[2])]))
+
+
+def base_kernel(index, gamma, first, second, came, out):
+    q = pl.program_id(0)
     low = low_lanes(256)
     for m in range(4):
         a = first[0, :, m * 128 : m * 128 + 128]
         b = second[0, :, m * 128 : m * 128 + 128]
         for c, phi in ((2 * m, jnp.where(low, a, b)), (2 * m + 1, swap_lanes(jnp.where(low, b, a)))):
             columns = slice(c * 128, c * 128 + 128)
-            out[0, :, columns] = gamma[0, :, columns].astype(F32) + phi
+            base = gamma[0, :, columns].astype(F32) + phi
+            for r in range(RS):
+                back = came[index[q * ITEMS + r * CB + c]].astype(F32)
+                straight, crossed = tile_rows(r, c)
+                out[0, straight, columns] = base[straight] + jnp.where(low[:32], back, 0.0)
+                out[0, crossed, columns] = base[crossed] + swap_lanes(jnp.where(low[:32], 0.0, back))
 
 
 def sum_kernel(index, base_in, came, out, base, total, in_sems, out_sems):
     loads = point_loads([base_in], [base], in_sems)
+    low = low_lanes(32)
     stores = []
     for q in range(4):
         wait_all(loads[q])
         for r in range(RS):
             for c in range(CB):
-                rows, columns = slice(r * 64, r * 64 + 64), slice(c * 128, c * 128 + 128)
+                columns = slice(c * 128, c * 128 + 128)
+                straight, crossed = tile_rows(r, c)
                 back = came[index[q * ITEMS + r * CB + c]].astype(F32)
-                total[q, rows, columns] = (base[q, rows, columns] + back).astype(BF16)
+                for rows, term in (
+                    (straight, jnp.where(low, 0.0, back)),
+                    (crossed, swap_lanes(jnp.where(low, back, 0.0))),
+                ):
+                    total[q, rows, columns] = (base[q, rows, columns] + term).astype(BF16)
         stores += start_all([pltpu.make_async_copy(total.at[q], out.at[q], out_sems.at[q])])
     wait_all(stores)
 
@@ -255,7 +276,6 @@
         cost_estimate=pl.CostEstimate(
             flops=int(us * 1e9), bytes_accessed=int(us * 3e6), transcendentals=0
         ),
-        input_output_aliases=other.get("aliases", {}),
     )(
         *index,
         *(
@@ -293,7 +313,6 @@
 
 
 HALF_TILES = (64 * CAP, 32, 128)
-TILES = (64 * CAP, 64, 128)
 ROWS = point_spec(256, 1024)
 CHI = whole_spec((4, 1024))
 
@@ -311,28 +330,20 @@
     return pltpu.VMEM(x.shape, x.dtype)
 
 
-def cut(full, high_lanes):
+def cut(full, high_lanes, pinned=False):
     def kernel(*refs):
         cut_kernel(high_lanes, *refs)
 
     parts = 1 if high_lanes else 2
     shape = (4, 256, 512 // parts)
     scratch = [vmem(full)] + [pltpu.VMEM(shape, BF16)] * parts + [DMA((1, 4)), DMA((parts, 4))]
-    outs = [jax.ShapeDtypeStruct(shape, BF16)] * parts
+    outs = [pltpu.HBM(shape, BF16) if pinned else jax.ShapeDtypeStruct(shape, BF16)] * parts
     return call(kernel, (), (full,), [ANY], [ANY] * parts, outs, scratch, 2, 6, grid=())
 
 
 def scale_rows(gamma, chi):
     out = jax.ShapeDtypeStruct(gamma.shape, BF16)
     return call(scale_kernel, (), (gamma, chi), [ROWS, CHI], ROWS, out, [], 2, 6)
-
-
-def hold(x, us):
-    anywhere = pl.BlockSpec(memory_space=pl.ANY)
-    out = pltpu.HBM(x.shape, x.dtype)
-    return call(
-        hold_kernel, (), (x,), [anywhere], anywhere, out, [], us, 1, grid=(1,), aliases={0: 0}
-    )
 
 
 def ph_half(second, index, scaled, pieces, us):
@@ -358,35 +369,40 @@
     )
 
 
-def pp_whole(index, came_1, came_2, chi, pieces):
-    scratch = [pltpu.VMEM((4, 1024, 1024), BF16), vmem(came_1), pltpu.VMEM(TILES, BF16)]
-    scratch += [pltpu.VMEM((256, 1024), BF16), DMA((8, 4)), DMA((2,))]
+def pp_half(second, index, came_1, came_2, chi, pieces, us):
+    def kernel(*refs):
+        pp_kernel(second, *refs)
+
+    n = len(pieces)
+    scratch = [pltpu.VMEM((4, 1024, 512), BF16), vmem(came_1), vmem(came_2)]
+    scratch += [pltpu.VMEM(HALF_TILES, BF16), pltpu.VMEM((256, 1024), BF16), DMA((n, 4)), DMA((3,))]
     return call(
-        pp_kernel,
+        kernel,
         (index,),
         (came_1, came_2, chi) + pieces,
-        [ANY, NEAR_BY, NEAR_BY] + [ANY] * 8,
+        [ANY, ANY, NEAR_BY] + [ANY] * n,
         ANY,
-        pltpu.HBM(TILES, BF16),
+        pltpu.HBM(HALF_TILES, BF16),
         scratch,
-        5,
-        20,
-        free=(1, 2, 9, 10),
+        us,
+        16,
+        free=(2,) if second else (1, 2),
         grid=(),
     )
 
 
-def base_sum(gamma, phi_1, phi_2):
+def base_sum(index, gamma, phi_1, phi_2, back, us):
     return call(
         base_kernel,
-        (),
-        (gamma, phi_1, phi_2),
-        [ROWS] + [point_spec(256, 512)] * 2,
+        (index,),
+        (gamma, phi_1, phi_2, back),
+        [ROWS] + [point_spec(256, 512)] * 2 + [whole_spec(HALF_TILES)],
         ROWS,
         pltpu.HBM(gamma.shape, F32),
         [],
-        4,
-        10,
+        us,
+        16,
+        free=(3,),
     )
 
 
@@ -417,20 +433,20 @@
 
     full_ph, gamma_ph = after((full_ph, gamma_ph), (send_index, recv_index))
     scaled = scale_rows(gamma_ph, chi_ph)
-    pp_halves = (pp_vertex[:, :128], pp_vertex[:, 128:])
-    pieces_1 = gather_rows(*cut(full_ph, False), between=pp_halves)
+    pp_first, pp_second = cut(pp_vertex, False, True), cut(pp_vertex, True, True)[0]
+    pieces_1 = gather_rows(*cut(full_ph, False), between=(pp_first, pp_second))
     phi_1, outgoing_1 = ph_half(False, send_index, scaled, pieces_1, 4)
     pieces_2 = gather_whole(after(cut(full_ph, True)[0], pieces_1), outgoing_1)
     came_1 = exchange(outgoing_1)
     phi_2, outgoing_2 = ph_half(True, send_index, scaled, pieces_2, NEAR)
-    pp_pieces = gather_rows(*after(pp_halves, pieces_2), between=outgoing_2)
+    pieces_3 = gather_rows(*after(pp_first, pieces_2), between=outgoing_2)
     came_2 = exchange(outgoing_2)
-    held = tuple(hold(x, FAR) for x in pp_pieces[2:6])
-    leaving = pp_whole(
-        recv_index, came_1, came_2, chi_pp, pp_pieces[:2] + held + pp_pieces[6:]
-    )
-    base = base_sum(gamma_ph, phi_1, phi_2)
-    return last_sum(send_index, base, exchange(leaving))
+    leaving_1 = pp_half(False, recv_index, came_1, came_2, chi_pp, pieces_3, 5)
+    pieces_4 = gather_whole(after(pp_second, pieces_3), leaving_1)
+    back_1 = exchange(leaving_1)
+    leaving_2 = pp_half(True, recv_index, came_1, came_2, chi_pp, pieces_4, LATE)
+    base = base_sum(send_index, gamma_ph, phi_1, phi_2, back_1, 5)
+    return last_sum(send_index, base, exchange(leaving_2))
 
 
 def solution(mesh):

time: 255 us -> 256 us (level)
  waiting for transfers between devices: 154 us -> 132 us
  Pallas kernels: 33.9 us -> 45.3 us
  starting transfers between devices: 56.5 us -> 66.6 us
    all_to_all x3 -> x4, waiting for transfers between devices: 73.5 us -> 53.8 us  [exchange(): lax.all_to_all(slots.reshape((nboson, CAP) + tile), 'boson', split_axis=0...]
    ppermute x2, waiting for transfers between devices: 30.9 us -> 14.1 us  [gather_rows(): below_low = lax.ppermute(low, 'block', up)]
    pallas_call x12 -> x11, Pallas kernels: 33.9 us -> 45.3 us  [call(): pl.pallas_call(kernel, grid_spec=pltpu.PrefetchScalarGridSpec(num_scalar_...]
    ppermute x1 -> x2, waiting for transfers between devices: 9.89 us -> 20 us  [gather_whole(): lax.ppermute(near_low, 'block', up)]
    ppermute x2, waiting for transfers between devices: 28.7 us -> 20.2 us  [gather_rows(): far_low = lax.ppermute(near[0], 'block', up)]
    ppermute x2, waiting for transfers between devices: 2.91 us -> 10.7 us  [gather_rows(): below_high = lax.ppermute(high, 'block', up)]
    ppermute x1 -> x2, waiting for transfers between devices: 6.83 us -> 12.6 us  [gather_whole(): below = lax.ppermute(own, 'block', up)]
    ppermute x1 -> x2, starting transfers between devices: 1.66 us -> 4.66 us  [gather_whole(): above = lax.ppermute(own, 'block', down)]
  transfers between devices with their start and end apart: 19 -> 24, of which waited for: 11 -> 15; matrix products, arithmetic and copies ran while one was open for 1% -> 1% of each run, Pallas kernels for 8% -> 15%
where the time goes in v5:
time: 256 us; the launch traced here: 255 us
  waiting for transfers between devices  132 us (52%)
  starting transfers between devices  66.6 us (26%)
  Pallas kernels  45.3 us (18%)
  local copies, waits for them, and re-layouts  9.84 us (4%)
    all_to_all x4, waiting for transfers between devices, exchange(): lax.all_to_all(slots.reshape((nboson, CAP) + tile), 'boson', split_axis=0...  53.8 us
    pallas_call x11, Pallas kernels, call(): pl.pallas_call(kernel, grid_spec=pltpu.PrefetchScalarGridSpec(num_scalar_...  45.3 us
    all_to_all x4, starting transfers between devices, exchange(): lax.all_to_all(slots.reshape((nboson, CAP) + tile), 'boson', split_axis=0...  33.2 us
    ppermute x2, waiting for transfers between devices, gather_rows(): far_low = lax.ppermute(near[0], 'block', up)  20.2 us
    ppermute x2, waiting for transfers between devices, gather_whole(): lax.ppermute(near_low, 'block', up)  20 us
    ppermute x2, waiting for transfers between devices, gather_rows(): below_low = lax.ppermute(low, 'block', up)  14.1 us
    ppermute x2, waiting for transfers between devices, gather_whole(): below = lax.ppermute(own, 'block', up)  12.6 us
    ppermute x2, waiting for transfers between devices, gather_rows(): below_high = lax.ppermute(high, 'block', up)  10.7 us
  transfers between devices with their start and end apart: 24, of which 15 were waited for; matrix products, arithmetic and copies ran while one was open for 1% of the time, Pallas kernels for 15%

profile of v5, /device:TPU:2, one launch (start us, length us, event | category | flops | bytes accessed | tf_op | source)
XLA Modules:
  0.0 254.7 jit_solution(3857998330701904378)
XLA Ops:
  16.1 4.6 %collective-permute-done.refs_4_ = bf16[4,256,256]{2,1,0:T(8,128)(2,1)S(1)} collective-permute-done((bf16[4,256,256]{2,1,0:T(8,128)(2,1)S(1)}, bf16[4,256,256]{2,1,0:T(8,128)(2,1)S(1)}, u32[]{:S(2)}, u32[]{:S(2)}) %collective-permute-start) | collective-permute-done | bytes 524320 | tf_op jit(solution)/shard_map/ppermute | solution.py:115
  32.3 9.7 %collective-permute-done.4.refs_8_ = bf16[4,256,256]{2,1,0:T(8,128)(2,1)S(1)} collective-permute-done((bf16[4,256,256]{2,1,0:T(8,128)(2,1)S(1)}, bf16[4,256,256]{2,1,0:T(8,128)(2,1)S(1)}, u32[]{:S(2)}, u32[]{:S(2)}) %collective-permute-start.4) | collective-permute-done | bytes 524320 | tf_op jit(solution)/shard_map/ppermute | solution.py:122
  45.4 3.3 %shard_map.68 = (f32[4,256,512]{2,1,0:T(8,128)}, bf16[192,32,128]{2,1,0:T(8,128)(2,1)}) custom-call(s32[136]{0:T(256)S(1)} %concatenate.6.refs_0_.index, bf16[4,256,1024]{2,1,0:T(8,128)(2,1)S(1)} %shard_map.64.refs_1_, bf16[4,256,256]{2,1,0:T(8,128)(2,1)S(1)} %get-tuple-element.29.refs_2_, bf16[4,256,256]{2,1,0:T(8,128)(2,1)S(1)} %get-tuple-element.30.refs_3_, ...), custom_call_target="tpu_custom_call" | custom-call | flops 4000000000 | bytes 12000000 | tf_op jit(solution)/shard_map/pallas_call | solution.py:265
  48.6 12.0 %all-to-all-start = ((bf16[64,3,32,128]{3,2,1,0:T(8,128)(2,1)}), bf16[64,3,32,128]{3,2,1,0:T(8,128)(2,1)S(1)}, u32[]{:S(2)}, u32[]{:S(2)}) async-start(bf16[64,3,32,128]{3,2,1,0:T(8,128)(2,1)} %bitcast.15), calls=%async_computation | async-start | bytes 3145728 | tf_op jit(solution)/shard_map/all_to_all | solution.py:310
  60.7 6.8 %collective-permute-done.6.refs_3_ = bf16[4,256,512]{2,1,0:T(8,128)(2,1)} collective-permute-done((bf16[4,256,512]{2,1,0:T(8,128)(2,1)S(1)}, bf16[4,256,512]{2,1,0:T(8,128)(2,1)}, u32[]{:S(2)}, u32[]{:S(2)}) %collective-permute-start.6) | collective-permute-done | bytes 1048608 | tf_op jit(solution)/shard_map/ppermute | solution.py:132
  69.8 3.2 %collective-permute-start.9 = (bf16[4,128,512]{2,1,0:T(8,128)(2,1)S(1)}, bf16[4,128,512]{2,1,0:T(8,128)(2,1)S(1)}, u32[]{:S(2)}, u32[]{:S(2)}) collective-permute-start(bf16[4,128,512]{2,1,0:T(8,128)(2,1)S(1)} %slice.17), channel_id=1, source_target_pairs={{0,3},{1,0},{2,1},{3,2},{4,7},{5,4},{6,5},{7,6},{8,11},{9,8},{10,9... | collective-permute-start | bytes 1572872 | tf_op jit(solution)/shard_map/ppermute | solution.py:140
  73.0 9.9 %collective-permute-done.8.refs_5_ = bf16[4,128,512]{2,1,0:T(8,128)(2,1)S(1)} collective-permute-done((bf16[4,128,512]{2,1,0:T(8,128)(2,1)S(1)}, bf16[4,128,512]{2,1,0:T(8,128)(2,1)S(1)}, u32[]{:S(2)}, u32[]{:S(2)}) %collective-permute-start.8) | collective-permute-done | bytes 524320 | tf_op jit(solution)/shard_map/ppermute | solution.py:139
  84.5 6.2 %shard_map.70 = (f32[4,256,512]{2,1,0:T(8,128)}, bf16[192,32,128]{2,1,0:T(8,128)(2,1)}) custom-call(s32[136]{0:T(256)S(1)} %concatenate.6.refs_0_.index, bf16[4,256,1024]{2,1,0:T(8,128)(2,1)} %copy-done.4, bf16[4,256,512]{2,1,0:T(8,128)(2,1)} %copy-done.2, bf16[4,256,512]{2,1,0:T(8,128)(2,1)} %collective-permute-done.6.refs_3_, ...), custom_call_target="tpu_custom_call" | custom-call | flops 20000000000 | bytes 60000000 | tf_op jit(solution)/shard_map/pallas_call | solution.py:265
  90.8 9.9 %all-to-all-done = bf16[64,3,32,128]{3,2,1,0:T(8,128)(2,1)S(1)} async-done(((bf16[64,3,32,128]{3,2,1,0:T(8,128)(2,1)}), bf16[64,3,32,128]{3,2,1,0:T(8,128)(2,1)S(1)}, u32[]{:S(2)}, u32[]{:S(2)}) %all-to-all-start) | async-done | bytes 1572896 | tf_op jit(solution)/shard_map/all_to_all | solution.py:310
  101.9 5.4 %all-to-all-start.1 = ((bf16[64,3,32,128]{3,2,1,0:T(8,128)(2,1)}), bf16[64,3,32,128]{3,2,1,0:T(8,128)(2,1)S(1)}, u32[]{:S(2)}, u32[]{:S(2)}) async-start(bf16[64,3,32,128]{3,2,1,0:T(8,128)(2,1)} %bitcast.14), calls=%async_computation.1 | async-start | bytes 3145728 | tf_op jit(solution)/shard_map/all_to_all | solution.py:310
  110.7 3.2 %collective-permute-start.12 = (bf16[4,256,256]{2,1,0:T(8,128)(2,1)S(1)}, bf16[4,256,256]{2,1,0:T(8,128)(2,1)S(1)}, u32[]{:S(2)}, u32[]{:S(2)}) collective-permute-start(bf16[4,256,256]{2,1,0:T(8,128)(2,1)S(1)} %copy-done.7), channel_id=1, source_target_pairs={{0,3},{1,0},{2,1},{3,2},{4,7},{5,4},{6,5},{7,6},{8,11},{9,8},{10,9... | collective-permute-start | bytes 1572872 | tf_op jit(solution)/shard_map/ppermute | solution.py:118
  113.9 9.5 %collective-permute-done.10.refs_6_ = bf16[4,256,256]{2,1,0:T(8,128)(2,1)S(1)} collective-permute-done((bf16[4,256,256]{2,1,0:T(8,128)(2,1)S(1)}, bf16[4,256,256]{2,1,0:T(8,128)(2,1)S(1)}, u32[]{:S(2)}, u32[]{:S(2)}) %collective-permute-start.10) | collective-permute-done | bytes 524320 | tf_op jit(solution)/shard_map/ppermute | solution.py:115
  126.9 7.7 %collective-permute-done.11.refs_7_ = bf16[4,256,256]{2,1,0:T(8,128)(2,1)S(1)} collective-permute-done((bf16[4,256,256]{2,1,0:T(8,128)(2,1)}, bf16[4,256,256]{2,1,0:T(8,128)(2,1)S(1)}, u32[]{:S(2)}, u32[]{:S(2)}) %collective-permute-start.11) | collective-permute-done | bytes 524320 | tf_op jit(solution)/shard_map/ppermute | solution.py:117
  134.6 10.4 %collective-permute-done.14.refs_10_ = bf16[4,256,256]{2,1,0:T(8,128)(2,1)S(1)} collective-permute-done((bf16[4,256,256]{2,1,0:T(8,128)(2,1)S(1)}, bf16[4,256,256]{2,1,0:T(8,128)(2,1)S(1)}, u32[]{:S(2)}, u32[]{:S(2)}) %collective-permute-start.14) | collective-permute-done | bytes 524320 | tf_op jit(solution)/shard_map/ppermute | solution.py:122
  149.1 5.8 %shard_map.71 = bf16[192,32,128]{2,1,0:T(8,128)(2,1)} custom-call(s32[136]{0:T(256)S(1)} %concatenate.7.refs_0_, bf16[192,32,128]{2,1,0:T(8,128)(2,1)} %bitcast.12, bf16[192,32,128]{2,1,0:T(8,128)(2,1)S(1)} %bitcast.8, f32[4,1024]{1,0:T(4,128)S(1)} %copy-done.3, bf16[4,256,256]{2,1,0:T(8,128)(2,1)} %get-tuple-element.42.refs_4_, ...), custom_call_target="tpu_custom_call" | custom-call | flops 5000000000 | bytes 15000000 | tf_op jit(solution)/shard_map/pallas_call | solution.py:265
  154.9 10.3 %all-to-all-start.2 = ((bf16[64,3,32,128]{3,2,1,0:T(8,128)(2,1)}), bf16[64,3,32,128]{3,2,1,0:T(8,128)(2,1)S(1)}, u32[]{:S(2)}, u32[]{:S(2)}) async-start(bf16[64,3,32,128]{3,2,1,0:T(8,128)(2,1)} %bitcast.16), calls=%async_computation.2 | async-start | bytes 3145728 | tf_op jit(solution)/shard_map/all_to_all | solution.py:310
  165.2 5.8 %collective-permute-done.16.refs_5_ = bf16[4,256,512]{2,1,0:T(8,128)(2,1)S(1)} collective-permute-done((bf16[4,256,512]{2,1,0:T(8,128)(2,1)}, bf16[4,256,512]{2,1,0:T(8,128)(2,1)S(1)}, u32[]{:S(2)}, u32[]{:S(2)}) %collective-permute-start.16) | collective-permute-done | bytes 1048608 | tf_op jit(solution)/shard_map/ppermute | solution.py:132
  176.1 10.1 %collective-permute-done.18.refs_7_ = bf16[4,128,512]{2,1,0:T(8,128)(2,1)S(1)} collective-permute-done((bf16[4,128,512]{2,1,0:T(8,128)(2,1)S(1)}, bf16[4,128,512]{2,1,0:T(8,128)(2,1)S(1)}, u32[]{:S(2)}, u32[]{:S(2)}) %collective-permute-start.18) | collective-permute-done | bytes 524320 | tf_op jit(solution)/shard_map/ppermute | solution.py:139
  187.8 7.4 %shard_map.73 = bf16[192,32,128]{2,1,0:T(8,128)(2,1)} custom-call(s32[136]{0:T(256)S(1)} %concatenate.7.refs_0_, bf16[192,32,128]{2,1,0:T(8,128)(2,1)} %bitcast.13, bf16[192,32,128]{2,1,0:T(8,128)(2,1)} %bitcast.9, f32[4,1024]{1,0:T(4,128)S(1)} %copy-done.3, bf16[4,256,512]{2,1,0:T(8,128)(2,1)} %shard_map.67.refs_4_, bf16[4,256,512]{2,1,0:T(8,128)(2,1)} %copy-done.6, ...), custom_call_target="tpu_custom_call" | custom-call | flops 20000000000 | bytes 60000000 | tf_op jit(solution)/shard_map/pallas_call | solution.py:265
  195.2 10.0 %all-to-all-done.2 = bf16[64,3,32,128]{3,2,1,0:T(8,128)(2,1)S(1)} async-done(((bf16[64,3,32,128]{3,2,1,0:T(8,128)(2,1)}), bf16[64,3,32,128]{3,2,1,0:T(8,128)(2,1)S(1)}, u32[]{:S(2)}, u32[]{:S(2)}) %all-to-all-start.2) | async-done | bytes 1572896 | tf_op jit(solution)/shard_map/all_to_all | solution.py:310
  205.3 5.4 %all-to-all-start.3 = ((bf16[64,3,32,128]{3,2,1,0:T(8,128)(2,1)}), bf16[64,3,32,128]{3,2,1,0:T(8,128)(2,1)S(1)}, u32[]{:S(2)}, u32[]{:S(2)}) async-start(bf16[64,3,32,128]{3,2,1,0:T(8,128)(2,1)} %bitcast.17), calls=%async_computation.3 | async-start | bytes 3145728 | tf_op jit(solution)/shard_map/all_to_all | solution.py:310
  210.7 6.2 %shard_map.72.base_in = f32[4,256,1024]{2,1,0:T(8,128)} custom-call(s32[136]{0:T(256)S(1)} %concatenate.6.refs_0_.index, bf16[4,256,1024]{2,1,0:T(8,128)(2,1)} %gamma.1, f32[4,256,512]{2,1,0:T(8,128)} %get-tuple-element.35.first, f32[4,256,512]{2,1,0:T(8,128)} %get-tuple-element.40.second, bf16[192,32,128]{2,1,0:T(8,128)(2,1)S(1)} %bitcast.10), custom_call_target="tpu_custom_call" | custom-call | flops 5000000000 | bytes 15000000 | tf_op jit(solution)/shard_map/pallas_call | solution.py:265
  216.9 33.8 %all-to-all-done.3 = bf16[64,3,32,128]{3,2,1,0:T(8,128)(2,1)S(1)} async-done(((bf16[64,3,32,128]{3,2,1,0:T(8,128)(2,1)}), bf16[64,3,32,128]{3,2,1,0:T(8,128)(2,1)S(1)}, u32[]{:S(2)}, u32[]{:S(2)}) %all-to-all-start.3) | async-done | bytes 1572896 | tf_op jit(solution)/shard_map/all_to_all | solution.py:310
  250.7 3.7 %shard_map.74 = bf16[4,256,1024]{2,1,0:T(8,128)(2,1)} custom-call(s32[136]{0:T(256)S(1)} %concatenate.6.refs_0_.index, f32[4,256,1024]{2,1,0:T(8,128)} %shard_map.72.base_in, bf16[192,32,128]{2,1,0:T(8,128)(2,1)S(1)} %bitcast.11), custom_call_target="tpu_custom_call" | custom-call | flops 3000000000 | bytes 9000000 | tf_op jit(solution)/shard_map/pallas_call | solution.py:265
  (84 shorter events, 53.4 us)
Async XLA Ops:
  4.6 16.1 %collective-permute-start = (bf16[4,256,256]{2,1,0:T(8,128)(2,1)S(1)}, bf16[4,256,256]{2,1,0:T(8,128)(2,1)S(1)}, u32[]{:S(2)}, u32[]{:S(2)}) collective-permute-start(bf16[4,256,256]{2,1,0:T(8,128)(2,1)S(1)} %get-tuple-element.29.refs_2_), channel_id=1, source_target_pairs={{0,1},{1,2},{2,3},{3,0},{4,5},{5,6},{6,7},{7,4},{8,9},{9,10},{10,1... | collective-permute-start | bytes 1572872 | tf_op jit(solution)/shard_map/ppermute | solution.py:115
  6.3 14.8 %collective-permute-start.3 = (bf16[4,256,256]{2,1,0:T(8,128)(2,1)S(1)}, bf16[4,256,256]{2,1,0:T(8,128)(2,1)S(1)}, u32[]{:S(2)}, u32[]{:S(2)}) collective-permute-start(bf16[4,256,256]{2,1,0:T(8,128)(2,1)S(1)} %get-tuple-element.30.refs_3_), channel_id=1, source_target_pairs={{0,3},{1,0},{2,1},{3,2},{4,7},{5,4},{6,5},{7,6},{8,11},{9,8},{10,9... | collective-permute-start | bytes 1572872 | tf_op jit(solution)/shard_map/ppermute | solution.py:116
  7.9 24.0 %collective-permute-start.1 = (bf16[4,256,256]{2,1,0:T(8,128)(2,1)S(1)}, bf16[4,256,256]{2,1,0:T(8,128)(2,1)S(1)}, u32[]{:S(2)}, u32[]{:S(2)}) collective-permute-start(bf16[4,256,256]{2,1,0:T(8,128)(2,1)S(1)} %get-tuple-element.30.refs_3_), channel_id=1, source_target_pairs={{0,1},{1,2},{2,3},{3,0},{4,5},{5,6},{6,7},{7,4},{8,9},{9,10},{10,1... | collective-permute-start | bytes 1572872 | tf_op jit(solution)/shard_map/ppermute | solution.py:117
  8.3 24.1 %collective-permute-start.2 = (bf16[4,256,256]{2,1,0:T(8,128)(2,1)S(1)}, bf16[4,256,256]{2,1,0:T(8,128)(2,1)S(1)}, u32[]{:S(2)}, u32[]{:S(2)}) collective-permute-start(bf16[4,256,256]{2,1,0:T(8,128)(2,1)S(1)} %get-tuple-element.29.refs_2_), channel_id=1, source_target_pairs={{0,3},{1,0},{2,1},{3,2},{4,7},{5,4},{6,5},{7,6},{8,11},{9,8},{10,9... | collective-permute-start | bytes 1572872 | tf_op jit(solution)/shard_map/ppermute | solution.py:118
  21.1 21.0 %collective-permute-start.4 = (bf16[4,256,256]{2,1,0:T(8,128)(2,1)S(1)}, bf16[4,256,256]{2,1,0:T(8,128)(2,1)S(1)}, u32[]{:S(2)}, u32[]{:S(2)}) collective-permute-start(bf16[4,256,256]{2,1,0:T(8,128)(2,1)S(1)} %collective-permute-done.refs_4_), channel_id=1, source_target_pairs={{0,1},{1,2},{2,3},{3,0},{4,5},{5,6},{6,7},{7,4},{8,9},{9,10},{10,1... | collective-permute-start | bytes 1572872 | tf_op jit(solution)/shard_map/ppermute | solution.py:122
  22.7 19.4 %collective-permute-start.5 = (bf16[4,256,256]{2,1,0:T(8,128)(2,1)S(1)}, bf16[4,256,256]{2,1,0:T(8,128)(2,1)S(1)}, u32[]{:S(2)}, u32[]{:S(2)}) collective-permute-start(bf16[4,256,256]{2,1,0:T(8,128)(2,1)S(1)} %collective-permute-done.3.refs_7_), channel_id=1, source_target_pairs={{0,3},{1,0},{2,1},{3,2},{4,7},{5,4},{6,5},{7,6},{8,11},{9,8},{10,9... | collective-permute-start | bytes 1572872 | tf_op jit(solution)/shard_map/ppermute | solution.py:123
  42.1 25.4 %collective-permute-start.6 = (bf16[4,256,512]{2,1,0:T(8,128)(2,1)S(1)}, bf16[4,256,512]{2,1,0:T(8,128)(2,1)}, u32[]{:S(2)}, u32[]{:S(2)}) collective-permute-start(bf16[4,256,512]{2,1,0:T(8,128)(2,1)S(1)} %shard_map.69.refs_2_), channel_id=1, source_target_pairs={{0,1},{1,2},{2,3},{3,0},{4,5},{5,6},{6,7},{7,4},{8,9},{9,10},{10,1... | collective-permute-start | bytes 3145736 | tf_op jit(solution)/shard_map/ppermute | solution.py:132
  43.7 24.9 %collective-permute-start.7 = (bf16[4,256,512]{2,1,0:T(8,128)(2,1)S(1)}, bf16[4,256,512]{2,1,0:T(8,128)(2,1)}, u32[]{:S(2)}, u32[]{:S(2)}) collective-permute-start(bf16[4,256,512]{2,1,0:T(8,128)(2,1)S(1)} %shard_map.69.refs_2_), channel_id=1, source_target_pairs={{0,3},{1,0},{2,1},{3,2},{4,7},{5,4},{6,5},{7,6},{8,11},{9,8},{10,9... | collective-permute-start | bytes 3145736 | tf_op jit(solution)/shard_map/ppermute | solution.py:133
  48.6 52.1 %all-to-all-start = ((bf16[64,3,32,128]{3,2,1,0:T(8,128)(2,1)}), bf16[64,3,32,128]{3,2,1,0:T(8,128)(2,1)S(1)}, u32[]{:S(2)}, u32[]{:S(2)}) async-start(bf16[64,3,32,128]{3,2,1,0:T(8,128)(2,1)} %bitcast.15), calls=%async_computation | async-start | bytes 3145728 | tf_op jit(solution)/shard_map/all_to_all | solution.py:310
  69.7 13.2 %collective-permute-start.8 = (bf16[4,128,512]{2,1,0:T(8,128)(2,1)S(1)}, bf16[4,128,512]{2,1,0:T(8,128)(2,1)S(1)}, u32[]{:S(2)}, u32[]{:S(2)}) collective-permute-start(bf16[4,128,512]{2,1,0:T(8,128)(2,1)S(1)} %slice.16), channel_id=1, source_target_pairs={{0,1},{1,2},{2,3},{3,0},{4,5},{5,6},{6,7},{7,4},{8,9},{9,10},{10,1... | collective-permute-start | bytes 1572872 | tf_op jit(solution)/shard_map/ppermute | solution.py:139
  69.8 13.1 %collective-permute-start.9 = (bf16[4,128,512]{2,1,0:T(8,128)(2,1)S(1)}, bf16[4,128,512]{2,1,0:T(8,128)(2,1)S(1)}, u32[]{:S(2)}, u32[]{:S(2)}) collective-permute-start(bf16[4,128,512]{2,1,0:T(8,128)(2,1)S(1)} %slice.17), channel_id=1, source_target_pairs={{0,3},{1,0},{2,1},{3,2},{4,7},{5,4},{6,5},{7,6},{8,11},{9,8},{10,9... | collective-permute-start | bytes 1572872 | tf_op jit(solution)/shard_map/ppermute | solution.py:140
  101.9 47.2 %all-to-all-start.1 = ((bf16[64,3,32,128]{3,2,1,0:T(8,128)(2,1)}), bf16[64,3,32,128]{3,2,1,0:T(8,128)(2,1)S(1)}, u32[]{:S(2)}, u32[]{:S(2)}) async-start(bf16[64,3,32,128]{3,2,1,0:T(8,128)(2,1)} %bitcast.14), calls=%async_computation.1 | async-start | bytes 3145728 | tf_op jit(solution)/shard_map/all_to_all | solution.py:310
  107.3 16.1 %collective-permute-start.10 = (bf16[4,256,256]{2,1,0:T(8,128)(2,1)S(1)}, bf16[4,256,256]{2,1,0:T(8,128)(2,1)S(1)}, u32[]{:S(2)}, u32[]{:S(2)}) collective-permute-start(bf16[4,256,256]{2,1,0:T(8,128)(2,1)S(1)} %copy-done.7), channel_id=1, source_target_pairs={{0,1},{1,2},{2,3},{3,0},{4,5},{5,6},{6,7},{7,4},{8,9},{9,10},{10,1... | collective-permute-start | bytes 1572872 | tf_op jit(solution)/shard_map/ppermute | solution.py:115
  107.8 15.6 %collective-permute-start.13 = (bf16[4,256,256]{2,1,0:T(8,128)(2,1)}, bf16[4,256,256]{2,1,0:T(8,128)(2,1)S(1)}, u32[]{:S(2)}, u32[]{:S(2)}) collective-permute-start(bf16[4,256,256]{2,1,0:T(8,128)(2,1)} %get-tuple-element.43.refs_5_), channel_id=1, source_target_pairs={{0,3},{1,0},{2,1},{3,2},{4,7},{5,4},{6,5},{7,6},{8,11},{9,8},{10,9... | collective-permute-start | bytes 1572872 | tf_op jit(solution)/shard_map/ppermute | solution.py:116
  110.7 24.0 %collective-permute-start.11 = (bf16[4,256,256]{2,1,0:T(8,128)(2,1)}, bf16[4,256,256]{2,1,0:T(8,128)(2,1)S(1)}, u32[]{:S(2)}, u32[]{:S(2)}) collective-permute-start(bf16[4,256,256]{2,1,0:T(8,128)(2,1)} %get-tuple-element.43.refs_5_), channel_id=1, source_target_pairs={{0,1},{1,2},{2,3},{3,0},{4,5},{5,6},{6,7},{7,4},{8,9},{9,10},{10,1... | collective-permute-start | bytes 1572872 | tf_op jit(solution)/shard_map/ppermute | solution.py:117
  110.7 24.0 %collective-permute-start.12 = (bf16[4,256,256]{2,1,0:T(8,128)(2,1)S(1)}, bf16[4,256,256]{2,1,0:T(8,128)(2,1)S(1)}, u32[]{:S(2)}, u32[]{:S(2)}) collective-permute-start(bf16[4,256,256]{2,1,0:T(8,128)(2,1)S(1)} %copy-done.7), channel_id=1, source_target_pairs={{0,3},{1,0},{2,1},{3,2},{4,7},{5,4},{6,5},{7,6},{8,11},{9,8},{10,9... | collective-permute-start | bytes 1572872 | tf_op jit(solution)/shard_map/ppermute | solution.py:118
  123.4 21.7 %collective-permute-start.14 = (bf16[4,256,256]{2,1,0:T(8,128)(2,1)S(1)}, bf16[4,256,256]{2,1,0:T(8,128)(2,1)S(1)}, u32[]{:S(2)}, u32[]{:S(2)}) collective-permute-start(bf16[4,256,256]{2,1,0:T(8,128)(2,1)S(1)} %collective-permute-done.10.refs_6_), channel_id=1, source_target_pairs={{0,1},{1,2},{2,3},{3,0},{4,5},{5,6},{6,7},{7,4},{8,9},{9,10},{10,1... | collective-permute-start | bytes 1572872 | tf_op jit(solution)/shard_map/ppermute | solution.py:122
  124.1 21.0 %collective-permute-start.15 = (bf16[4,256,256]{2,1,0:T(8,128)(2,1)S(1)}, bf16[4,256,256]{2,1,0:T(8,128)(2,1)S(1)}, u32[]{:S(2)}, u32[]{:S(2)}) collective-permute-start(bf16[4,256,256]{2,1,0:T(8,128)(2,1)S(1)} %collective-permute-done.13.refs_9_), channel_id=1, source_target_pairs={{0,3},{1,0},{2,1},{3,2},{4,7},{5,4},{6,5},{7,6},{8,11},{9,8},{10,9... | collective-permute-start | bytes 1572872 | tf_op jit(solution)/shard_map/ppermute | solution.py:123
  145.1 25.9 %collective-permute-start.16 = (bf16[4,256,512]{2,1,0:T(8,128)(2,1)}, bf16[4,256,512]{2,1,0:T(8,128)(2,1)S(1)}, u32[]{:S(2)}, u32[]{:S(2)}) collective-permute-start(bf16[4,256,512]{2,1,0:T(8,128)(2,1)} %shard_map.67.refs_4_), channel_id=1, source_target_pairs={{0,1},{1,2},{2,3},{3,0},{4,5},{5,6},{6,7},{7,4},{8,9},{9,10},{10,1... | collective-permute-start | bytes 3145736 | tf_op jit(solution)/shard_map/ppermute | solution.py:132
  146.1 25.0 %collective-permute-start.17 = (bf16[4,256,512]{2,1,0:T(8,128)(2,1)}, bf16[4,256,512]{2,1,0:T(8,128)(2,1)}, u32[]{:S(2)}, u32[]{:S(2)}) collective-permute-start(bf16[4,256,512]{2,1,0:T(8,128)(2,1)} %shard_map.67.refs_4_), channel_id=1, source_target_pairs={{0,3},{1,0},{2,1},{3,2},{4,7},{5,4},{6,5},{7,6},{8,11},{9,8},{10,9... | collective-permute-start | bytes 3145736 | tf_op jit(solution)/shard_map/ppermute | solution.py:133
  154.9 50.3 %all-to-all-start.2 = ((bf16[64,3,32,128]{3,2,1,0:T(8,128)(2,1)}), bf16[64,3,32,128]{3,2,1,0:T(8,128)(2,1)S(1)}, u32[]{:S(2)}, u32[]{:S(2)}) async-start(bf16[64,3,32,128]{3,2,1,0:T(8,128)(2,1)} %bitcast.16), calls=%async_computation.2 | async-start | bytes 3145728 | tf_op jit(solution)/shard_map/all_to_all | solution.py:310
  172.5 13.7 %collective-permute-start.18 = (bf16[4,128,512]{2,1,0:T(8,128)(2,1)S(1)}, bf16[4,128,512]{2,1,0:T(8,128)(2,1)S(1)}, u32[]{:S(2)}, u32[]{:S(2)}) collective-permute-start(bf16[4,128,512]{2,1,0:T(8,128)(2,1)S(1)} %slice.18), channel_id=1, source_target_pairs={{0,1},{1,2},{2,3},{3,0},{4,5},{5,6},{6,7},{7,4},{8,9},{9,10},{10,1... | collective-permute-start | bytes 1572872 | tf_op jit(solution)/shard_map/ppermute | solution.py:139
  173.5 12.7 %collective-permute-start.19 = (bf16[4,128,512]{2,1,0:T(8,128)(2,1)S(1)}, bf16[4,128,512]{2,1,0:T(8,128)(2,1)S(1)}, u32[]{:S(2)}, u32[]{:S(2)}) collective-permute-start(bf16[4,128,512]{2,1,0:T(8,128)(2,1)S(1)} %slice.19), channel_id=1, source_target_pairs={{0,3},{1,0},{2,1},{3,2},{4,7},{5,4},{6,5},{7,6},{8,11},{9,8},{10,9... | collective-permute-start | bytes 1572872 | tf_op jit(solution)/shard_map/ppermute | solution.py:140
  205.3 45.5 %all-to-all-start.3 = ((bf16[64,3,32,128]{3,2,1,0:T(8,128)(2,1)}), bf16[64,3,32,128]{3,2,1,0:T(8,128)(2,1)S(1)}, u32[]{:S(2)}, u32[]{:S(2)}) async-start(bf16[64,3,32,128]{3,2,1,0:T(8,128)(2,1)} %bitcast.17), calls=%async_computation.3 | async-start | bytes 3145728 | tf_op jit(solution)/shard_map/all_to_all | solution.py:310
  (18 other events, 205.3 us)

commit v6 on v4

--- a/solution.py
+++ b/solution.py
@@ -10,7 +10,7 @@
 CAP = 3
 ITEMS = RS * CB
 MIB = 1 << 20
-NEAR, FAR = 20, 8
+NEAR, FAR = 20, 14
 BF16 = jnp.bfloat16
 F32 = jnp.float32
 
@@ -371,7 +371,7 @@
         scratch,
         5,
         20,
-        free=(1, 2, 9, 10),
+        free=(1, 2),
         grid=(),
     )
 
@@ -425,7 +425,7 @@
     phi_2, outgoing_2 = ph_half(True, send_index, scaled, pieces_2, NEAR)
     pp_pieces = gather_rows(*after(pp_halves, pieces_2), between=outgoing_2)
     came_2 = exchange(outgoing_2)
-    held = tuple(hold(x, FAR) for x in pp_pieces[2:6])
+    held = tuple(hold(x, FAR) if k in (1, 2) else x for k, x in enumerate(pp_pieces[2:6]))
     leaving = pp_whole(
         recv_index, came_1, came_2, chi_pp, pp_pieces[:2] + held + pp_pieces[6:]
     )

time: 255 us -> 253 us (level)
  starting transfers between devices: 56.5 us -> 53.4 us
    pallas_call x12 -> x10, Pallas kernels: 33.9 us -> 36.3 us  [call(): pl.pallas_call(kernel, grid_spec=pltpu.PrefetchScalarGridSpec(num_scalar_...]
    unnamed x22 -> x20, local copies, waits for them, and re-layouts: 5.3 us -> 2.92 us
  transfers between devices with their start and end apart: 19 -> 19, of which waited for: 11 -> 12; matrix products, arithmetic and copies ran while one was open for 1% -> 1% of each run, Pallas kernels for 8% -> 8%
where the time goes in v6:
time: 253 us; the launch traced here: 252 us
  waiting for transfers between devices  155 us (61%)
  starting transfers between devices  53.4 us (21%)
  Pallas kernels  36.3 us (14%)
  local copies, waits for them, and re-layouts  6.89 us (3%)
    all_to_all x3, waiting for transfers between devices, exchange(): lax.all_to_all(slots.reshape((nboson, CAP) + tile), 'boson', split_axis=0...  76 us
    pallas_call x10, Pallas kernels, call(): pl.pallas_call(kernel, grid_spec=pltpu.PrefetchScalarGridSpec(num_scalar_...  36.3 us
    ppermute x2, waiting for transfers between devices, gather_rows(): below_low = lax.ppermute(low, 'block', up)  29.3 us
    all_to_all x3, starting transfers between devices, exchange(): lax.all_to_all(slots.reshape((nboson, CAP) + tile), 'boson', split_axis=0...  28.4 us
    ppermute x2, waiting for transfers between devices, gather_rows(): far_low = lax.ppermute(near[0], 'block', up)  28.2 us
    ppermute x1, waiting for transfers between devices, gather_whole(): lax.ppermute(near_low, 'block', up)  9.89 us
    ppermute x1, waiting for transfers between devices, gather_whole(): below = lax.ppermute(own, 'block', up)  6.84 us
  transfers between devices with their start and end apart: 19, of which 12 were waited for; matrix products, arithmetic and copies ran while one was open for 1% of the time, Pallas kernels for 8%

profile of v6, /device:TPU:2, one launch (start us, length us, event | category | flops | bytes accessed | tf_op | source)
XLA Modules:
  0.0 252.4 jit_solution(3337929956995017555)
XLA Ops:
  1.5 3.2 %shard_map.65 = (bf16[4,256,256]{2,1,0:T(8,128)(2,1)S(1)}, bf16[4,256,256]{2,1,0:T(8,128)(2,1)S(1)}) custom-call(bf16[4,256,1024]{2,1,0:T(8,128)(2,1)} %refs_0_.1), custom_call_target="tpu_custom_call" | custom-call | flops 2000000000 | bytes 6000000 | tf_op jit(solution)/shard_map/pallas_call | solution.py:244
  8.4 2.9 %collective-permute-start.2 = (bf16[4,256,256]{2,1,0:T(8,128)(2,1)S(1)}, bf16[4,256,256]{2,1,0:T(8,128)(2,1)S(1)}, u32[]{:S(2)}, u32[]{:S(2)}) collective-permute-start(bf16[4,256,256]{2,1,0:T(8,128)(2,1)S(1)} %get-tuple-element.24.refs_2_), channel_id=1, source_target_pairs={{0,3},{1,0},{2,1},{3,2},{4,7},{5,4},{6,5},{7,6},{8,11},{9,8},{10,9... | collective-permute-start | bytes 1572872 | tf_op jit(solution)/shard_map/ppermute | solution.py:102
  12.8 8.0 %collective-permute-done.refs_4_ = bf16[4,256,256]{2,1,0:T(8,128)(2,1)S(1)} collective-permute-done((bf16[4,256,256]{2,1,0:T(8,128)(2,1)S(1)}, bf16[4,256,256]{2,1,0:T(8,128)(2,1)S(1)}, u32[]{:S(2)}, u32[]{:S(2)}) %collective-permute-start) | collective-permute-done | bytes 524320 | tf_op jit(solution)/shard_map/ppermute | solution.py:99
  26.3 2.9 %shard_map.64.refs_1_ = bf16[4,256,1024]{2,1,0:T(8,128)(2,1)S(1)} custom-call(bf16[4,256,1024]{2,1,0:T(8,128)(2,1)} %gamma.1, f32[4,1024]{1,0:T(4,128)} %chi.2), custom_call_target="tpu_custom_call" | custom-call | flops 2000000000 | bytes 6000000 | tf_op jit(solution)/shard_map/pallas_call | solution.py:244
  29.2 2.9 %collective-permute-done.1.refs_5_ = bf16[4,256,256]{2,1,0:T(8,128)(2,1)S(1)} collective-permute-done((bf16[4,256,256]{2,1,0:T(8,128)(2,1)S(1)}, bf16[4,256,256]{2,1,0:T(8,128)(2,1)S(1)}, u32[]{:S(2)}, u32[]{:S(2)}) %collective-permute-start.1) | collective-permute-done | bytes 524320 | tf_op jit(solution)/shard_map/ppermute | solution.py:101
  32.5 9.7 %collective-permute-done.4.refs_8_ = bf16[4,256,256]{2,1,0:T(8,128)(2,1)S(1)} collective-permute-done((bf16[4,256,256]{2,1,0:T(8,128)(2,1)S(1)}, bf16[4,256,256]{2,1,0:T(8,128)(2,1)S(1)}, u32[]{:S(2)}, u32[]{:S(2)}) %collective-permute-start.4) | collective-permute-done | bytes 524320 | tf_op jit(solution)/shard_map/ppermute | solution.py:106
  45.5 3.3 %shard_map.66 = (f32[4,256,512]{2,1,0:T(8,128)}, bf16[192,32,128]{2,1,0:T(8,128)(2,1)}) custom-call(s32[136]{0:T(256)S(1)} %concatenate.6.refs_0_.index, bf16[4,256,1024]{2,1,0:T(8,128)(2,1)S(1)} %shard_map.64.refs_1_, bf16[4,256,256]{2,1,0:T(8,128)(2,1)S(1)} %get-tuple-element.24.refs_2_, bf16[4,256,256]{2,1,0:T(8,128)(2,1)S(1)} %get-tuple-element.25.refs_3_, ...), custom_call_target="tpu_custom_call" | custom-call | flops 4000000000 | bytes 12000000 | tf_op jit(solution)/shard_map/pallas_call | solution.py:244
  48.8 12.0 %all-to-all-start = ((bf16[64,3,32,128]{3,2,1,0:T(8,128)(2,1)}), bf16[64,3,32,128]{3,2,1,0:T(8,128)(2,1)S(1)}, u32[]{:S(2)}, u32[]{:S(2)}) async-start(bf16[64,3,32,128]{3,2,1,0:T(8,128)(2,1)} %bitcast.10), calls=%async_computation | async-start | bytes 3145728 | tf_op jit(solution)/shard_map/all_to_all | solution.py:290
  60.8 6.8 %collective-permute-done.6.refs_3_ = bf16[4,256,512]{2,1,0:T(8,128)(2,1)} collective-permute-done((bf16[4,256,512]{2,1,0:T(8,128)(2,1)S(1)}, bf16[4,256,512]{2,1,0:T(8,128)(2,1)}, u32[]{:S(2)}, u32[]{:S(2)}) %collective-permute-start.6) | collective-permute-done | bytes 1048608 | tf_op jit(solution)/shard_map/ppermute | solution.py:116
  69.9 3.2 %collective-permute-start.9 = (bf16[4,128,512]{2,1,0:T(8,128)(2,1)S(1)}, bf16[4,128,512]{2,1,0:T(8,128)(2,1)S(1)}, u32[]{:S(2)}, u32[]{:S(2)}) collective-permute-start(bf16[4,128,512]{2,1,0:T(8,128)(2,1)S(1)} %slice.17), channel_id=1, source_target_pairs={{0,3},{1,0},{2,1},{3,2},{4,7},{5,4},{6,5},{7,6},{8,11},{9,8},{10,9... | collective-permute-start | bytes 1572872 | tf_op jit(solution)/shard_map/ppermute | solution.py:124
  73.2 9.9 %collective-permute-done.8.refs_5_ = bf16[4,128,512]{2,1,0:T(8,128)(2,1)S(1)} collective-permute-done((bf16[4,128,512]{2,1,0:T(8,128)(2,1)S(1)}, bf16[4,128,512]{2,1,0:T(8,128)(2,1)S(1)}, u32[]{:S(2)}, u32[]{:S(2)}) %collective-permute-start.8) | collective-permute-done | bytes 524320 | tf_op jit(solution)/shard_map/ppermute | solution.py:123
  83.3 3.2 %collective-permute-start.13 = (bf16[4,128,1024]{2,1,0:T(8,128)(2,1)}, bf16[4,128,1024]{2,1,0:T(8,128)(2,1)}, u32[]{:S(2)}, u32[]{:S(2)}) collective-permute-start(bf16[4,128,1024]{2,1,0:T(8,128)(2,1)} %get-tuple-element.36.refs_1_), channel_id=1, source_target_pairs={{0,3},{1,0},{2,1},{3,2},{4,7},{5,4},{6,5},{7,6},{8,11},{9,8},{10,9... | collective-permute-start | bytes 3145736 | tf_op jit(solution)/shard_map/ppermute | solution.py:100
  86.6 6.3 %shard_map.68 = (f32[4,256,512]{2,1,0:T(8,128)}, bf16[192,32,128]{2,1,0:T(8,128)(2,1)}) custom-call(s32[136]{0:T(256)S(1)} %concatenate.6.refs_0_.index, bf16[4,256,1024]{2,1,0:T(8,128)(2,1)} %copy-done.3, bf16[4,256,512]{2,1,0:T(8,128)(2,1)} %copy-done.1, bf16[4,256,512]{2,1,0:T(8,128)(2,1)} %collective-permute-done.6.refs_3_, ...), custom_call_target="tpu_custom_call" | custom-call | flops 20000000000 | bytes 60000000 | tf_op jit(solution)/shard_map/pallas_call | solution.py:244
  92.9 8.0 %all-to-all-done = bf16[64,3,32,128]{3,2,1,0:T(8,128)(2,1)S(1)} async-done(((bf16[64,3,32,128]{3,2,1,0:T(8,128)(2,1)}), bf16[64,3,32,128]{3,2,1,0:T(8,128)(2,1)S(1)}, u32[]{:S(2)}, u32[]{:S(2)}) %all-to-all-start) | async-done | bytes 1572896 | tf_op jit(solution)/shard_map/all_to_all | solution.py:290
  100.9 5.4 %all-to-all-start.1 = ((bf16[64,3,32,128]{3,2,1,0:T(8,128)(2,1)}), bf16[64,3,32,128]{3,2,1,0:T(8,128)(2,1)S(1)}, u32[]{:S(2)}, u32[]{:S(2)}) async-start(bf16[64,3,32,128]{3,2,1,0:T(8,128)(2,1)} %bitcast.11), calls=%async_computation.1 | async-start | bytes 3145728 | tf_op jit(solution)/shard_map/all_to_all | solution.py:290
  106.3 1.9 collective-permute-start.12
  108.2 21.3 %collective-permute-done.10.refs_2_ = bf16[4,128,1024]{2,1,0:T(8,128)(2,1)} collective-permute-done((bf16[4,128,1024]{2,1,0:T(8,128)(2,1)}, bf16[4,128,1024]{2,1,0:T(8,128)(2,1)}, u32[]{:S(2)}, u32[]{:S(2)}) %collective-permute-start.10) | collective-permute-done | bytes 1048608 | tf_op jit(solution)/shard_map/ppermute | solution.py:99
  129.5 3.2 %collective-permute-start.15 = (bf16[4,128,1024]{2,1,0:T(8,128)(2,1)}, bf16[4,128,1024]{2,1,0:T(8,128)(2,1)}, u32[]{:S(2)}, u32[]{:S(2)}) collective-permute-start(bf16[4,128,1024]{2,1,0:T(8,128)(2,1)} %collective-permute-done.13.refs_5_), channel_id=1, source_target_pairs={{0,3},{1,0},{2,1},{3,2},{4,7},{5,4},{6,5},{7,6},{8,11},{9,8},{10,9... | collective-permute-start | bytes 3145736 | tf_op jit(solution)/shard_map/ppermute | solution.py:107
  133.8 18.5 %collective-permute-done.14.refs_6_ = bf16[4,128,1024]{2,1,0:T(8,128)(2,1)S(1)} collective-permute-done((bf16[4,128,1024]{2,1,0:T(8,128)(2,1)}, bf16[4,128,1024]{2,1,0:T(8,128)(2,1)S(1)}, u32[]{:S(2)}, u32[]{:S(2)}) %collective-permute-start.14) | collective-permute-done | bytes 1048608 | tf_op jit(solution)/shard_map/ppermute | solution.py:106
  154.4 9.5 %shard_map.72 = bf16[192,64,128]{2,1,0:T(8,128)(2,1)} custom-call(s32[136]{0:T(256)S(1)} %concatenate.7.index, bf16[192,32,128]{2,1,0:T(8,128)(2,1)} %bitcast.9, bf16[192,32,128]{2,1,0:T(8,128)(2,1)S(1)} %bitcast.7, f32[4,1024]{1,0:T(4,128)S(1)} %copy-done.2, bf16[4,128,1024]{2,1,0:T(8,128)(2,1)} %get-tuple-element.35.refs_0_, ...), custom_call_target="tpu_custom_call" | custom-call | flops 5000000000 | bytes 15000000 | tf_op jit(solution)/shard_map/pallas_call | solution.py:244
  163.9 10.9 %all-to-all-start.2 = ((bf16[64,3,64,128]{3,2,1,0:T(8,128)(2,1)}), bf16[64,3,64,128]{3,2,1,0:T(8,128)(2,1)S(1)}, u32[]{:S(2)}, u32[]{:S(2)}) async-start(bf16[64,3,64,128]{3,2,1,0:T(8,128)(2,1)} %bitcast.8), calls=%async_computation.2 | async-start | bytes 6291456 | tf_op jit(solution)/shard_map/all_to_all | solution.py:290
  174.8 5.7 %shard_map.69.base_in = f32[4,256,1024]{2,1,0:T(8,128)} custom-call(bf16[4,256,1024]{2,1,0:T(8,128)(2,1)} %gamma.1, f32[4,256,512]{2,1,0:T(8,128)} %get-tuple-element.28.first, f32[4,256,512]{2,1,0:T(8,128)} %get-tuple-element.33.second), custom_call_target="tpu_custom_call" | custom-call | flops 4000000000 | bytes 12000000 | tf_op jit(solution)/shard_map/pallas_call | solution.py:244
  180.5 68.0 %all-to-all-done.2 = bf16[64,3,64,128]{3,2,1,0:T(8,128)(2,1)S(1)} async-done(((bf16[64,3,64,128]{3,2,1,0:T(8,128)(2,1)}), bf16[64,3,64,128]{3,2,1,0:T(8,128)(2,1)S(1)}, u32[]{:S(2)}, u32[]{:S(2)}) %all-to-all-start.2) | async-done | bytes 3145760 | tf_op jit(solution)/shard_map/all_to_all | solution.py:290
  248.6 3.7 %shard_map.73 = bf16[4,256,1024]{2,1,0:T(8,128)(2,1)} custom-call(s32[136]{0:T(256)S(1)} %concatenate.6.refs_0_.index, f32[4,256,1024]{2,1,0:T(8,128)} %shard_map.69.base_in, bf16[192,64,128]{2,1,0:T(8,128)(2,1)S(1)} %bitcast.6), custom_call_target="tpu_custom_call" | custom-call | flops 3000000000 | bytes 9000000 | tf_op jit(solution)/shard_map/pallas_call | solution.py:244
  (56 shorter events, 21.4 us)
Async XLA Ops:
  1.5 9.8 %copy-start.4 = (bf16[4,256,1024]{2,1,0:T(8,128)(2,1)S(1)}, bf16[4,256,1024]{2,1,0:T(8,128)(2,1)}, u32[]{:S(2)}) copy-start(bf16[4,256,1024]{2,1,0:T(8,128)(2,1)} %param.9) | copy-start | bytes 6291460
  4.8 16.1 %collective-permute-start = (bf16[4,256,256]{2,1,0:T(8,128)(2,1)S(1)}, bf16[4,256,256]{2,1,0:T(8,128)(2,1)S(1)}, u32[]{:S(2)}, u32[]{:S(2)}) collective-permute-start(bf16[4,256,256]{2,1,0:T(8,128)(2,1)S(1)} %get-tuple-element.24.refs_2_), channel_id=1, source_target_pairs={{0,1},{1,2},{2,3},{3,0},{4,5},{5,6},{6,7},{7,4},{8,9},{9,10},{10,1... | collective-permute-start | bytes 1572872 | tf_op jit(solution)/shard_map/ppermute | solution.py:99
  6.4 14.8 %collective-permute-start.3 = (bf16[4,256,256]{2,1,0:T(8,128)(2,1)S(1)}, bf16[4,256,256]{2,1,0:T(8,128)(2,1)S(1)}, u32[]{:S(2)}, u32[]{:S(2)}) collective-permute-start(bf16[4,256,256]{2,1,0:T(8,128)(2,1)S(1)} %get-tuple-element.25.refs_3_), channel_id=1, source_target_pairs={{0,3},{1,0},{2,1},{3,2},{4,7},{5,4},{6,5},{7,6},{8,11},{9,8},{10,9... | collective-permute-start | bytes 1572872 | tf_op jit(solution)/shard_map/ppermute | solution.py:100
  8.1 24.0 %collective-permute-start.1 = (bf16[4,256,256]{2,1,0:T(8,128)(2,1)S(1)}, bf16[4,256,256]{2,1,0:T(8,128)(2,1)S(1)}, u32[]{:S(2)}, u32[]{:S(2)}) collective-permute-start(bf16[4,256,256]{2,1,0:T(8,128)(2,1)S(1)} %get-tuple-element.25.refs_3_), channel_id=1, source_target_pairs={{0,1},{1,2},{2,3},{3,0},{4,5},{5,6},{6,7},{7,4},{8,9},{9,10},{10,1... | collective-permute-start | bytes 1572872 | tf_op jit(solution)/shard_map/ppermute | solution.py:101
  8.4 24.1 %collective-permute-start.2 = (bf16[4,256,256]{2,1,0:T(8,128)(2,1)S(1)}, bf16[4,256,256]{2,1,0:T(8,128)(2,1)S(1)}, u32[]{:S(2)}, u32[]{:S(2)}) collective-permute-start(bf16[4,256,256]{2,1,0:T(8,128)(2,1)S(1)} %get-tuple-element.24.refs_2_), channel_id=1, source_target_pairs={{0,3},{1,0},{2,1},{3,2},{4,7},{5,4},{6,5},{7,6},{8,11},{9,8},{10,9... | collective-permute-start | bytes 1572872 | tf_op jit(solution)/shard_map/ppermute | solution.py:102
  21.3 21.0 %collective-permute-start.4 = (bf16[4,256,256]{2,1,0:T(8,128)(2,1)S(1)}, bf16[4,256,256]{2,1,0:T(8,128)(2,1)S(1)}, u32[]{:S(2)}, u32[]{:S(2)}) collective-permute-start(bf16[4,256,256]{2,1,0:T(8,128)(2,1)S(1)} %collective-permute-done.refs_4_), channel_id=1, source_target_pairs={{0,1},{1,2},{2,3},{3,0},{4,5},{5,6},{6,7},{7,4},{8,9},{9,10},{10,1... | collective-permute-start | bytes 1572872 | tf_op jit(solution)/shard_map/ppermute | solution.py:106
  22.8 19.4 %collective-permute-start.5 = (bf16[4,256,256]{2,1,0:T(8,128)(2,1)S(1)}, bf16[4,256,256]{2,1,0:T(8,128)(2,1)S(1)}, u32[]{:S(2)}, u32[]{:S(2)}) collective-permute-start(bf16[4,256,256]{2,1,0:T(8,128)(2,1)S(1)} %collective-permute-done.3.refs_7_), channel_id=1, source_target_pairs={{0,3},{1,0},{2,1},{3,2},{4,7},{5,4},{6,5},{7,6},{8,11},{9,8},{10,9... | collective-permute-start | bytes 1572872 | tf_op jit(solution)/shard_map/ppermute | solution.py:107
  26.3 17.6 %copy-start.1 = (bf16[4,256,512]{2,1,0:T(8,128)(2,1)}, bf16[4,256,512]{2,1,0:T(8,128)(2,1)S(1)}, u32[]{:S(2)}) copy-start(bf16[4,256,512]{2,1,0:T(8,128)(2,1)S(1)} %shard_map.67.refs_2_) | copy-start | bytes 3145732
  29.2 19.6 %copy-start.3 = (bf16[4,256,1024]{2,1,0:T(8,128)(2,1)}, bf16[4,256,1024]{2,1,0:T(8,128)(2,1)S(1)}, u32[]{:S(2)}) copy-start(bf16[4,256,1024]{2,1,0:T(8,128)(2,1)S(1)} %shard_map.64.refs_1_) | copy-start | bytes 6291460
  42.3 25.4 %collective-permute-start.6 = (bf16[4,256,512]{2,1,0:T(8,128)(2,1)S(1)}, bf16[4,256,512]{2,1,0:T(8,128)(2,1)}, u32[]{:S(2)}, u32[]{:S(2)}) collective-permute-start(bf16[4,256,512]{2,1,0:T(8,128)(2,1)S(1)} %shard_map.67.refs_2_), channel_id=1, source_target_pairs={{0,1},{1,2},{2,3},{3,0},{4,5},{5,6},{6,7},{7,4},{8,9},{9,10},{10,1... | collective-permute-start | bytes 3145736 | tf_op jit(solution)/shard_map/ppermute | solution.py:116
  43.8 24.9 %collective-permute-start.7 = (bf16[4,256,512]{2,1,0:T(8,128)(2,1)S(1)}, bf16[4,256,512]{2,1,0:T(8,128)(2,1)}, u32[]{:S(2)}, u32[]{:S(2)}) collective-permute-start(bf16[4,256,512]{2,1,0:T(8,128)(2,1)S(1)} %shard_map.67.refs_2_), channel_id=1, source_target_pairs={{0,3},{1,0},{2,1},{3,2},{4,7},{5,4},{6,5},{7,6},{8,11},{9,8},{10,9... | collective-permute-start | bytes 3145736 | tf_op jit(solution)/shard_map/ppermute | solution.py:117
  48.8 52.1 %all-to-all-start = ((bf16[64,3,32,128]{3,2,1,0:T(8,128)(2,1)}), bf16[64,3,32,128]{3,2,1,0:T(8,128)(2,1)S(1)}, u32[]{:S(2)}, u32[]{:S(2)}) async-start(bf16[64,3,32,128]{3,2,1,0:T(8,128)(2,1)} %bitcast.10), calls=%async_computation | async-start | bytes 3145728 | tf_op jit(solution)/shard_map/all_to_all | solution.py:290
  69.8 13.2 %collective-permute-start.8 = (bf16[4,128,512]{2,1,0:T(8,128)(2,1)S(1)}, bf16[4,128,512]{2,1,0:T(8,128)(2,1)S(1)}, u32[]{:S(2)}, u32[]{:S(2)}) collective-permute-start(bf16[4,128,512]{2,1,0:T(8,128)(2,1)S(1)} %slice.16), channel_id=1, source_target_pairs={{0,1},{1,2},{2,3},{3,0},{4,5},{5,6},{6,7},{7,4},{8,9},{9,10},{10,1... | collective-permute-start | bytes 1572872 | tf_op jit(solution)/shard_map/ppermute | solution.py:123
  69.9 13.1 %collective-permute-start.9 = (bf16[4,128,512]{2,1,0:T(8,128)(2,1)S(1)}, bf16[4,128,512]{2,1,0:T(8,128)(2,1)S(1)}, u32[]{:S(2)}, u32[]{:S(2)}) collective-permute-start(bf16[4,128,512]{2,1,0:T(8,128)(2,1)S(1)} %slice.17), channel_id=1, source_target_pairs={{0,3},{1,0},{2,1},{3,2},{4,7},{5,4},{6,5},{7,6},{8,11},{9,8},{10,9... | collective-permute-start | bytes 1572872 | tf_op jit(solution)/shard_map/ppermute | solution.py:124
  83.1 49.7 %collective-permute-start.11 = (bf16[4,128,1024]{2,1,0:T(8,128)(2,1)}, bf16[4,128,1024]{2,1,0:T(8,128)(2,1)}, u32[]{:S(2)}, u32[]{:S(2)}) collective-permute-start(bf16[4,128,1024]{2,1,0:T(8,128)(2,1)} %get-tuple-element.36.refs_1_), channel_id=1, source_target_pairs={{0,1},{1,2},{2,3},{3,0},{4,5},{5,6},{6,7},{7,4},{8,9},{9,10},{10,1... | collective-permute-start | bytes 3145736 | tf_op jit(solution)/shard_map/ppermute | solution.py:101
  83.3 46.2 %collective-permute-start.13 = (bf16[4,128,1024]{2,1,0:T(8,128)(2,1)}, bf16[4,128,1024]{2,1,0:T(8,128)(2,1)}, u32[]{:S(2)}, u32[]{:S(2)}) collective-permute-start(bf16[4,128,1024]{2,1,0:T(8,128)(2,1)} %get-tuple-element.36.refs_1_), channel_id=1, source_target_pairs={{0,3},{1,0},{2,1},{3,2},{4,7},{5,4},{6,5},{7,6},{8,11},{9,8},{10,9... | collective-permute-start | bytes 3145736 | tf_op jit(solution)/shard_map/ppermute | solution.py:100
  86.5 43.0 %collective-permute-start.10 = (bf16[4,128,1024]{2,1,0:T(8,128)(2,1)}, bf16[4,128,1024]{2,1,0:T(8,128)(2,1)}, u32[]{:S(2)}, u32[]{:S(2)}) collective-permute-start(bf16[4,128,1024]{2,1,0:T(8,128)(2,1)} %get-tuple-element.35.refs_0_), channel_id=1, source_target_pairs={{0,1},{1,2},{2,3},{3,0},{4,5},{5,6},{6,7},{7,4},{8,9},{9,10},{10,1... | collective-permute-start | bytes 3145736 | tf_op jit(solution)/shard_map/ppermute | solution.py:99
  100.9 31.9 %copy-start.5 = (bf16[64,3,32,128]{3,2,1,0:T(8,128)(2,1)}, bf16[64,3,32,128]{3,2,1,0:T(8,128)(2,1)S(1)}, u32[]{:S(2)}) copy-start(bf16[64,3,32,128]{3,2,1,0:T(8,128)(2,1)S(1)} %all-to-all-done) | copy-start | bytes 4718596
  100.9 53.5 %all-to-all-start.1 = ((bf16[64,3,32,128]{3,2,1,0:T(8,128)(2,1)}), bf16[64,3,32,128]{3,2,1,0:T(8,128)(2,1)S(1)}, u32[]{:S(2)}, u32[]{:S(2)}) async-start(bf16[64,3,32,128]{3,2,1,0:T(8,128)(2,1)} %bitcast.11), calls=%async_computation.1 | async-start | bytes 3145728 | tf_op jit(solution)/shard_map/all_to_all | solution.py:290
  106.3 26.5 %collective-permute-start.12 = (bf16[4,128,1024]{2,1,0:T(8,128)(2,1)}, bf16[4,128,1024]{2,1,0:T(8,128)(2,1)S(1)}, u32[]{:S(2)}, u32[]{:S(2)}) collective-permute-start(bf16[4,128,1024]{2,1,0:T(8,128)(2,1)} %get-tuple-element.35.refs_0_), channel_id=1, source_target_pairs={{0,3},{1,0},{2,1},{3,2},{4,7},{5,4},{6,5},{7,6},{8,11},{9,8},{10,9... | collective-permute-start | bytes 3145736 | tf_op jit(solution)/shard_map/ppermute | solution.py:102
  129.5 22.7 %collective-permute-start.14 = (bf16[4,128,1024]{2,1,0:T(8,128)(2,1)}, bf16[4,128,1024]{2,1,0:T(8,128)(2,1)S(1)}, u32[]{:S(2)}, u32[]{:S(2)}) collective-permute-start(bf16[4,128,1024]{2,1,0:T(8,128)(2,1)} %collective-permute-done.10.refs_2_), channel_id=1, source_target_pairs={{0,1},{1,2},{2,3},{3,0},{4,5},{5,6},{6,7},{7,4},{8,9},{9,10},{10,1... | collective-permute-start | bytes 3145736 | tf_op jit(solution)/shard_map/ppermute | solution.py:106
  129.5 24.8 %collective-permute-start.15 = (bf16[4,128,1024]{2,1,0:T(8,128)(2,1)}, bf16[4,128,1024]{2,1,0:T(8,128)(2,1)}, u32[]{:S(2)}, u32[]{:S(2)}) collective-permute-start(bf16[4,128,1024]{2,1,0:T(8,128)(2,1)} %collective-permute-done.13.refs_5_), channel_id=1, source_target_pairs={{0,3},{1,0},{2,1},{3,2},{4,7},{5,4},{6,5},{7,6},{8,11},{9,8},{10,9... | collective-permute-start | bytes 3145736 | tf_op jit(solution)/shard_map/ppermute | solution.py:107
  132.8 21.6 %copy-start.2 = (f32[4,1024]{1,0:T(4,128)S(1)}, f32[4,1024]{1,0:T(4,128)}, u32[]{:S(2)}) copy-start(f32[4,1024]{1,0:T(4,128)} %chi.3) | copy-start | bytes 49156
  163.9 84.7 %all-to-all-start.2 = ((bf16[64,3,64,128]{3,2,1,0:T(8,128)(2,1)}), bf16[64,3,64,128]{3,2,1,0:T(8,128)(2,1)S(1)}, u32[]{:S(2)}, u32[]{:S(2)}) async-start(bf16[64,3,64,128]{3,2,1,0:T(8,128)(2,1)} %bitcast.8), calls=%async_computation.2 | async-start | bytes 6291456 | tf_op jit(solution)/shard_map/all_to_all | solution.py:290
  (5 other events, 9.9 us)

commit v7 on v6

--- a/solution.py
+++ b/solution.py
@@ -177,7 +177,7 @@
 
 def pp_kernel(index, first_in, second, chi, *refs):
     pieces, slots_out = refs[:8], refs[8]
-    right, first, slots, lhs, in_sems, slot_sems = refs[9:]
+    right, first, tiles, lhs, in_sems, slot_sems = refs[9:]
     arrivals = start_all([pltpu.make_async_copy(first_in, first, slot_sems.at[0])])
     loads = right_loads(pieces, index[128], right, in_sems)
     wait_all(arrivals)
@@ -201,9 +201,11 @@
             phi = jnp.dot(lhs[...], right[p, :, columns], preferred_element_type=F32).astype(BF16)
             for r in range(RS):
                 for c in range(4):
-                    slot = index[p * ITEMS + r * CB + half * 4 + c]
-                    slots[slot] = phi[r * 64 : r * 64 + 64, c * 128 : c * 128 + 128]
-    wait_all(start_all([pltpu.make_async_copy(slots, slots_out, slot_sems.at[1])]))
+                    item = p * ITEMS + r * CB + half * 4 + c
+                    tiles[item] = phi[r * 64 : r * 64 + 64, c * 128 : c * 128 + 128]
+                    to = slots_out.at[index[item]]
+                    pltpu.make_async_copy(tiles.at[item], to, slot_sems.at[1]).start()
+    pltpu.make_async_copy(tiles, slots_out.at[: 4 * ITEMS], slot_sems.at[1]).wait()
 
 
 def base_kernel(gamma, first, second, out):
@@ -359,7 +361,7 @@
 
 
 def pp_whole(index, came_1, came_2, chi, pieces):
-    scratch = [pltpu.VMEM((4, 1024, 1024), BF16), vmem(came_1), pltpu.VMEM(TILES, BF16)]
+    scratch = [pltpu.VMEM((4, 1024, 1024), BF16), vmem(came_1), pltpu.VMEM((4 * ITEMS, 64, 128), BF16)]
     scratch += [pltpu.VMEM((256, 1024), BF16), DMA((8, 4)), DMA((2,))]
     return call(
         pp_kernel,

time: 253 us -> 252 us (level)
  no operation moved by 1% of the time
where the time goes in v7:
time: 252 us; the launch traced here: 251 us
  waiting for transfers between devices  155 us (62%)
  starting transfers between devices  53.3 us (21%)
  Pallas kernels  35.3 us (14%)
  local copies, waits for them, and re-layouts  6.89 us (3%)
    all_to_all x3, waiting for transfers between devices, exchange(): lax.all_to_all(slots.reshape((nboson, CAP) + tile), 'boson', split_axis=0...  76 us
    pallas_call x10, Pallas kernels, call(): pl.pallas_call(kernel, grid_spec=pltpu.PrefetchScalarGridSpec(num_scalar_...  35.3 us
    ppermute x2, waiting for transfers between devices, gather_rows(): below_low = lax.ppermute(low, 'block', up)  29.3 us
    all_to_all x3, starting transfers between devices, exchange(): lax.all_to_all(slots.reshape((nboson, CAP) + tile), 'boson', split_axis=0...  28.4 us
    ppermute x2, waiting for transfers between devices, gather_rows(): far_low = lax.ppermute(near[0], 'block', up)  28.2 us
    ppermute x1, waiting for transfers between devices, gather_whole(): lax.ppermute(near_low, 'block', up)  9.89 us
    ppermute x1, waiting for transfers between devices, gather_whole(): below = lax.ppermute(own, 'block', up)  6.84 us
  transfers between devices with their start and end apart: 19, of which 12 were waited for; matrix products, arithmetic and copies ran while one was open for 1% of the time, Pallas kernels for 8%

profile of v7, /device:TPU:2, one launch (start us, length us, event | category | flops | bytes accessed | tf_op | source)
XLA Modules:
  0.0 251.4 jit_solution(1037275805518728895)
XLA Ops:
  1.5 3.2 %shard_map.65 = (bf16[4,256,256]{2,1,0:T(8,128)(2,1)S(1)}, bf16[4,256,256]{2,1,0:T(8,128)(2,1)S(1)}) custom-call(bf16[4,256,1024]{2,1,0:T(8,128)(2,1)} %refs_0_.1), custom_call_target="tpu_custom_call" | custom-call | flops 2000000000 | bytes 6000000 | tf_op jit(solution)/shard_map/pallas_call | solution.py:246
  8.4 2.9 %collective-permute-start.2 = (bf16[4,256,256]{2,1,0:T(8,128)(2,1)S(1)}, bf16[4,256,256]{2,1,0:T(8,128)(2,1)S(1)}, u32[]{:S(2)}, u32[]{:S(2)}) collective-permute-start(bf16[4,256,256]{2,1,0:T(8,128)(2,1)S(1)} %get-tuple-element.24.refs_2_), channel_id=1, source_target_pairs={{0,3},{1,0},{2,1},{3,2},{4,7},{5,4},{6,5},{7,6},{8,11},{9,8},{10,9... | collective-permute-start | bytes 1572872 | tf_op jit(solution)/shard_map/ppermute | solution.py:102
  12.8 8.0 %collective-permute-done.refs_4_ = bf16[4,256,256]{2,1,0:T(8,128)(2,1)S(1)} collective-permute-done((bf16[4,256,256]{2,1,0:T(8,128)(2,1)S(1)}, bf16[4,256,256]{2,1,0:T(8,128)(2,1)S(1)}, u32[]{:S(2)}, u32[]{:S(2)}) %collective-permute-start) | collective-permute-done | bytes 524320 | tf_op jit(solution)/shard_map/ppermute | solution.py:99
  26.3 2.9 %shard_map.64.refs_1_ = bf16[4,256,1024]{2,1,0:T(8,128)(2,1)S(1)} custom-call(bf16[4,256,1024]{2,1,0:T(8,128)(2,1)} %gamma.1, f32[4,1024]{1,0:T(4,128)} %chi.2), custom_call_target="tpu_custom_call" | custom-call | flops 2000000000 | bytes 6000000 | tf_op jit(solution)/shard_map/pallas_call | solution.py:246
  29.2 2.9 %collective-permute-done.1.refs_5_ = bf16[4,256,256]{2,1,0:T(8,128)(2,1)S(1)} collective-permute-done((bf16[4,256,256]{2,1,0:T(8,128)(2,1)S(1)}, bf16[4,256,256]{2,1,0:T(8,128)(2,1)S(1)}, u32[]{:S(2)}, u32[]{:S(2)}) %collective-permute-start.1) | collective-permute-done | bytes 524320 | tf_op jit(solution)/shard_map/ppermute | solution.py:101
  32.5 9.7 %collective-permute-done.4.refs_8_ = bf16[4,256,256]{2,1,0:T(8,128)(2,1)S(1)} collective-permute-done((bf16[4,256,256]{2,1,0:T(8,128)(2,1)S(1)}, bf16[4,256,256]{2,1,0:T(8,128)(2,1)S(1)}, u32[]{:S(2)}, u32[]{:S(2)}) %collective-permute-start.4) | collective-permute-done | bytes 524320 | tf_op jit(solution)/shard_map/ppermute | solution.py:106
  45.5 3.3 %shard_map.66 = (f32[4,256,512]{2,1,0:T(8,128)}, bf16[192,32,128]{2,1,0:T(8,128)(2,1)}) custom-call(s32[136]{0:T(256)S(1)} %concatenate.6.refs_0_.index, bf16[4,256,1024]{2,1,0:T(8,128)(2,1)S(1)} %shard_map.64.refs_1_, bf16[4,256,256]{2,1,0:T(8,128)(2,1)S(1)} %get-tuple-element.24.refs_2_, bf16[4,256,256]{2,1,0:T(8,128)(2,1)S(1)} %get-tuple-element.25.refs_3_, ...), custom_call_target="tpu_custom_call" | custom-call | flops 4000000000 | bytes 12000000 | tf_op jit(solution)/shard_map/pallas_call | solution.py:246
  48.8 12.0 %all-to-all-start = ((bf16[64,3,32,128]{3,2,1,0:T(8,128)(2,1)}), bf16[64,3,32,128]{3,2,1,0:T(8,128)(2,1)S(1)}, u32[]{:S(2)}, u32[]{:S(2)}) async-start(bf16[64,3,32,128]{3,2,1,0:T(8,128)(2,1)} %bitcast.10), calls=%async_computation | async-start | bytes 3145728 | tf_op jit(solution)/shard_map/all_to_all | solution.py:292
  60.8 6.8 %collective-permute-done.6.refs_3_ = bf16[4,256,512]{2,1,0:T(8,128)(2,1)} collective-permute-done((bf16[4,256,512]{2,1,0:T(8,128)(2,1)S(1)}, bf16[4,256,512]{2,1,0:T(8,128)(2,1)}, u32[]{:S(2)}, u32[]{:S(2)}) %collective-permute-start.6) | collective-permute-done | bytes 1048608 | tf_op jit(solution)/shard_map/ppermute | solution.py:116
  69.9 3.2 %collective-permute-start.9 = (bf16[4,128,512]{2,1,0:T(8,128)(2,1)S(1)}, bf16[4,128,512]{2,1,0:T(8,128)(2,1)S(1)}, u32[]{:S(2)}, u32[]{:S(2)}) collective-permute-start(bf16[4,128,512]{2,1,0:T(8,128)(2,1)S(1)} %slice.17), channel_id=1, source_target_pairs={{0,3},{1,0},{2,1},{3,2},{4,7},{5,4},{6,5},{7,6},{8,11},{9,8},{10,9... | collective-permute-start | bytes 1572872 | tf_op jit(solution)/shard_map/ppermute | solution.py:124
  73.2 9.9 %collective-permute-done.8.refs_5_ = bf16[4,128,512]{2,1,0:T(8,128)(2,1)S(1)} collective-permute-done((bf16[4,128,512]{2,1,0:T(8,128)(2,1)S(1)}, bf16[4,128,512]{2,1,0:T(8,128)(2,1)S(1)}, u32[]{:S(2)}, u32[]{:S(2)}) %collective-permute-start.8) | collective-permute-done | bytes 524320 | tf_op jit(solution)/shard_map/ppermute | solution.py:123
  83.3 3.2 %collective-permute-start.13 = (bf16[4,128,1024]{2,1,0:T(8,128)(2,1)}, bf16[4,128,1024]{2,1,0:T(8,128)(2,1)}, u32[]{:S(2)}, u32[]{:S(2)}) collective-permute-start(bf16[4,128,1024]{2,1,0:T(8,128)(2,1)} %get-tuple-element.36.refs_1_), channel_id=1, source_target_pairs={{0,3},{1,0},{2,1},{3,2},{4,7},{5,4},{6,5},{7,6},{8,11},{9,8},{10,9... | collective-permute-start | bytes 3145736 | tf_op jit(solution)/shard_map/ppermute | solution.py:100
  86.6 6.3 %shard_map.68 = (f32[4,256,512]{2,1,0:T(8,128)}, bf16[192,32,128]{2,1,0:T(8,128)(2,1)}) custom-call(s32[136]{0:T(256)S(1)} %concatenate.6.refs_0_.index, bf16[4,256,1024]{2,1,0:T(8,128)(2,1)} %copy-done.3, bf16[4,256,512]{2,1,0:T(8,128)(2,1)} %copy-done.1, bf16[4,256,512]{2,1,0:T(8,128)(2,1)} %collective-permute-done.6.refs_3_, ...), custom_call_target="tpu_custom_call" | custom-call | flops 20000000000 | bytes 60000000 | tf_op jit(solution)/shard_map/pallas_call | solution.py:246
  92.9 8.0 %all-to-all-done = bf16[64,3,32,128]{3,2,1,0:T(8,128)(2,1)S(1)} async-done(((bf16[64,3,32,128]{3,2,1,0:T(8,128)(2,1)}), bf16[64,3,32,128]{3,2,1,0:T(8,128)(2,1)S(1)}, u32[]{:S(2)}, u32[]{:S(2)}) %all-to-all-start) | async-done | bytes 1572896 | tf_op jit(solution)/shard_map/all_to_all | solution.py:292
  100.9 5.4 %all-to-all-start.1 = ((bf16[64,3,32,128]{3,2,1,0:T(8,128)(2,1)}), bf16[64,3,32,128]{3,2,1,0:T(8,128)(2,1)S(1)}, u32[]{:S(2)}, u32[]{:S(2)}) async-start(bf16[64,3,32,128]{3,2,1,0:T(8,128)(2,1)} %bitcast.11), calls=%async_computation.1 | async-start | bytes 3145728 | tf_op jit(solution)/shard_map/all_to_all | solution.py:292
  106.3 1.9 collective-permute-start.12
  108.2 21.3 %collective-permute-done.10.refs_2_ = bf16[4,128,1024]{2,1,0:T(8,128)(2,1)} collective-permute-done((bf16[4,128,1024]{2,1,0:T(8,128)(2,1)}, bf16[4,128,1024]{2,1,0:T(8,128)(2,1)}, u32[]{:S(2)}, u32[]{:S(2)}) %collective-permute-start.10) | collective-permute-done | bytes 1048608 | tf_op jit(solution)/shard_map/ppermute | solution.py:99
  129.5 3.2 %collective-permute-start.15 = (bf16[4,128,1024]{2,1,0:T(8,128)(2,1)}, bf16[4,128,1024]{2,1,0:T(8,128)(2,1)}, u32[]{:S(2)}, u32[]{:S(2)}) collective-permute-start(bf16[4,128,1024]{2,1,0:T(8,128)(2,1)} %collective-permute-done.13.refs_5_), channel_id=1, source_target_pairs={{0,3},{1,0},{2,1},{3,2},{4,7},{5,4},{6,5},{7,6},{8,11},{9,8},{10,9... | collective-permute-start | bytes 3145736 | tf_op jit(solution)/shard_map/ppermute | solution.py:107
  133.8 18.5 %collective-permute-done.14.refs_6_ = bf16[4,128,1024]{2,1,0:T(8,128)(2,1)S(1)} collective-permute-done((bf16[4,128,1024]{2,1,0:T(8,128)(2,1)}, bf16[4,128,1024]{2,1,0:T(8,128)(2,1)S(1)}, u32[]{:S(2)}, u32[]{:S(2)}) %collective-permute-start.14) | collective-permute-done | bytes 1048608 | tf_op jit(solution)/shard_map/ppermute | solution.py:106
  154.4 8.5 %shard_map.72 = bf16[192,64,128]{2,1,0:T(8,128)(2,1)} custom-call(s32[136]{0:T(256)S(1)} %concatenate.7.index, bf16[192,32,128]{2,1,0:T(8,128)(2,1)} %bitcast.9, bf16[192,32,128]{2,1,0:T(8,128)(2,1)S(1)} %bitcast.7, f32[4,1024]{1,0:T(4,128)S(1)} %copy-done.2, bf16[4,128,1024]{2,1,0:T(8,128)(2,1)} %get-tuple-element.35.refs_0_, ...), custom_call_target="tpu_custom_call" | custom-call | flops 5000000000 | bytes 15000000 | tf_op jit(solution)/shard_map/pallas_call | solution.py:246
  162.9 10.9 %all-to-all-start.2 = ((bf16[64,3,64,128]{3,2,1,0:T(8,128)(2,1)}), bf16[64,3,64,128]{3,2,1,0:T(8,128)(2,1)S(1)}, u32[]{:S(2)}, u32[]{:S(2)}) async-start(bf16[64,3,64,128]{3,2,1,0:T(8,128)(2,1)} %bitcast.8), calls=%async_computation.2 | async-start | bytes 6291456 | tf_op jit(solution)/shard_map/all_to_all | solution.py:292
  173.8 5.7 %shard_map.69.base_in = f32[4,256,1024]{2,1,0:T(8,128)} custom-call(bf16[4,256,1024]{2,1,0:T(8,128)(2,1)} %gamma.1, f32[4,256,512]{2,1,0:T(8,128)} %get-tuple-element.28.first, f32[4,256,512]{2,1,0:T(8,128)} %get-tuple-element.33.second), custom_call_target="tpu_custom_call" | custom-call | flops 4000000000 | bytes 12000000 | tf_op jit(solution)/shard_map/pallas_call | solution.py:246
  179.5 68.0 %all-to-all-done.2 = bf16[64,3,64,128]{3,2,1,0:T(8,128)(2,1)S(1)} async-done(((bf16[64,3,64,128]{3,2,1,0:T(8,128)(2,1)}), bf16[64,3,64,128]{3,2,1,0:T(8,128)(2,1)S(1)}, u32[]{:S(2)}, u32[]{:S(2)}) %all-to-all-start.2) | async-done | bytes 3145760 | tf_op jit(solution)/shard_map/all_to_all | solution.py:292
  247.6 3.7 %shard_map.73 = bf16[4,256,1024]{2,1,0:T(8,128)(2,1)} custom-call(s32[136]{0:T(256)S(1)} %concatenate.6.refs_0_.index, f32[4,256,1024]{2,1,0:T(8,128)} %shard_map.69.base_in, bf16[192,64,128]{2,1,0:T(8,128)(2,1)S(1)} %bitcast.6), custom_call_target="tpu_custom_call" | custom-call | flops 3000000000 | bytes 9000000 | tf_op jit(solution)/shard_map/pallas_call | solution.py:246
  (56 shorter events, 21.4 us)
Async XLA Ops:
  1.5 9.8 %copy-start.4 = (bf16[4,256,1024]{2,1,0:T(8,128)(2,1)S(1)}, bf16[4,256,1024]{2,1,0:T(8,128)(2,1)}, u32[]{:S(2)}) copy-start(bf16[4,256,1024]{2,1,0:T(8,128)(2,1)} %param.9) | copy-start | bytes 6291460
  4.8 16.1 %collective-permute-start = (bf16[4,256,256]{2,1,0:T(8,128)(2,1)S(1)}, bf16[4,256,256]{2,1,0:T(8,128)(2,1)S(1)}, u32[]{:S(2)}, u32[]{:S(2)}) collective-permute-start(bf16[4,256,256]{2,1,0:T(8,128)(2,1)S(1)} %get-tuple-element.24.refs_2_), channel_id=1, source_target_pairs={{0,1},{1,2},{2,3},{3,0},{4,5},{5,6},{6,7},{7,4},{8,9},{9,10},{10,1... | collective-permute-start | bytes 1572872 | tf_op jit(solution)/shard_map/ppermute | solution.py:99
  6.4 14.8 %collective-permute-start.3 = (bf16[4,256,256]{2,1,0:T(8,128)(2,1)S(1)}, bf16[4,256,256]{2,1,0:T(8,128)(2,1)S(1)}, u32[]{:S(2)}, u32[]{:S(2)}) collective-permute-start(bf16[4,256,256]{2,1,0:T(8,128)(2,1)S(1)} %get-tuple-element.25.refs_3_), channel_id=1, source_target_pairs={{0,3},{1,0},{2,1},{3,2},{4,7},{5,4},{6,5},{7,6},{8,11},{9,8},{10,9... | collective-permute-start | bytes 1572872 | tf_op jit(solution)/shard_map/ppermute | solution.py:100
  8.1 24.0 %collective-permute-start.1 = (bf16[4,256,256]{2,1,0:T(8,128)(2,1)S(1)}, bf16[4,256,256]{2,1,0:T(8,128)(2,1)S(1)}, u32[]{:S(2)}, u32[]{:S(2)}) collective-permute-start(bf16[4,256,256]{2,1,0:T(8,128)(2,1)S(1)} %get-tuple-element.25.refs_3_), channel_id=1, source_target_pairs={{0,1},{1,2},{2,3},{3,0},{4,5},{5,6},{6,7},{7,4},{8,9},{9,10},{10,1... | collective-permute-start | bytes 1572872 | tf_op jit(solution)/shard_map/ppermute | solution.py:101
  8.4 24.1 %collective-permute-start.2 = (bf16[4,256,256]{2,1,0:T(8,128)(2,1)S(1)}, bf16[4,256,256]{2,1,0:T(8,128)(2,1)S(1)}, u32[]{:S(2)}, u32[]{:S(2)}) collective-permute-start(bf16[4,256,256]{2,1,0:T(8,128)(2,1)S(1)} %get-tuple-element.24.refs_2_), channel_id=1, source_target_pairs={{0,3},{1,0},{2,1},{3,2},{4,7},{5,4},{6,5},{7,6},{8,11},{9,8},{10,9... | collective-permute-start | bytes 1572872 | tf_op jit(solution)/shard_map/ppermute | solution.py:102
  21.3 21.0 %collective-permute-start.4 = (bf16[4,256,256]{2,1,0:T(8,128)(2,1)S(1)}, bf16[4,256,256]{2,1,0:T(8,128)(2,1)S(1)}, u32[]{:S(2)}, u32[]{:S(2)}) collective-permute-start(bf16[4,256,256]{2,1,0:T(8,128)(2,1)S(1)} %collective-permute-done.refs_4_), channel_id=1, source_target_pairs={{0,1},{1,2},{2,3},{3,0},{4,5},{5,6},{6,7},{7,4},{8,9},{9,10},{10,1... | collective-permute-start | bytes 1572872 | tf_op jit(solution)/shard_map/ppermute | solution.py:106
  22.8 19.4 %collective-permute-start.5 = (bf16[4,256,256]{2,1,0:T(8,128)(2,1)S(1)}, bf16[4,256,256]{2,1,0:T(8,128)(2,1)S(1)}, u32[]{:S(2)}, u32[]{:S(2)}) collective-permute-start(bf16[4,256,256]{2,1,0:T(8,128)(2,1)S(1)} %collective-permute-done.3.refs_7_), channel_id=1, source_target_pairs={{0,3},{1,0},{2,1},{3,2},{4,7},{5,4},{6,5},{7,6},{8,11},{9,8},{10,9... | collective-permute-start | bytes 1572872 | tf_op jit(solution)/shard_map/ppermute | solution.py:107
  26.3 17.6 %copy-start.1 = (bf16[4,256,512]{2,1,0:T(8,128)(2,1)}, bf16[4,256,512]{2,1,0:T(8,128)(2,1)S(1)}, u32[]{:S(2)}) copy-start(bf16[4,256,512]{2,1,0:T(8,128)(2,1)S(1)} %shard_map.67.refs_2_) | copy-start | bytes 3145732
  29.2 19.6 %copy-start.3 = (bf16[4,256,1024]{2,1,0:T(8,128)(2,1)}, bf16[4,256,1024]{2,1,0:T(8,128)(2,1)S(1)}, u32[]{:S(2)}) copy-start(bf16[4,256,1024]{2,1,0:T(8,128)(2,1)S(1)} %shard_map.64.refs_1_) | copy-start | bytes 6291460
  42.3 25.4 %collective-permute-start.6 = (bf16[4,256,512]{2,1,0:T(8,128)(2,1)S(1)}, bf16[4,256,512]{2,1,0:T(8,128)(2,1)}, u32[]{:S(2)}, u32[]{:S(2)}) collective-permute-start(bf16[4,256,512]{2,1,0:T(8,128)(2,1)S(1)} %shard_map.67.refs_2_), channel_id=1, source_target_pairs={{0,1},{1,2},{2,3},{3,0},{4,5},{5,6},{6,7},{7,4},{8,9},{9,10},{10,1... | collective-permute-start | bytes 3145736 | tf_op jit(solution)/shard_map/ppermute | solution.py:116
  43.8 24.9 %collective-permute-start.7 = (bf16[4,256,512]{2,1,0:T(8,128)(2,1)S(1)}, bf16[4,256,512]{2,1,0:T(8,128)(2,1)}, u32[]{:S(2)}, u32[]{:S(2)}) collective-permute-start(bf16[4,256,512]{2,1,0:T(8,128)(2,1)S(1)} %shard_map.67.refs_2_), channel_id=1, source_target_pairs={{0,3},{1,0},{2,1},{3,2},{4,7},{5,4},{6,5},{7,6},{8,11},{9,8},{10,9... | collective-permute-start | bytes 3145736 | tf_op jit(solution)/shard_map/ppermute | solution.py:117
  48.8 52.1 %all-to-all-start = ((bf16[64,3,32,128]{3,2,1,0:T(8,128)(2,1)}), bf16[64,3,32,128]{3,2,1,0:T(8,128)(2,1)S(1)}, u32[]{:S(2)}, u32[]{:S(2)}) async-start(bf16[64,3,32,128]{3,2,1,0:T(8,128)(2,1)} %bitcast.10), calls=%async_computation | async-start | bytes 3145728 | tf_op jit(solution)/shard_map/all_to_all | solution.py:292
  69.8 13.2 %collective-permute-start.8 = (bf16[4,128,512]{2,1,0:T(8,128)(2,1)S(1)}, bf16[4,128,512]{2,1,0:T(8,128)(2,1)S(1)}, u32[]{:S(2)}, u32[]{:S(2)}) collective-permute-start(bf16[4,128,512]{2,1,0:T(8,128)(2,1)S(1)} %slice.16), channel_id=1, source_target_pairs={{0,1},{1,2},{2,3},{3,0},{4,5},{5,6},{6,7},{7,4},{8,9},{9,10},{10,1... | collective-permute-start | bytes 1572872 | tf_op jit(solution)/shard_map/ppermute | solution.py:123
  69.9 13.1 %collective-permute-start.9 = (bf16[4,128,512]{2,1,0:T(8,128)(2,1)S(1)}, bf16[4,128,512]{2,1,0:T(8,128)(2,1)S(1)}, u32[]{:S(2)}, u32[]{:S(2)}) collective-permute-start(bf16[4,128,512]{2,1,0:T(8,128)(2,1)S(1)} %slice.17), channel_id=1, source_target_pairs={{0,3},{1,0},{2,1},{3,2},{4,7},{5,4},{6,5},{7,6},{8,11},{9,8},{10,9... | collective-permute-start | bytes 1572872 | tf_op jit(solution)/shard_map/ppermute | solution.py:124
  83.1 49.7 %collective-permute-start.11 = (bf16[4,128,1024]{2,1,0:T(8,128)(2,1)}, bf16[4,128,1024]{2,1,0:T(8,128)(2,1)}, u32[]{:S(2)}, u32[]{:S(2)}) collective-permute-start(bf16[4,128,1024]{2,1,0:T(8,128)(2,1)} %get-tuple-element.36.refs_1_), channel_id=1, source_target_pairs={{0,1},{1,2},{2,3},{3,0},{4,5},{5,6},{6,7},{7,4},{8,9},{9,10},{10,1... | collective-permute-start | bytes 3145736 | tf_op jit(solution)/shard_map/ppermute | solution.py:101
  83.3 46.2 %collective-permute-start.13 = (bf16[4,128,1024]{2,1,0:T(8,128)(2,1)}, bf16[4,128,1024]{2,1,0:T(8,128)(2,1)}, u32[]{:S(2)}, u32[]{:S(2)}) collective-permute-start(bf16[4,128,1024]{2,1,0:T(8,128)(2,1)} %get-tuple-element.36.refs_1_), channel_id=1, source_target_pairs={{0,3},{1,0},{2,1},{3,2},{4,7},{5,4},{6,5},{7,6},{8,11},{9,8},{10,9... | collective-permute-start | bytes 3145736 | tf_op jit(solution)/shard_map/ppermute | solution.py:100
  86.5 43.0 %collective-permute-start.10 = (bf16[4,128,1024]{2,1,0:T(8,128)(2,1)}, bf16[4,128,1024]{2,1,0:T(8,128)(2,1)}, u32[]{:S(2)}, u32[]{:S(2)}) collective-permute-start(bf16[4,128,1024]{2,1,0:T(8,128)(2,1)} %get-tuple-element.35.refs_0_), channel_id=1, source_target_pairs={{0,1},{1,2},{2,3},{3,0},{4,5},{5,6},{6,7},{7,4},{8,9},{9,10},{10,1... | collective-permute-start | bytes 3145736 | tf_op jit(solution)/shard_map/ppermute | solution.py:99
  100.9 31.9 %copy-start.5 = (bf16[64,3,32,128]{3,2,1,0:T(8,128)(2,1)}, bf16[64,3,32,128]{3,2,1,0:T(8,128)(2,1)S(1)}, u32[]{:S(2)}) copy-start(bf16[64,3,32,128]{3,2,1,0:T(8,128)(2,1)S(1)} %all-to-all-done) | copy-start | bytes 4718596
  100.9 53.5 %all-to-all-start.1 = ((bf16[64,3,32,128]{3,2,1,0:T(8,128)(2,1)}), bf16[64,3,32,128]{3,2,1,0:T(8,128)(2,1)S(1)}, u32[]{:S(2)}, u32[]{:S(2)}) async-start(bf16[64,3,32,128]{3,2,1,0:T(8,128)(2,1)} %bitcast.11), calls=%async_computation.1 | async-start | bytes 3145728 | tf_op jit(solution)/shard_map/all_to_all | solution.py:292
  106.3 26.5 %collective-permute-start.12 = (bf16[4,128,1024]{2,1,0:T(8,128)(2,1)}, bf16[4,128,1024]{2,1,0:T(8,128)(2,1)S(1)}, u32[]{:S(2)}, u32[]{:S(2)}) collective-permute-start(bf16[4,128,1024]{2,1,0:T(8,128)(2,1)} %get-tuple-element.35.refs_0_), channel_id=1, source_target_pairs={{0,3},{1,0},{2,1},{3,2},{4,7},{5,4},{6,5},{7,6},{8,11},{9,8},{10,9... | collective-permute-start | bytes 3145736 | tf_op jit(solution)/shard_map/ppermute | solution.py:102
  129.5 22.7 %collective-permute-start.14 = (bf16[4,128,1024]{2,1,0:T(8,128)(2,1)}, bf16[4,128,1024]{2,1,0:T(8,128)(2,1)S(1)}, u32[]{:S(2)}, u32[]{:S(2)}) collective-permute-start(bf16[4,128,1024]{2,1,0:T(8,128)(2,1)} %collective-permute-done.10.refs_2_), channel_id=1, source_target_pairs={{0,1},{1,2},{2,3},{3,0},{4,5},{5,6},{6,7},{7,4},{8,9},{9,10},{10,1... | collective-permute-start | bytes 3145736 | tf_op jit(solution)/shard_map/ppermute | solution.py:106
  129.5 24.8 %collective-permute-start.15 = (bf16[4,128,1024]{2,1,0:T(8,128)(2,1)}, bf16[4,128,1024]{2,1,0:T(8,128)(2,1)}, u32[]{:S(2)}, u32[]{:S(2)}) collective-permute-start(bf16[4,128,1024]{2,1,0:T(8,128)(2,1)} %collective-permute-done.13.refs_5_), channel_id=1, source_target_pairs={{0,3},{1,0},{2,1},{3,2},{4,7},{5,4},{6,5},{7,6},{8,11},{9,8},{10,9... | collective-permute-start | bytes 3145736 | tf_op jit(solution)/shard_map/ppermute | solution.py:107
  132.8 21.6 %copy-start.2 = (f32[4,1024]{1,0:T(4,128)S(1)}, f32[4,1024]{1,0:T(4,128)}, u32[]{:S(2)}) copy-start(f32[4,1024]{1,0:T(4,128)} %chi.3) | copy-start | bytes 49156
  162.9 84.6 %all-to-all-start.2 = ((bf16[64,3,64,128]{3,2,1,0:T(8,128)(2,1)}), bf16[64,3,64,128]{3,2,1,0:T(8,128)(2,1)S(1)}, u32[]{:S(2)}, u32[]{:S(2)}) async-start(bf16[64,3,64,128]{3,2,1,0:T(8,128)(2,1)} %bitcast.8), calls=%async_computation.2 | async-start | bytes 6291456 | tf_op jit(solution)/shard_map/all_to_all | solution.py:292
  (5 other events, 9.9 us)

commit v8 on v7

--- a/solution.py
+++ b/solution.py
@@ -175,12 +175,8 @@
     wait_all(stores)
 
 
-def pp_kernel(index, first_in, second, chi, *refs):
-    pieces, slots_out = refs[:8], refs[8]
-    right, first, tiles, lhs, in_sems, slot_sems = refs[9:]
-    arrivals = start_all([pltpu.make_async_copy(first_in, first, slot_sems.at[0])])
-    loads = right_loads(pieces, index[128], right, in_sems)
-    wait_all(arrivals)
+def unpack_kernel(index, first_in, second, chi, lhs, first, sems):
+    wait_all(start_all([pltpu.make_async_copy(first_in, first, sems.at[0])]))
     low = low_lanes(32)
     for p in range(4):
         row = chi[p : p + 1, :]
@@ -193,19 +189,26 @@
                 crossed = (swap_lanes(jnp.where(low, b, a)) * scale).astype(BF16)
                 top = r * 64 + c % 2 * 32
                 other = r * 64 + 32 - c % 2 * 32
-                lhs[top : top + 32, c * 128 : c * 128 + 128] = straight
-                lhs[other : other + 32, c * 128 : c * 128 + 128] = crossed
+                lhs[p, top : top + 32, c * 128 : c * 128 + 128] = straight
+                lhs[p, other : other + 32, c * 128 : c * 128 + 128] = crossed
+
+
+def pp_kernel(index, lhs, *refs):
+    pieces, slots_out = refs[:8], refs[8]
+    right, tiles, in_sems, slot_sems = refs[9:]
+    loads = right_loads(pieces, index[128], right, in_sems)
+    for p in range(4):
         wait_all(loads[p])
         for half in range(2):
             columns = slice(half * 512, half * 512 + 512)
-            phi = jnp.dot(lhs[...], right[p, :, columns], preferred_element_type=F32).astype(BF16)
+            phi = jnp.dot(lhs[p], right[p, :, columns], preferred_element_type=F32).astype(BF16)
             for r in range(RS):
                 for c in range(4):
                     item = p * ITEMS + r * CB + half * 4 + c
                     tiles[item] = phi[r * 64 : r * 64 + 64, c * 128 : c * 128 + 128]
                     to = slots_out.at[index[item]]
-                    pltpu.make_async_copy(tiles.at[item], to, slot_sems.at[1]).start()
-    pltpu.make_async_copy(tiles, slots_out.at[: 4 * ITEMS], slot_sems.at[1]).wait()
+                    pltpu.make_async_copy(tiles.at[item], to, slot_sems.at[0]).start()
+    pltpu.make_async_copy(tiles, slots_out.at[: 4 * ITEMS], slot_sems.at[0]).wait()
 
 
 def base_kernel(gamma, first, second, out):
@@ -360,20 +363,35 @@
     )
 
 
-def pp_whole(index, came_1, came_2, chi, pieces):
-    scratch = [pltpu.VMEM((4, 1024, 1024), BF16), vmem(came_1), pltpu.VMEM((4 * ITEMS, 64, 128), BF16)]
-    scratch += [pltpu.VMEM((256, 1024), BF16), DMA((8, 4)), DMA((2,))]
+def unpack(index, came_1, came_2, chi):
+    return call(
+        unpack_kernel,
+        (index,),
+        (came_1, came_2, chi),
+        [ANY, NEAR_BY, NEAR_BY],
+        NEAR_BY,
+        jax.ShapeDtypeStruct((4, 256, 1024), BF16),
+        [vmem(came_1), DMA((1,))],
+        4,
+        8,
+        free=(1, 2),
+        grid=(),
+    )
+
+
+def pp_whole(index, lhs, pieces):
+    scratch = [pltpu.VMEM((4, 1024, 1024), BF16), pltpu.VMEM((4 * ITEMS, 64, 128), BF16)]
     return call(
         pp_kernel,
         (index,),
-        (came_1, came_2, chi) + pieces,
-        [ANY, NEAR_BY, NEAR_BY] + [ANY] * 8,
+        (lhs,) + pieces,
+        [NEAR_BY] + [ANY] * 8,
         ANY,
         pltpu.HBM(TILES, BF16),
-        scratch,
+        scratch + [DMA((8, 4)), DMA((1,))],
         5,
-        20,
-        free=(1, 2),
+        16,
+        free=(0, 7, 8),
         grid=(),
     )
 
@@ -428,9 +446,8 @@
     pp_pieces = gather_rows(*after(pp_halves, pieces_2), between=outgoing_2)
     came_2 = exchange(outgoing_2)
     held = tuple(hold(x, FAR) if k in (1, 2) else x for k, x in enumerate(pp_pieces[2:6]))
-    leaving = pp_whole(
-        recv_index, came_1, came_2, chi_pp, pp_pieces[:2] + held + pp_pieces[6:]
-    )
+    lhs = unpack(recv_index, came_1, came_2, chi_pp)
+    leaving = pp_whole(recv_index, lhs, pp_pieces[:2] + held + pp_pieces[6:])
     base = base_sum(gamma_ph, phi_1, phi_2)
     return last_sum(send_index, base, exchange(leaving))
 

time: 252 us -> 250 us (level)
    ppermute x2, waiting for transfers between devices: 28.2 us -> 12.8 us  [gather_rows(): far_low = lax.ppermute(near[0], 'block', up)]
    all_to_all x3, waiting for transfers between devices: 76 us -> 88.9 us  [exchange(): lax.all_to_all(slots.reshape((nboson, CAP) + tile), 'boson', split_axis=0...]
    pallas_call x10 -> x11, Pallas kernels: 35.3 us -> 35.3 us  [call(): pl.pallas_call(kernel, grid_spec=pltpu.PrefetchScalarGridSpec(num_scalar_...]
  transfers between devices with their start and end apart: 19 -> 19, of which waited for: 12 -> 14; matrix products, arithmetic and copies ran while one was open for 1% -> 1% of each run, Pallas kernels for 8% -> 9%
where the time goes in v8:
time: 250 us; the launch traced here: 249 us
  waiting for transfers between devices  153 us (61%)
  starting transfers between devices  52.7 us (21%)
  Pallas kernels  35.3 us (14%)
  local copies, waits for them, and re-layouts  8.14 us (3%)
    all_to_all x3, waiting for transfers between devices, exchange(): lax.all_to_all(slots.reshape((nboson, CAP) + tile), 'boson', split_axis=0...  88.9 us
    pallas_call x11, Pallas kernels, call(): pl.pallas_call(kernel, grid_spec=pltpu.PrefetchScalarGridSpec(num_scalar_...  35.3 us
    ppermute x2, waiting for transfers between devices, gather_rows(): below_low = lax.ppermute(low, 'block', up)  28 us
    all_to_all x3, starting transfers between devices, exchange(): lax.all_to_all(slots.reshape((nboson, CAP) + tile), 'boson', split_axis=0...  27.7 us
    ppermute x2, waiting for transfers between devices, gather_rows(): far_low = lax.ppermute(near[0], 'block', up)  12.8 us
    ppermute x1, waiting for transfers between devices, gather_whole(): lax.ppermute(near_low, 'block', up)  9.89 us
    ppermute x1, waiting for transfers between devices, gather_whole(): below = lax.ppermute(own, 'block', up)  6.79 us
  transfers between devices with their start and end apart: 19, of which 14 were waited for; matrix products, arithmetic and copies ran while one was open for 1% of the time, Pallas kernels for 9%

profile of v8, /device:TPU:2, one launch (start us, length us, event | category | flops | bytes accessed | tf_op | source)
XLA Modules:
  0.0 249.4 jit_solution(14970084436023776403)
XLA Ops:
  1.5 3.2 %shard_map.65 = (bf16[4,256,256]{2,1,0:T(8,128)(2,1)S(1)}, bf16[4,256,256]{2,1,0:T(8,128)(2,1)S(1)}) custom-call(bf16[4,256,1024]{2,1,0:T(8,128)(2,1)} %refs_0_.1), custom_call_target="tpu_custom_call" | custom-call | flops 2000000000 | bytes 6000000 | tf_op jit(solution)/shard_map/pallas_call | solution.py:249
  8.4 2.9 %collective-permute-start.2 = (bf16[4,256,256]{2,1,0:T(8,128)(2,1)S(1)}, bf16[4,256,256]{2,1,0:T(8,128)(2,1)S(1)}, u32[]{:S(2)}, u32[]{:S(2)}) collective-permute-start(bf16[4,256,256]{2,1,0:T(8,128)(2,1)S(1)} %get-tuple-element.24.refs_2_), channel_id=1, source_target_pairs={{0,3},{1,0},{2,1},{3,2},{4,7},{5,4},{6,5},{7,6},{8,11},{9,8},{10,9... | collective-permute-start | bytes 1572872 | tf_op jit(solution)/shard_map/ppermute | solution.py:102
  12.8 8.0 %collective-permute-done.refs_4_ = bf16[4,256,256]{2,1,0:T(8,128)(2,1)S(1)} collective-permute-done((bf16[4,256,256]{2,1,0:T(8,128)(2,1)S(1)}, bf16[4,256,256]{2,1,0:T(8,128)(2,1)S(1)}, u32[]{:S(2)}, u32[]{:S(2)}) %collective-permute-start) | collective-permute-done | bytes 524320 | tf_op jit(solution)/shard_map/ppermute | solution.py:99
  26.3 2.9 %shard_map.64.refs_1_ = bf16[4,256,1024]{2,1,0:T(8,128)(2,1)S(1)} custom-call(bf16[4,256,1024]{2,1,0:T(8,128)(2,1)} %gamma.1, f32[4,1024]{1,0:T(4,128)} %chi.2), custom_call_target="tpu_custom_call" | custom-call | flops 2000000000 | bytes 6000000 | tf_op jit(solution)/shard_map/pallas_call | solution.py:249
  29.2 2.9 %collective-permute-done.1.refs_5_ = bf16[4,256,256]{2,1,0:T(8,128)(2,1)S(1)} collective-permute-done((bf16[4,256,256]{2,1,0:T(8,128)(2,1)S(1)}, bf16[4,256,256]{2,1,0:T(8,128)(2,1)S(1)}, u32[]{:S(2)}, u32[]{:S(2)}) %collective-permute-start.1) | collective-permute-done | bytes 524320 | tf_op jit(solution)/shard_map/ppermute | solution.py:101
  32.5 9.7 %collective-permute-done.4.refs_8_ = bf16[4,256,256]{2,1,0:T(8,128)(2,1)S(1)} collective-permute-done((bf16[4,256,256]{2,1,0:T(8,128)(2,1)S(1)}, bf16[4,256,256]{2,1,0:T(8,128)(2,1)S(1)}, u32[]{:S(2)}, u32[]{:S(2)}) %collective-permute-start.4) | collective-permute-done | bytes 524320 | tf_op jit(solution)/shard_map/ppermute | solution.py:106
  45.5 3.3 %shard_map.66 = (f32[4,256,512]{2,1,0:T(8,128)}, bf16[192,32,128]{2,1,0:T(8,128)(2,1)}) custom-call(s32[136]{0:T(256)S(1)} %concatenate.6.refs_0_.index, bf16[4,256,1024]{2,1,0:T(8,128)(2,1)S(1)} %shard_map.64.refs_1_, bf16[4,256,256]{2,1,0:T(8,128)(2,1)S(1)} %get-tuple-element.24.refs_2_, bf16[4,256,256]{2,1,0:T(8,128)(2,1)S(1)} %get-tuple-element.25.refs_3_, ...), custom_call_target="tpu_custom_call" | custom-call | flops 4000000000 | bytes 12000000 | tf_op jit(solution)/shard_map/pallas_call | solution.py:249
  48.8 12.0 %all-to-all-start = ((bf16[64,3,32,128]{3,2,1,0:T(8,128)(2,1)}), bf16[64,3,32,128]{3,2,1,0:T(8,128)(2,1)S(1)}, u32[]{:S(2)}, u32[]{:S(2)}) async-start(bf16[64,3,32,128]{3,2,1,0:T(8,128)(2,1)} %bitcast.10), calls=%async_computation | async-start | bytes 3145728 | tf_op jit(solution)/shard_map/all_to_all | solution.py:295
  60.9 6.8 %collective-permute-done.6.refs_3_ = bf16[4,256,512]{2,1,0:T(8,128)(2,1)} collective-permute-done((bf16[4,256,512]{2,1,0:T(8,128)(2,1)S(1)}, bf16[4,256,512]{2,1,0:T(8,128)(2,1)}, u32[]{:S(2)}, u32[]{:S(2)}) %collective-permute-start.6) | collective-permute-done | bytes 1048608 | tf_op jit(solution)/shard_map/ppermute | solution.py:116
  69.9 3.2 %collective-permute-start.9 = (bf16[4,128,512]{2,1,0:T(8,128)(2,1)S(1)}, bf16[4,128,512]{2,1,0:T(8,128)(2,1)S(1)}, u32[]{:S(2)}, u32[]{:S(2)}) collective-permute-start(bf16[4,128,512]{2,1,0:T(8,128)(2,1)S(1)} %slice.17), channel_id=1, source_target_pairs={{0,3},{1,0},{2,1},{3,2},{4,7},{5,4},{6,5},{7,6},{8,11},{9,8},{10,9... | collective-permute-start | bytes 1572872 | tf_op jit(solution)/shard_map/ppermute | solution.py:124
  73.2 9.9 %collective-permute-done.8.refs_5_ = bf16[4,128,512]{2,1,0:T(8,128)(2,1)S(1)} collective-permute-done((bf16[4,128,512]{2,1,0:T(8,128)(2,1)S(1)}, bf16[4,128,512]{2,1,0:T(8,128)(2,1)S(1)}, u32[]{:S(2)}, u32[]{:S(2)}) %collective-permute-start.8) | collective-permute-done | bytes 524320 | tf_op jit(solution)/shard_map/ppermute | solution.py:123
  83.3 3.2 %collective-permute-start.13 = (bf16[4,128,1024]{2,1,0:T(8,128)(2,1)}, bf16[4,128,1024]{2,1,0:T(8,128)(2,1)}, u32[]{:S(2)}, u32[]{:S(2)}) collective-permute-start(bf16[4,128,1024]{2,1,0:T(8,128)(2,1)} %get-tuple-element.36.refs_1_), channel_id=1, source_target_pairs={{0,3},{1,0},{2,1},{3,2},{4,7},{5,4},{6,5},{7,6},{8,11},{9,8},{10,9... | collective-permute-start | bytes 3145736 | tf_op jit(solution)/shard_map/ppermute | solution.py:100
  86.6 6.2 %shard_map.68 = (f32[4,256,512]{2,1,0:T(8,128)}, bf16[192,32,128]{2,1,0:T(8,128)(2,1)}) custom-call(s32[136]{0:T(256)S(1)} %concatenate.6.refs_0_.index, bf16[4,256,1024]{2,1,0:T(8,128)(2,1)} %copy-done.3, bf16[4,256,512]{2,1,0:T(8,128)(2,1)} %copy-done.1, bf16[4,256,512]{2,1,0:T(8,128)(2,1)} %collective-permute-done.6.refs_3_, ...), custom_call_target="tpu_custom_call" | custom-call | flops 20000000000 | bytes 60000000 | tf_op jit(solution)/shard_map/pallas_call | solution.py:249
  92.8 8.1 %all-to-all-done = bf16[64,3,32,128]{3,2,1,0:T(8,128)(2,1)S(1)} async-done(((bf16[64,3,32,128]{3,2,1,0:T(8,128)(2,1)}), bf16[64,3,32,128]{3,2,1,0:T(8,128)(2,1)S(1)}, u32[]{:S(2)}, u32[]{:S(2)}) %all-to-all-start) | async-done | bytes 1572896 | tf_op jit(solution)/shard_map/all_to_all | solution.py:295
  102.1 5.4 %all-to-all-start.1 = ((bf16[64,3,32,128]{3,2,1,0:T(8,128)(2,1)}), bf16[64,3,32,128]{3,2,1,0:T(8,128)(2,1)S(1)}, u32[]{:S(2)}, u32[]{:S(2)}) async-start(bf16[64,3,32,128]{3,2,1,0:T(8,128)(2,1)} %bitcast.11), calls=%async_computation.1 | async-start | bytes 3145728 | tf_op jit(solution)/shard_map/all_to_all | solution.py:295
  109.4 20.0 %collective-permute-done.10.refs_2_ = bf16[4,128,1024]{2,1,0:T(8,128)(2,1)S(1)} collective-permute-done((bf16[4,128,1024]{2,1,0:T(8,128)(2,1)}, bf16[4,128,1024]{2,1,0:T(8,128)(2,1)S(1)}, u32[]{:S(2)}, u32[]{:S(2)}) %collective-permute-start.10) | collective-permute-done | bytes 1048608 | tf_op jit(solution)/shard_map/ppermute | solution.py:99
  130.5 3.2 %collective-permute-start.15 = (bf16[4,128,1024]{2,1,0:T(8,128)(2,1)}, bf16[4,128,1024]{2,1,0:T(8,128)(2,1)}, u32[]{:S(2)}, u32[]{:S(2)}) collective-permute-start(bf16[4,128,1024]{2,1,0:T(8,128)(2,1)} %collective-permute-done.13.refs_5_), channel_id=1, source_target_pairs={{0,3},{1,0},{2,1},{3,2},{4,7},{5,4},{6,5},{7,6},{8,11},{9,8},{10,9... | collective-permute-start | bytes 3145736 | tf_op jit(solution)/shard_map/ppermute | solution.py:107
  134.8 12.8 %all-to-all-done.1 = bf16[64,3,32,128]{3,2,1,0:T(8,128)(2,1)S(1)} async-done(((bf16[64,3,32,128]{3,2,1,0:T(8,128)(2,1)}), bf16[64,3,32,128]{3,2,1,0:T(8,128)(2,1)S(1)}, u32[]{:S(2)}, u32[]{:S(2)}) %all-to-all-start.1) | async-done | bytes 1572896 | tf_op jit(solution)/shard_map/all_to_all | solution.py:295
  150.2 3.0 %collective-permute-done.14.refs_6_ = bf16[4,128,1024]{2,1,0:T(8,128)(2,1)S(1)} collective-permute-done((bf16[4,128,1024]{2,1,0:T(8,128)(2,1)}, bf16[4,128,1024]{2,1,0:T(8,128)(2,1)S(1)}, u32[]{:S(2)}, u32[]{:S(2)}) %collective-permute-start.14) | collective-permute-done | bytes 1048608 | tf_op jit(solution)/shard_map/ppermute | solution.py:106
  155.6 5.9 %shard_map.73 = bf16[192,64,128]{2,1,0:T(8,128)(2,1)} custom-call(s32[136]{0:T(256)S(1)} %concatenate.7.index, bf16[4,256,1024]{2,1,0:T(8,128)(2,1)S(1)} %shard_map.70.lhs, bf16[4,128,1024]{2,1,0:T(8,128)(2,1)} %get-tuple-element.35.refs_0_, bf16[4,128,1024]{2,1,0:T(8,128)(2,1)} %get-tuple-element.36.refs_1_, bf16[4,128,1024]{2,1,0:T(8,128)(2,1)} %copy-done.6, ...), custom_call_target="tpu_custom_call" | custom-call | flops 5000000000 | bytes 15000000 | tf_op jit(solution)/shard_map/pallas_call | solution.py:249
  161.5 10.3 %all-to-all-start.2 = ((bf16[64,3,64,128]{3,2,1,0:T(8,128)(2,1)}), bf16[64,3,64,128]{3,2,1,0:T(8,128)(2,1)S(1)}, u32[]{:S(2)}, u32[]{:S(2)}) async-start(bf16[64,3,64,128]{3,2,1,0:T(8,128)(2,1)} %bitcast.8), calls=%async_computation.2 | async-start | bytes 6291456 | tf_op jit(solution)/shard_map/all_to_all | solution.py:295
  171.8 5.7 %shard_map.69.base_in = f32[4,256,1024]{2,1,0:T(8,128)} custom-call(bf16[4,256,1024]{2,1,0:T(8,128)(2,1)} %gamma.1, f32[4,256,512]{2,1,0:T(8,128)} %get-tuple-element.28.first, f32[4,256,512]{2,1,0:T(8,128)} %get-tuple-element.33.second), custom_call_target="tpu_custom_call" | custom-call | flops 4000000000 | bytes 12000000 | tf_op jit(solution)/shard_map/pallas_call | solution.py:249
  177.5 68.0 %all-to-all-done.2 = bf16[64,3,64,128]{3,2,1,0:T(8,128)(2,1)S(1)} async-done(((bf16[64,3,64,128]{3,2,1,0:T(8,128)(2,1)}), bf16[64,3,64,128]{3,2,1,0:T(8,128)(2,1)S(1)}, u32[]{:S(2)}, u32[]{:S(2)}) %all-to-all-start.2) | async-done | bytes 3145760 | tf_op jit(solution)/shard_map/all_to_all | solution.py:295
  245.6 3.7 %shard_map.74 = bf16[4,256,1024]{2,1,0:T(8,128)(2,1)} custom-call(s32[136]{0:T(256)S(1)} %concatenate.6.refs_0_.index, f32[4,256,1024]{2,1,0:T(8,128)} %shard_map.69.base_in, bf16[192,64,128]{2,1,0:T(8,128)(2,1)S(1)} %bitcast.6), custom_call_target="tpu_custom_call" | custom-call | flops 3000000000 | bytes 9000000 | tf_op jit(solution)/shard_map/pallas_call | solution.py:249
  (57 shorter events, 28.5 us)
Async XLA Ops:
  1.5 9.8 %copy-start.4 = (bf16[4,256,1024]{2,1,0:T(8,128)(2,1)S(1)}, bf16[4,256,1024]{2,1,0:T(8,128)(2,1)}, u32[]{:S(2)}) copy-start(bf16[4,256,1024]{2,1,0:T(8,128)(2,1)} %param.9) | copy-start | bytes 6291460
  4.8 16.1 %collective-permute-start = (bf16[4,256,256]{2,1,0:T(8,128)(2,1)S(1)}, bf16[4,256,256]{2,1,0:T(8,128)(2,1)S(1)}, u32[]{:S(2)}, u32[]{:S(2)}) collective-permute-start(bf16[4,256,256]{2,1,0:T(8,128)(2,1)S(1)} %get-tuple-element.24.refs_2_), channel_id=1, source_target_pairs={{0,1},{1,2},{2,3},{3,0},{4,5},{5,6},{6,7},{7,4},{8,9},{9,10},{10,1... | collective-permute-start | bytes 1572872 | tf_op jit(solution)/shard_map/ppermute | solution.py:99
  6.4 14.8 %collective-permute-start.3 = (bf16[4,256,256]{2,1,0:T(8,128)(2,1)S(1)}, bf16[4,256,256]{2,1,0:T(8,128)(2,1)S(1)}, u32[]{:S(2)}, u32[]{:S(2)}) collective-permute-start(bf16[4,256,256]{2,1,0:T(8,128)(2,1)S(1)} %get-tuple-element.25.refs_3_), channel_id=1, source_target_pairs={{0,3},{1,0},{2,1},{3,2},{4,7},{5,4},{6,5},{7,6},{8,11},{9,8},{10,9... | collective-permute-start | bytes 1572872 | tf_op jit(solution)/shard_map/ppermute | solution.py:100
  8.1 24.0 %collective-permute-start.1 = (bf16[4,256,256]{2,1,0:T(8,128)(2,1)S(1)}, bf16[4,256,256]{2,1,0:T(8,128)(2,1)S(1)}, u32[]{:S(2)}, u32[]{:S(2)}) collective-permute-start(bf16[4,256,256]{2,1,0:T(8,128)(2,1)S(1)} %get-tuple-element.25.refs_3_), channel_id=1, source_target_pairs={{0,1},{1,2},{2,3},{3,0},{4,5},{5,6},{6,7},{7,4},{8,9},{9,10},{10,1... | collective-permute-start | bytes 1572872 | tf_op jit(solution)/shard_map/ppermute | solution.py:101
  8.4 24.1 %collective-permute-start.2 = (bf16[4,256,256]{2,1,0:T(8,128)(2,1)S(1)}, bf16[4,256,256]{2,1,0:T(8,128)(2,1)S(1)}, u32[]{:S(2)}, u32[]{:S(2)}) collective-permute-start(bf16[4,256,256]{2,1,0:T(8,128)(2,1)S(1)} %get-tuple-element.24.refs_2_), channel_id=1, source_target_pairs={{0,3},{1,0},{2,1},{3,2},{4,7},{5,4},{6,5},{7,6},{8,11},{9,8},{10,9... | collective-permute-start | bytes 1572872 | tf_op jit(solution)/shard_map/ppermute | solution.py:102
  21.3 21.0 %collective-permute-start.4 = (bf16[4,256,256]{2,1,0:T(8,128)(2,1)S(1)}, bf16[4,256,256]{2,1,0:T(8,128)(2,1)S(1)}, u32[]{:S(2)}, u32[]{:S(2)}) collective-permute-start(bf16[4,256,256]{2,1,0:T(8,128)(2,1)S(1)} %collective-permute-done.refs_4_), channel_id=1, source_target_pairs={{0,1},{1,2},{2,3},{3,0},{4,5},{5,6},{6,7},{7,4},{8,9},{9,10},{10,1... | collective-permute-start | bytes 1572872 | tf_op jit(solution)/shard_map/ppermute | solution.py:106
  22.8 19.4 %collective-permute-start.5 = (bf16[4,256,256]{2,1,0:T(8,128)(2,1)S(1)}, bf16[4,256,256]{2,1,0:T(8,128)(2,1)S(1)}, u32[]{:S(2)}, u32[]{:S(2)}) collective-permute-start(bf16[4,256,256]{2,1,0:T(8,128)(2,1)S(1)} %collective-permute-done.3.refs_7_), channel_id=1, source_target_pairs={{0,3},{1,0},{2,1},{3,2},{4,7},{5,4},{6,5},{7,6},{8,11},{9,8},{10,9... | collective-permute-start | bytes 1572872 | tf_op jit(solution)/shard_map/ppermute | solution.py:107
  26.3 17.6 %copy-start.1 = (bf16[4,256,512]{2,1,0:T(8,128)(2,1)}, bf16[4,256,512]{2,1,0:T(8,128)(2,1)S(1)}, u32[]{:S(2)}) copy-start(bf16[4,256,512]{2,1,0:T(8,128)(2,1)S(1)} %shard_map.67.refs_2_) | copy-start | bytes 3145732
  29.2 19.7 %copy-start.3 = (bf16[4,256,1024]{2,1,0:T(8,128)(2,1)}, bf16[4,256,1024]{2,1,0:T(8,128)(2,1)S(1)}, u32[]{:S(2)}) copy-start(bf16[4,256,1024]{2,1,0:T(8,128)(2,1)S(1)} %shard_map.64.refs_1_) | copy-start | bytes 6291460
  42.3 25.4 %collective-permute-start.6 = (bf16[4,256,512]{2,1,0:T(8,128)(2,1)S(1)}, bf16[4,256,512]{2,1,0:T(8,128)(2,1)}, u32[]{:S(2)}, u32[]{:S(2)}) collective-permute-start(bf16[4,256,512]{2,1,0:T(8,128)(2,1)S(1)} %shard_map.67.refs_2_), channel_id=1, source_target_pairs={{0,1},{1,2},{2,3},{3,0},{4,5},{5,6},{6,7},{7,4},{8,9},{9,10},{10,1... | collective-permute-start | bytes 3145736 | tf_op jit(solution)/shard_map/ppermute | solution.py:116
  43.8 24.9 %collective-permute-start.7 = (bf16[4,256,512]{2,1,0:T(8,128)(2,1)S(1)}, bf16[4,256,512]{2,1,0:T(8,128)(2,1)}, u32[]{:S(2)}, u32[]{:S(2)}) collective-permute-start(bf16[4,256,512]{2,1,0:T(8,128)(2,1)S(1)} %shard_map.67.refs_2_), channel_id=1, source_target_pairs={{0,3},{1,0},{2,1},{3,2},{4,7},{5,4},{6,5},{7,6},{8,11},{9,8},{10,9... | collective-permute-start | bytes 3145736 | tf_op jit(solution)/shard_map/ppermute | solution.py:117
  48.8 52.1 %all-to-all-start = ((bf16[64,3,32,128]{3,2,1,0:T(8,128)(2,1)}), bf16[64,3,32,128]{3,2,1,0:T(8,128)(2,1)S(1)}, u32[]{:S(2)}, u32[]{:S(2)}) async-start(bf16[64,3,32,128]{3,2,1,0:T(8,128)(2,1)} %bitcast.10), calls=%async_computation | async-start | bytes 3145728 | tf_op jit(solution)/shard_map/all_to_all | solution.py:295
  69.8 13.2 %collective-permute-start.8 = (bf16[4,128,512]{2,1,0:T(8,128)(2,1)S(1)}, bf16[4,128,512]{2,1,0:T(8,128)(2,1)S(1)}, u32[]{:S(2)}, u32[]{:S(2)}) collective-permute-start(bf16[4,128,512]{2,1,0:T(8,128)(2,1)S(1)} %slice.16), channel_id=1, source_target_pairs={{0,1},{1,2},{2,3},{3,0},{4,5},{5,6},{6,7},{7,4},{8,9},{9,10},{10,1... | collective-permute-start | bytes 1572872 | tf_op jit(solution)/shard_map/ppermute | solution.py:123
  69.9 13.1 %collective-permute-start.9 = (bf16[4,128,512]{2,1,0:T(8,128)(2,1)S(1)}, bf16[4,128,512]{2,1,0:T(8,128)(2,1)S(1)}, u32[]{:S(2)}, u32[]{:S(2)}) collective-permute-start(bf16[4,128,512]{2,1,0:T(8,128)(2,1)S(1)} %slice.17), channel_id=1, source_target_pairs={{0,3},{1,0},{2,1},{3,2},{4,7},{5,4},{6,5},{7,6},{8,11},{9,8},{10,9... | collective-permute-start | bytes 1572872 | tf_op jit(solution)/shard_map/ppermute | solution.py:124
  83.0 3.5 %copy-start.8 = (bf16[4,128,512]{2,1,0:T(8,128)(2,1)}, bf16[4,128,512]{2,1,0:T(8,128)(2,1)S(1)}, u32[]{:S(2)}) copy-start(bf16[4,128,512]{2,1,0:T(8,128)(2,1)S(1)} %collective-permute-done.8.refs_5_) | copy-start | bytes 1572868
  83.1 50.7 %collective-permute-start.11 = (bf16[4,128,1024]{2,1,0:T(8,128)(2,1)}, bf16[4,128,1024]{2,1,0:T(8,128)(2,1)}, u32[]{:S(2)}, u32[]{:S(2)}) collective-permute-start(bf16[4,128,1024]{2,1,0:T(8,128)(2,1)} %get-tuple-element.36.refs_1_), channel_id=1, source_target_pairs={{0,1},{1,2},{2,3},{3,0},{4,5},{5,6},{6,7},{7,4},{8,9},{9,10},{10,1... | collective-permute-start | bytes 3145736 | tf_op jit(solution)/shard_map/ppermute | solution.py:101
  83.3 47.2 %collective-permute-start.13 = (bf16[4,128,1024]{2,1,0:T(8,128)(2,1)}, bf16[4,128,1024]{2,1,0:T(8,128)(2,1)}, u32[]{:S(2)}, u32[]{:S(2)}) collective-permute-start(bf16[4,128,1024]{2,1,0:T(8,128)(2,1)} %get-tuple-element.36.refs_1_), channel_id=1, source_target_pairs={{0,3},{1,0},{2,1},{3,2},{4,7},{5,4},{6,5},{7,6},{8,11},{9,8},{10,9... | collective-permute-start | bytes 3145736 | tf_op jit(solution)/shard_map/ppermute | solution.py:100
  86.5 42.9 %collective-permute-start.10 = (bf16[4,128,1024]{2,1,0:T(8,128)(2,1)}, bf16[4,128,1024]{2,1,0:T(8,128)(2,1)S(1)}, u32[]{:S(2)}, u32[]{:S(2)}) collective-permute-start(bf16[4,128,1024]{2,1,0:T(8,128)(2,1)} %get-tuple-element.35.refs_0_), channel_id=1, source_target_pairs={{0,1},{1,2},{2,3},{3,0},{4,5},{5,6},{6,7},{7,4},{8,9},{9,10},{10,1... | collective-permute-start | bytes 3145736 | tf_op jit(solution)/shard_map/ppermute | solution.py:99
  102.1 45.5 %all-to-all-start.1 = ((bf16[64,3,32,128]{3,2,1,0:T(8,128)(2,1)}), bf16[64,3,32,128]{3,2,1,0:T(8,128)(2,1)S(1)}, u32[]{:S(2)}, u32[]{:S(2)}) async-start(bf16[64,3,32,128]{3,2,1,0:T(8,128)(2,1)} %bitcast.11), calls=%async_computation.1 | async-start | bytes 3145728 | tf_op jit(solution)/shard_map/all_to_all | solution.py:295
  107.5 26.3 %collective-permute-start.12 = (bf16[4,128,1024]{2,1,0:T(8,128)(2,1)}, bf16[4,128,1024]{2,1,0:T(8,128)(2,1)S(1)}, u32[]{:S(2)}, u32[]{:S(2)}) collective-permute-start(bf16[4,128,1024]{2,1,0:T(8,128)(2,1)} %get-tuple-element.35.refs_0_), channel_id=1, source_target_pairs={{0,3},{1,0},{2,1},{3,2},{4,7},{5,4},{6,5},{7,6},{8,11},{9,8},{10,9... | collective-permute-start | bytes 3145736 | tf_op jit(solution)/shard_map/ppermute | solution.py:102
  130.5 22.7 %collective-permute-start.14 = (bf16[4,128,1024]{2,1,0:T(8,128)(2,1)}, bf16[4,128,1024]{2,1,0:T(8,128)(2,1)S(1)}, u32[]{:S(2)}, u32[]{:S(2)}) collective-permute-start(bf16[4,128,1024]{2,1,0:T(8,128)(2,1)} %copy-done.6), channel_id=1, source_target_pairs={{0,1},{1,2},{2,3},{3,0},{4,5},{5,6},{6,7},{7,4},{8,9},{9,10},{10,1... | collective-permute-start | bytes 3145736 | tf_op jit(solution)/shard_map/ppermute | solution.py:106
  130.5 25.1 %collective-permute-start.15 = (bf16[4,128,1024]{2,1,0:T(8,128)(2,1)}, bf16[4,128,1024]{2,1,0:T(8,128)(2,1)}, u32[]{:S(2)}, u32[]{:S(2)}) collective-permute-start(bf16[4,128,1024]{2,1,0:T(8,128)(2,1)} %collective-permute-done.13.refs_5_), channel_id=1, source_target_pairs={{0,3},{1,0},{2,1},{3,2},{4,7},{5,4},{6,5},{7,6},{8,11},{9,8},{10,9... | collective-permute-start | bytes 3145736 | tf_op jit(solution)/shard_map/ppermute | solution.py:107
  133.7 13.8 %copy-start.2 = (f32[4,1024]{1,0:T(4,128)S(1)}, f32[4,1024]{1,0:T(4,128)}, u32[]{:S(2)}) copy-start(f32[4,1024]{1,0:T(4,128)} %chi.3) | copy-start | bytes 49156
  161.5 84.0 %all-to-all-start.2 = ((bf16[64,3,64,128]{3,2,1,0:T(8,128)(2,1)}), bf16[64,3,64,128]{3,2,1,0:T(8,128)(2,1)S(1)}, u32[]{:S(2)}, u32[]{:S(2)}) async-start(bf16[64,3,64,128]{3,2,1,0:T(8,128)(2,1)} %bitcast.8), calls=%async_computation.2 | async-start | bytes 6291456 | tf_op jit(solution)/shard_map/all_to_all | solution.py:295
  (5 other events, 7.6 us)
